TPU v7x, 32 devices: a whole 2x2x4 slice. The times are simulated.
32 devices in a mesh: dp: 16 (over z, y, x), shard: 2 (over core).
Axes of the slice: x: 2, y: 2, z: 4, core: 2. Of those that a mesh axis runs over, the one named last changes fastest.
Arguments:
- inputs: bfloat16 [32, 768, 576], P(None, ('dp', 'shard')), may hold values from -6 to 6
- cotangent: bfloat16 [32, 768, 576], P(None, ('dp', 'shard')), may hold values from -6 to 6
- lengths: int32 [32], replicated, may hold values from 1 to 768, 14745 in all
- assignment: int32 [32], replicated, may hold values from 0 to 31, each once
- return_order: int32 [32], replicated, may hold values from 0 to 31, each once
- master: float32 [3540096], P('shard'), as said below
- momentum: float32 [3540096], P('shard'), as said below
- average: float32 [3540096], P('shard'), as said below
Outputs:
- block_output: bfloat16 [32, 768, 576], P(None, ('dp', 'shard'))
- input_grad: bfloat16 [32, 768, 576], P(None, ('dp', 'shard'))
- weight_grad: float32 [3540096], P('shard')
- new_momentum: float32 [3540096], P('shard')
- new_master: float32 [3540096], P('shard')
- new_average: float32 [3540096], P('shard')
Inputs may be any that keep to these rules, and one draw needn't show every extreme that they name: `lengths`: the longest live length is exactly 768. `assignment`: each slot gets a different sequence. `return_order`: each slot fills one output row. `master`: packed in the weights' order. `momentum`: packed in the weights' order. `average`: packed in the weights' order.
All inputs are finite; a program needn't handle non-finite values.
Results may differ from a plain program's by a relative error of at most 0.017.
The roundings to bfloat16 on the way count: a program that leaves them out, or rounds other values in their place, can miss the bound.
Values may be sent and summed in bfloat16 or wider, within the bound.
No kernel may reach another device: no remote copies, remote signals or barrier semaphores. Data moves between devices by JAX's collectives and lax.ppermute only.
A program may use at most 192 MiB of HBM per device.

v0:
```python
import functools
import math

import jax
import jax.numpy as jnp
from jax import lax
from jax.experimental import pallas as pl
from jax.experimental.pallas import tpu as pltpu
from jax.sharding import PartitionSpec as P

D = 576
H = 9
KV = 3
HD = 64
FF = 1536
LANES = 128
BLOCK = 256
Q_TILES = 5
PAD_D = Q_TILES * LANES
KV_COLS = 2 * KV * HD
FF_TILES = FF // LANES
DOWN_FIRST = 4
EARLY_TILES = 21
EARLY_ROWS = 12288
EXTRA = EARLY_TILES * D
HALF = 27657 * LANES // 2
PART_ROWS = EARLY_ROWS // 3
SWAP_START = EXTRA - DOWN_FIRST * D - 2 * PART_ROWS
SWAP_TAIL = EXTRA + 16 - 2 * PART_ROWS
REST_FIRST = 2 * PART_ROWS - FF_TILES * D
REST_SLOT = REST_FIRST + 16
REST = REST_SLOT + 16
LATE_HALF = 2432
HALF_ROWS = 13832
FLAT_SCRATCH = 13848
O_ROW = 4329
GATE_ROW = 6921
MLP_COLS = 256
MLP_UNROLL = 6
MLP_BLOCK = 256
CHUNK = 576
STEP = 288
LATE_CHUNKS = 7

EPSILON = 1e-05
MOMENTUM_DECAY = 0.55
AVERAGE_DECAY = 0.45
MASKED = -1000000000.0

BF = jnp.bfloat16
F32 = jnp.float32
MIB = 1024 * 1024


def nn(a, b):
    return jnp.dot(a, b, preferred_element_type=F32)


def nt(a, b):
    return lax.dot_general(a, b, (((1,), (1,)), ((), ())), preferred_element_type=F32)


def tn(a, b):
    return lax.dot_general(a, b, (((0,), (0,)), ((), ())), preferred_element_type=F32)


def tile(value, index):
    return value[:, index * LANES : (index + 1) * LANES]


def low_half(rows):
    return lax.broadcasted_iota(jnp.int32, (rows, LANES), 1) < HD


def swap_halves(value):
    lane = lax.broadcasted_iota(jnp.int32, value.shape, 1)
    return jnp.where(lane % HD < HD // 2, pltpu.roll(value, 96, 1), pltpu.roll(value, 32, 1))


def flip(value):
    return pltpu.roll(value, HD, 1)


def rms(value):
    return lax.rsqrt(jnp.mean(value * value, axis=-1, keepdims=True) + EPSILON)


def attention_forward(
    x_ref, ga_ref, wq_ref, wkv_ref, wo_ref, cos_ref, sin_ref,
    h1_ref, mixed_ref, q_ref, k_ref, v_ref, lse_ref, o_acc,
):
    seq_len = x_ref.shape[0]
    low = low_half(BLOCK)

    def project(b, carry):
        rows = pl.ds(pl.multiple_of(b * BLOCK, BLOCK), BLOCK)
        stream = x_ref[rows, :].astype(F32)
        normed = (stream * rms(stream) * ga_ref[...]).astype(BF)
        cosine = cos_ref[rows, :]
        sine = sin_ref[rows, :]

        def rope(value):
            return value * cosine + swap_halves(value) * sine

        queries = nn(normed, wq_ref[...])
        for j in range(Q_TILES):
            q_ref[j, rows, :] = (rope(tile(queries, j)) * HD ** (-0.5)).astype(BF)
        keys_values = nn(normed, wkv_ref[...])
        first = rope(tile(keys_values, 0))
        second = tile(keys_values, 1)
        third = tile(keys_values, 2)
        mid = rope(second)

        def put(ref, index, value):
            ref[index, rows, :] = value.astype(BF)

        put(k_ref, 0, jnp.where(low, first, 0.0))
        put(k_ref, 1, jnp.where(low, 0.0, flip(first)))
        put(k_ref, 2, jnp.where(low, flip(first), 0.0))
        put(k_ref, 3, jnp.where(low, 0.0, first))
        put(k_ref, 4, jnp.where(low, mid, 0.0))
        put(k_ref, 5, jnp.where(low, 0.0, flip(mid)))
        put(v_ref, 0, jnp.where(low, flip(second), 0.0))
        put(v_ref, 1, jnp.where(low, 0.0, second))
        put(v_ref, 2, jnp.where(low, third, 0.0))
        put(v_ref, 3, jnp.where(low, 0.0, flip(third)))
        put(v_ref, 4, jnp.where(low, flip(third), 0.0))
        put(v_ref, 5, jnp.where(low, 0.0, third))
        return carry

    lax.fori_loop(0, seq_len // BLOCK, project, 0)
    lane = lax.broadcasted_iota(jnp.int32, (BLOCK, LANES), 1)
    keep = lax.broadcasted_iota(jnp.int32, (BLOCK, BLOCK), 1) <= lax.broadcasted_iota(
        jnp.int32, (BLOCK, BLOCK), 0
    )
    for b in range(seq_len // BLOCK):
        rows = slice(b * BLOCK, (b + 1) * BLOCK)
        n_keys = (b + 1) * BLOCK
        o_acc[...] = jnp.zeros_like(o_acc)

        def group(g, lse, rows=rows, n_keys=n_keys):
            for u in range(3):
                head = 3 * g + u
                j = head // 2
                side = 2 * g + head % 2
                scores = nt(q_ref[j, rows, :], k_ref[side, 0:n_keys, :])
                diag = jnp.where(keep, scores[:, n_keys - BLOCK :], MASKED)
                if n_keys > BLOCK:
                    scores = jnp.concatenate([scores[:, : n_keys - BLOCK], diag], axis=1)
                else:
                    scores = diag
                row_max = jnp.max(scores, axis=-1, keepdims=True)
                exponent = jnp.exp(scores - row_max)
                total = jnp.sum(exponent, axis=-1, keepdims=True)
                prob = (exponent * (1.0 / total)).astype(BF)
                o_acc[j] += nn(prob, v_ref[side, 0:n_keys, :])
                lse = jnp.where(lane == head, row_max + jnp.log(total), lse)
            return lse

        lse = lax.fori_loop(0, KV, group, jnp.zeros((BLOCK, LANES), F32))
        lse_ref[:, rows] = lse.T[:16]
        mixed = jnp.concatenate([o_acc[j].astype(BF) for j in range(Q_TILES)], axis=1)
        mixed_ref[rows, :] = mixed
        h1_ref[rows, :] = x_ref[rows, :].astype(F32) + nn(mixed, wo_ref[...])


def prepare_weights(
    core_ref, own_ref, other_ref,
    ga_ref, gm_ref, wq_ref, wkv_ref, wo_ref, wg_ref, wu_ref, wd_ref,
    both, flat, tmp, sem,
):
    core = core_ref[0]
    copies = [
        pltpu.make_async_copy(own_ref, both.at[core], sem.at[0]),
        pltpu.make_async_copy(other_ref, both.at[1 - core], sem.at[1]),
    ]
    for copy in copies:
        copy.start()
    for copy in copies:
        copy.wait()
    step = HALF_ROWS // 13

    def widen(which):
        def body(i, carry):
            rows = pl.ds(pl.multiple_of(i * step, 8), step)
            flat[rows, :] = both[which, rows, :].astype(F32)
            return carry

        lax.fori_loop(0, 13, body, 0)

    def interleave(even, odd, pairs, out_ref, first_row, pad):
        low = low_half(2 * pairs)
        for t in range(Q_TILES):
            tmp[pl.ds(t * D, pairs, stride=2), :] = even[t]
            tmp[pl.ds(t * D + 1, pairs, stride=2), :] = odd[t]
        rows = pl.ds(first_row, 2 * pairs)
        for t in range(Q_TILES):
            value = tmp[t * D : t * D + 2 * pairs, :]
            if t < 4:
                out_ref[rows, t * LANES : (t + 1) * LANES] = value.astype(BF)
            elif pad:
                out_ref[rows, t * LANES :] = jnp.where(low, value, 0.0).astype(BF)
            else:
                out_ref[rows, t * LANES :] = value[:, :HD].astype(BF)

    def wide(row, out_ref, pad):
        pairs = D // 2
        low = low_half(pairs)
        cols = [flat[pl.ds(row + c, pairs, stride=9), :] for c in range(9)]
        turned = [flip(cols[c]) for c in range(4, 9)]
        odd = [jnp.where(low, turned[t], turned[t + 1]) for t in range(4)] + [turned[4]]
        interleave(cols[:5], odd, pairs, out_ref, 0, pad)

    widen(0)
    low1 = low_half(1)
    turned = [flip(flat[4 + r : 5 + r, :]) for r in range(5)]
    for r in range(4):
        ga_ref[:, r * LANES : (r + 1) * LANES] = flat[r : r + 1, :]
        gm_ref[:, r * LANES : (r + 1) * LANES] = jnp.where(low1, turned[r], turned[r + 1])
    ga_ref[:, 4 * LANES :] = flat[4:5, :HD]
    gm_ref[:, 4 * LANES :] = turned[4][:, :HD]
    wide(9, wq_ref, True)
    wide(O_ROW, wo_ref, False)
    wo_ref[D:, :] = jnp.zeros((PAD_D - D, D), BF)
    pairs = D // 2
    low = low_half(pairs)
    narrow = []
    for row in (2601, 3465):
        cols = [flat[pl.ds(row + c, pairs, stride=3), :] for c in range(3)]
        turned = [flip(cols[1]), flip(cols[2])]
        even = cols[:2]
        odd = [jnp.where(low, turned[0], turned[1]), turned[1]]
        for t in range(2):
            tmp[pl.ds(t * D, pairs, stride=2), :] = even[t]
            tmp[pl.ds(t * D + 1, pairs, stride=2), :] = odd[t]
        narrow.append((tmp[0:D, :], tmp[D : 2 * D, :]))
    (k0, k1), (v0, v1) = narrow
    low = low_half(D)
    v0 = flip(v0)
    v1 = flip(v1)
    wkv_ref[:, 0:LANES] = k0.astype(BF)
    wkv_ref[:, LANES : 2 * LANES] = jnp.where(low, k1, v0).astype(BF)
    wkv_ref[:, 2 * LANES :] = jnp.where(low, v0, v1).astype(BF)
    head = both[1, 0:16, :].astype(F32)
    turned = flip(head)
    for r in range(5):
        row = GATE_ROW + FF_TILES * (D - 1) + 7 + r
        before = flat[row : row + 1, :] if r == 0 else turned[r - 1 : r]
        flat[row : row + 1, :] = jnp.where(low1, before, turned[r : r + 1])
    for t in range(FF_TILES):
        wg_ref[:, t * LANES : (t + 1) * LANES] = flat[
            pl.ds(GATE_ROW + t, D, stride=FF_TILES), :
        ].astype(BF)
    widen(1)
    here = flip(flat[pl.ds(4, D, stride=FF_TILES), :])
    for t in range(FF_TILES):
        after = flip(flat[pl.ds(5 + t, D, stride=FF_TILES), :])
        wu_ref[:, t * LANES : (t + 1) * LANES] = jnp.where(low, here, after).astype(BF)
        here = after

    def down(i, carry):
        n_pairs = 96
        low = low_half(n_pairs)
        start = 6916 + 9 * n_pairs * i
        cols = [flat[pl.ds(start + c, n_pairs, stride=9), :] for c in range(10)]
        turned = [flip(cols[c]) for c in range(6)]
        even = [jnp.where(low, turned[c], turned[c + 1]) for c in range(5)]
        interleave(even, cols[5:], n_pairs, wd_ref, pl.multiple_of(2 * n_pairs * i, 16), False)
        return carry

    lax.fori_loop(0, FF // 192, down, 0)


def transposed(value):
    rows = value.shape[0]
    pieces = [tile(value, t) for t in range(4)]
    pieces.append(
        jnp.concatenate([value[:, 4 * LANES :], jnp.zeros((rows, LANES - HD), F32)], axis=1)
    )
    return jnp.concatenate([piece.T for piece in pieces], axis=0)


def mlp_pass(
    core_ref, slot_ref, lengths_ref, assignment_ref,
    h1_hbm, cot_hbm, mixed_hbm, gm_ref, wo_hbm, wg_hbm, wu_hbm, wd_hbm,
    out_hbm, dh1_hbm, dm_hbm, ggm_ref, keep_ref, send_ref,
    h1_ref, cot_ref, mixed_ref, wo_ref, wg_ref, wu_ref, wd_ref, out_ref, dh1_ref, dm_ref,
    nmt_s, backt_s, inner_s, dg_s, du_s, da_s, grads, in_sem, out_sem, sem,
):
    seq_len = h1_ref.shape[0]
    core = core_ref[0]
    live_len = lengths_ref[assignment_ref[slot_ref[0]]]
    n_cols = FF // MLP_COLS
    loads = [
        pltpu.make_async_copy(source, target, in_sem.at[i])
        for i, (source, target) in enumerate(
            (
                (h1_hbm, h1_ref),
                (cot_hbm, cot_ref),
                (wg_hbm, wg_ref),
                (wu_hbm, wu_ref),
                (wd_hbm, wd_ref),
                (wo_hbm, wo_ref),
                (mixed_hbm, mixed_ref),
            )
        )
    ]
    for copy in loads:
        copy.start()
    for copy in loads[:6]:
        copy.wait()

    def results(b):
        rows = pl.ds(pl.multiple_of(b * MLP_BLOCK, MLP_BLOCK), MLP_BLOCK)
        pairs = [(out_ref.at[rows], out_hbm.at[rows]), (dh1_ref.at[rows], dh1_hbm.at[rows])]
        pairs.append((dm_ref.at[:, rows], dm_hbm.at[:, rows]))
        return [
            pltpu.make_async_copy(source, target, out_sem.at[b, i])
            for i, (source, target) in enumerate(pairs)
        ]

    def block(b, ggm):
        start = pl.multiple_of(b * MLP_BLOCK, MLP_BLOCK)
        rows = pl.ds(start, MLP_BLOCK)
        hidden1 = h1_ref[rows, :]
        r2 = rms(hidden1)
        gain = gm_ref[...]
        normed2_wide = hidden1 * r2 * gain
        normed2 = normed2_wide.astype(BF)
        nmt_s[:, rows] = transposed(normed2_wide).astype(BF)
        live = (
            start + lax.broadcasted_iota(jnp.int32, (MLP_BLOCK, 1), 0) < live_len
        ).astype(F32)

        back = cot_ref[rows, :].astype(F32) * live
        back_low = back.astype(BF)
        backt_s[:, rows] = transposed(back).astype(BF)
        def columns(c):
            cols = pl.ds(pl.multiple_of(c * MLP_COLS, MLP_COLS), MLP_COLS)
            gate = nn(normed2, wg_ref[:, cols])
            up = nn(normed2, wu_ref[:, cols])
            d_inner = nt(back_low, wd_ref[cols, :])
            sig = jax.nn.sigmoid(gate)
            silu = gate * sig
            inner_s[rows, cols] = (silu * up).astype(BF)
            dg_s[rows, cols] = (d_inner * up * sig * (1.0 + gate * (1.0 - sig))).astype(BF)
            du_s[rows, cols] = (d_inner * silu).astype(BF)

        def some_columns(i, carry):
            for c in range(MLP_UNROLL):
                columns(MLP_UNROLL * i + c)
            return carry

        lax.fori_loop(0, n_cols // MLP_UNROLL, some_columns, 0)
        out_ref[rows, :] = ((hidden1 + nn(inner_s[rows, :], wd_ref[...])) * live).astype(BF)
        d_normed2 = nt(dg_s[rows, :], wg_ref[...]) + nt(du_s[rows, :], wu_ref[...])
        scaled = d_normed2 * gain
        d_hidden1 = (
            back
            + r2 * scaled
            - hidden1 * (r2 * r2 * r2) * jnp.mean(scaled * hidden1, axis=-1, keepdims=True)
        )
        dh1_ref[rows, :] = d_hidden1
        d_attn = d_hidden1.astype(BF)
        da_s[rows, :] = d_attn

        d_mixed = nt(d_attn, wo_ref[...]).astype(BF)
        for j in range(Q_TILES):
            dm_ref[j, rows, :] = tile(d_mixed, j)
        for copy in results(b):
            copy.start()
        return ggm + jnp.sum(d_normed2 * hidden1 * r2, axis=0, keepdims=True)

    ggm_ref[...] = lax.fori_loop(0, seq_len // MLP_BLOCK, block, jnp.zeros((1, D), F32))

    def put(half, index, value):
        grads[half, pl.ds(pl.multiple_of(index * D, D), D), :] = value

    def leave(c):
        rows = pl.ds(pl.multiple_of(2 * c * D, D), 2 * D)
        return [
            pltpu.make_async_copy(grads.at[1 - core, rows], send_ref.at[rows], sem.at[c, 0]),
            pltpu.make_async_copy(grads.at[core, rows], keep_ref.at[rows], sem.at[c, 1]),
        ]

    def weights(c, carry):
        cols = pl.ds(pl.multiple_of(c * 2 * LANES, 2 * LANES), 2 * LANES)
        grad_gate = nn(nmt_s[:D, :], dg_s[:, cols]).astype(BF)
        grad_up = nn(nmt_s[:D, :], du_s[:, cols]).astype(BF)
        for t in range(2):
            put(0, 2 * c + t, tile(grad_gate, t))
            put(1, 2 * c + t, tile(grad_up, t))
        for copy in leave(c):
            copy.start()
        grad_down = nn(backt_s[:D, :], inner_s[:, cols]).astype(BF)
        part = jnp.where(c < DOWN_FIRST // 2, 0, 1)
        base = jnp.where(c < DOWN_FIRST // 2, FF_TILES + Q_TILES, FF_TILES - DOWN_FIRST)
        for t in range(2):
            put(part, base + 2 * c + t, tile(grad_down, t))
        return carry

    lax.fori_loop(0, n_cols, weights, 0)
    loads[6].wait()
    grad_o = tn(mixed_ref[...], da_s[...])[:D]
    for t in range(4):
        put(0, FF_TILES + t, tile(grad_o, t).astype(BF))
    put(0, FF_TILES + 4, half_tile(grad_o).astype(BF))
    grads[0, EXTRA:, :] = jnp.zeros((EARLY_ROWS - EXTRA, LANES), BF)
    grads[1, EXTRA - D :, :] = jnp.zeros((EARLY_ROWS - EXTRA + D, LANES), BF)
    row = lax.broadcasted_iota(jnp.int32, (16, LANES), 0)
    rest = jnp.zeros((16, LANES), F32)
    for r in range(5):
        start = (8 + r) * D - 16
        last = grads[0, start : start + 16, :].astype(F32)[15:16]
        rest = jnp.where(row == r, jnp.broadcast_to(last, (16, LANES)), rest)
    grads[0, EXTRA + 16 : EXTRA + 32, :] = rest.astype(BF)
    rows = pl.ds(FF_TILES * D, EARLY_ROWS - FF_TILES * D)
    final = [
        pltpu.make_async_copy(grads.at[1 - core, rows], send_ref.at[rows], sem.at[n_cols, 0]),
        pltpu.make_async_copy(grads.at[core, rows], keep_ref.at[rows], sem.at[n_cols, 1]),
    ]
    for copy in final:
        copy.start()

    def drain(c, carry):
        for copy in leave(c):
            copy.wait()
        return carry

    def drain_results(b, carry):
        for copy in results(b):
            copy.wait()
        return carry

    lax.fori_loop(0, n_cols, drain, 0)
    lax.fori_loop(0, seq_len // MLP_BLOCK, drain_results, 0)
    for copy in final:
        copy.wait()


def half_tile(value):
    rows = value.shape[0]
    return jnp.concatenate([value[:, 4 * LANES : D], jnp.zeros((rows, HD), value.dtype)], axis=1)


def gain_rows(value):
    row = lax.broadcasted_iota(jnp.int32, (16, LANES), 0)
    whole = jnp.zeros((16, LANES), F32)
    for t in range(Q_TILES):
        piece = tile(value, t) if t < 4 else half_tile(value)
        whole = jnp.where(row == t, jnp.broadcast_to(piece, (16, LANES)), whole)
    return whole


def backward_groups(
    first, q_ref, dm_ref, k_ref, v_ref, lse_ref, dq_ref, dk_ref, dv_ref, dk_acc, dv_acc
):
    seq_len = q_ref.shape[1]
    group = first + pl.program_id(0)
    dq_ref[...] = jnp.zeros_like(dq_ref)
    dk_acc[...] = jnp.zeros_like(dk_acc)
    dv_acc[...] = jnp.zeros_like(dv_acc)
    keep = lax.broadcasted_iota(jnp.int32, (BLOCK, BLOCK), 0) <= lax.broadcasted_iota(
        jnp.int32, (BLOCK, BLOCK), 1
    )
    for b in range(seq_len // BLOCK):
        rows = slice(b * BLOCK, (b + 1) * BLOCK)
        n_keys = (b + 1) * BLOCK
        for u in range(3):
            head = 3 * group + u
            j = lax.shift_right_logical(head, 1)
            own = j - lax.shift_right_logical(3 * group, 1)
            side = head - 2 * j
            queries = q_ref[j, rows, :]
            d_mixed = dm_ref[j, rows, :]
            keys = k_ref[side, 0:n_keys, :]
            values = v_ref[side, 0:n_keys, :]
            prob = jnp.exp(nt(keys, queries) - lse_ref[pl.ds(head, 1), rows])
            diag = jnp.where(keep, prob[n_keys - BLOCK :, :], 0.0)
            if n_keys > BLOCK:
                prob = jnp.concatenate([prob[: n_keys - BLOCK, :], diag], axis=0)
            else:
                prob = diag
            d_prob = nt(values, d_mixed)
            delta = jnp.sum(d_prob * prob, axis=0, keepdims=True)
            d_score = (prob * (d_prob - delta)).astype(BF)
            dv_acc[side, 0:n_keys, :] += nn(prob.astype(BF), d_mixed)
            dk_acc[side, 0:n_keys, :] += nn(d_score, queries)
            dq_ref[0, own, rows, :] += tn(d_score, keys)
    dk_ref[0] = dk_acc[0] + flip(dk_acc[1])
    dv_ref[0] = dv_acc[0] + flip(dv_acc[1])


def backward_finish(
    x_ref, ga_ref, dh1_ref, dqa_ref, dka_ref, dva_ref, dqb_ref, dkb_ref, dvb_ref,
    wq_ref, wkv_ref, cos_ref, sin_ref,
    dx_ref, dq_s, dkv_s, nm_s, gga_ref,
):
    seq_len = x_ref.shape[0]
    low = low_half(BLOCK)

    def block(b, gga):
        rows = pl.ds(pl.multiple_of(b * BLOCK, BLOCK), BLOCK)
        cosine = cos_ref[rows, :]
        sine = sin_ref[rows, :]

        def unrope(value):
            return value * cosine - swap_halves(value) * sine

        d_rot = [
            dqa_ref[0, 0, rows, :],
            dqa_ref[0, 1, rows, :] + dqb_ref[0, 0, rows, :],
            dqb_ref[0, 1, rows, :],
            dqb_ref[1, 0, rows, :],
            dqb_ref[1, 1, rows, :],
        ]
        for j in range(Q_TILES):
            d_query = unrope(d_rot[j]) * HD ** (-0.5)
            dq_s[rows, j * LANES : (j + 1) * LANES] = d_query.astype(BF)
        dk = [dka_ref[0, rows, :], dkb_ref[0, rows, :], dkb_ref[1, rows, :]]
        dv = [dva_ref[0, rows, :], dvb_ref[0, rows, :], dvb_ref[1, rows, :]]
        first = unrope(jnp.where(low, dk[0], flip(dk[1])))
        second = jnp.where(low, unrope(dk[2]), flip(dv[0]))
        third = jnp.where(low, dv[1], flip(dv[2]))
        dkv_s[rows, 0:LANES] = first.astype(BF)
        dkv_s[rows, LANES : 2 * LANES] = second.astype(BF)
        dkv_s[rows, 2 * LANES :] = third.astype(BF)
        d_normed = nt(dq_s[rows, :], wq_ref[...]) + nt(dkv_s[rows, :], wkv_ref[...])
        stream = x_ref[rows, :].astype(F32)
        r1 = rms(stream)
        gain = ga_ref[...]
        nm_s[rows, :] = (stream * r1 * gain).astype(BF)
        scaled = d_normed * gain
        dx_ref[rows, :] = (
            dh1_ref[rows, :]
            + r1 * scaled
            - stream * (r1 * r1 * r1) * jnp.mean(scaled * stream, axis=-1, keepdims=True)
        ).astype(BF)
        return gga + jnp.sum(d_normed * stream * r1, axis=0, keepdims=True)

    gga_ref[...] = lax.fori_loop(0, seq_len // BLOCK, block, jnp.zeros((1, D), F32))


def late_weights(
    core_ref, nm_s, dq_s, dkv_s, gga_ref, ggm_ref, keep_ref, send_ref, late, sem
):
    grad_q = tn(nm_s[...], dq_s[...]).astype(BF)
    grad_kv = tn(nm_s[...], dkv_s[...]).astype(BF)
    for t in range(Q_TILES):
        late[t * D : (t + 1) * D, :] = tile(grad_q, t)
    for t in range(3):
        late[(Q_TILES + t) * D : (Q_TILES + t + 1) * D, :] = tile(grad_kv, t)
    late[8 * D :, :] = jnp.zeros((2 * LATE_HALF - 8 * D, LANES), BF)
    late[8 * D : 8 * D + 16, :] = gain_rows(gga_ref[...]).astype(BF)
    late[8 * D + 16 : 8 * D + 32, :] = gain_rows(ggm_ref[...]).astype(BF)
    copies = []
    for i, (which, ref) in enumerate(((1 - core_ref[0], send_ref), (core_ref[0], keep_ref))):
        rows = pl.ds(pl.multiple_of(which * LATE_HALF, 8), LATE_HALF)
        copies.append(pltpu.make_async_copy(late.at[rows], ref, sem.at[i]))
    for copy in copies:
        copy.start()
    for copy in copies:
        copy.wait()


def gather_sum(bits_ref, *refs, n_parts, rows, split, merge, joined):
    n_in = 1 if joined else n_parts
    kept, got = refs[:n_in], refs[n_in : 2 * n_in]
    kinds = 2 if split else 1
    n_out = kinds * (1 if merge else n_parts)
    outs = refs[2 * n_in : 2 * n_in + n_out]
    scratch, sem = refs[2 * n_in + n_out :]
    size = rows // kinds
    copies = []
    for p in range(n_parts):
        if joined:
            part = slice(p * rows, (p + 1) * rows)
            total = kept[0][part, :].astype(F32) + got[0][part, :].astype(F32)
        else:
            total = kept[p][...].astype(F32) + got[p][...].astype(F32)
        scratch[p] = total.astype(BF)
        for i in range(kinds):
            if merge:
                target = outs[i].at[pl.ds(p * size, size)]
            else:
                target = outs[p + i * n_parts]
            start = (bits_ref[p] if i else 1 - bits_ref[p]) * size if split else 0
            source = scratch.at[p, pl.ds(pl.multiple_of(start, 8), size)]
            copies.append(pltpu.make_async_copy(source, target, sem.at[2 * p + i]))
            copies[-1].start()
    for copy in copies:
        copy.wait()


def join_halves(bits_ref, *refs, n_parts, rows, merged):
    n_in = 1 if merged else n_parts
    own, got, outs = refs[:n_in], refs[n_in : 2 * n_in], refs[2 * n_in : 2 * n_in + n_parts]
    sem = refs[2 * n_in + n_parts]
    copies = []
    for p in range(n_parts):
        for i, (group, which) in enumerate(((own, bits_ref[p]), (got, 1 - bits_ref[p]))):
            source = group[0].at[pl.ds(p * rows, rows)] if merged else group[p]
            span = pl.ds(pl.multiple_of(which * rows, 8), rows)
            copies.append(pltpu.make_async_copy(source, outs[p].at[span], sem.at[2 * p + i]))
            copies[-1].start()
    for copy in copies:
        copy.wait()


def put_wide(flat, tmp, values, rows, row):
    pairs = rows // 2
    for index, value in enumerate(values):
        tmp[pl.ds(index * D, rows), :] = value
    even = [tmp[pl.ds(i * D, pairs, stride=2), :] for i in range(Q_TILES)]
    odd = [flip(tmp[pl.ds(i * D + 1, pairs, stride=2), :]) for i in range(Q_TILES)]
    low = low_half(pairs)
    for c in range(4):
        flat[pl.ds(row + c, pairs, stride=9), :] = even[c]
    flat[pl.ds(row + 4, pairs, stride=9), :] = jnp.where(low, even[4], odd[0])
    for c in range(4):
        flat[pl.ds(row + 5 + c, pairs, stride=9), :] = jnp.where(low, odd[c], odd[c + 1])


def update_rule(scale, rate, grad, master, momentum, average):
    weight_grad = grad * scale
    new_momentum = MOMENTUM_DECAY * momentum + weight_grad
    new_master = master - rate * (weight_grad + MOMENTUM_DECAY * new_momentum)
    new_average = AVERAGE_DECAY * average + (1.0 - AVERAGE_DECAY) * new_master
    return weight_grad, new_momentum, new_master, new_average


class Chunks:
    def __init__(self, rows, base, count, rule, refs):
        self.rows, self.base, self.count, self.rule = rows, base, count, rule
        self.ins, self.outs, self.in_buf, self.out_buf, self.in_sem, self.out_sem = refs
        self.size = rows * LANES

    def span(self, c):
        return pl.ds(pl.multiple_of((self.base + c * self.rows) * LANES, LANES), self.size)

    def place(self, index, start=0, length=None):
        start = pl.multiple_of(index * self.size + start, 8 * LANES)
        return pl.ds(start, self.size if length is None else length)

    def fetch(self, c):
        return [
            pltpu.make_async_copy(
                self.ins[i].at[self.span(c)],
                self.in_buf.at[self.place(c * 3 + i)],
                self.in_sem.at[c, i],
            )
            for i in range(3)
        ]

    def flush(self, c):
        return [
            pltpu.make_async_copy(
                self.out_buf.at[self.place(c * 4 + i)],
                self.outs[i].at[self.span(c)],
                self.out_sem.at[c, i],
            )
            for i in range(4)
        ]

    def start(self):
        def body(c, carry):
            for copy in self.fetch(c):
                copy.start()
            return carry

        lax.fori_loop(0, self.count, body, 0)

    def run(self, stage, gradient):
        sub = STEP * LANES

        def body(c, carry):
            stage(c)
            for copy in self.fetch(c):
                copy.wait()

            def step(s, inner):
                grad = gradient(c, s * STEP, STEP).reshape(sub)
                values = self.rule(
                    grad, *[self.in_buf[self.place(c * 3 + i, s * sub, sub)] for i in range(3)]
                )
                for i in range(4):
                    self.out_buf[self.place(c * 4 + i, s * sub, sub)] = values[i]
                return inner

            lax.fori_loop(0, self.rows // STEP, step, 0)
            for copy in self.flush(c):
                copy.start()
            return carry

        def drain(c, carry):
            for copy in self.flush(c):
                copy.wait()
            return carry

        lax.fori_loop(0, self.count, body, 0)
        return lambda: lax.fori_loop(0, self.count, drain, 0)


class Extra:
    def __init__(self, start, ins, outs, rest):
        self.bufs, self.sem = rest[:8], rest[8]
        count = self.bufs[0].shape[0]
        span = pl.ds(start, count)
        self.count = count
        self.loads = [
            pltpu.make_async_copy(ins[i].at[span], self.bufs[i], self.sem.at[i]) for i in range(3)
        ]
        self.stores = [
            pltpu.make_async_copy(self.bufs[3 + i], outs[i].at[span], self.sem.at[3 + i])
            for i in range(4)
        ]

    def start(self):
        for copy in self.loads:
            copy.start()

    def finish(self, grad, rule):
        for copy in self.loads:
            copy.wait()
        self.bufs[7][...] = grad.reshape(grad.shape[0] * LANES)
        values = rule(self.bufs[7][pl.ds(0, self.count)], *[self.bufs[i][...] for i in range(3)])
        for i in range(4):
            self.bufs[3 + i][...] = values[i]
            self.stores[i].start()

    def drain(self):
        for copy in self.stores:
            copy.wait()


def shifted(flat, row, count):
    here = flip(flat[pl.ds(row - 1, count), :])
    after = flip(flat[pl.ds(row, count), :])
    return jnp.where(low_half(count), here, after)


def load_parts(pieces, sem):
    copies = [
        pltpu.make_async_copy(source, target, sem.at[i]) for i, (source, target) in enumerate(pieces)
    ]
    for copy in copies:
        copy.start()
    return copies


FLAT_BASE = 8
TAIL_ZERO = HALF - (GATE_ROW + 11 * CHUNK) * LANES
TAIL_ONE = HALF - (6916 + 11 * CHUNK) * LANES


def update_first(scale, rate, core_ref, bits_ref, *rest):
    halves, ins, outs = rest[:4], rest[4:7], rest[7:11]
    early_ref, flat, in_buf, out_buf, in_sem, out_sem, part_sem = rest[11:18]
    refs = (ins, outs, in_buf, out_buf, in_sem, out_sem)
    core = core_ref[0]
    rule = functools.partial(update_rule, scale, rate)
    half = PART_ROWS // 2
    pieces = []
    for p in range(2):
        for i, which in enumerate((bits_ref[p], 1 - bits_ref[p])):
            span = pl.ds(pl.multiple_of(p * PART_ROWS + which * half, 8), half)
            pieces.append((halves[2 * p + i], early_ref.at[span]))
    copies = load_parts(pieces, part_sem)
    extra = Extra((GATE_ROW + 11 * CHUNK) * LANES, ins, outs, rest[18:])
    base = jnp.where(core == 0, GATE_ROW, 4)
    chunks = Chunks(CHUNK, base, 11 + core, rule, refs)
    chunks.start()

    @pl.when(core == 0)
    def _():
        extra.start()

    for copy in copies:
        copy.wait()
    flat[0:FLAT_BASE, :] = jnp.zeros((FLAT_BASE, LANES), F32)

    def stage(c):
        for t in range(FF_TILES):
            rows = pl.ds(pl.multiple_of(t * D + c * 48, 16), 48)
            flat[pl.ds(FLAT_BASE + t, 48, stride=FF_TILES), :] = early_ref[rows, :].astype(F32)

    def gradient(c, start, count):
        row = pl.multiple_of(FLAT_BASE + start, 8)
        return jnp.where(core == 0, flat[pl.ds(row, count), :], shifted(flat, row, count))

    def stage_next(c):
        flat[FLAT_BASE - 1 : FLAT_BASE, :] = flat[FLAT_BASE + CHUNK - 1 : FLAT_BASE + CHUNK, :]
        stage(c)

    drain = chunks.run(stage_next, gradient)

    @pl.when(core == 0)
    def _():
        stage(11)
        extra.finish(flat[FLAT_BASE : FLAT_BASE + CHUNK, :], rule)

    drain()

    @pl.when(core == 0)
    def _():
        extra.drain()


def update_second(scale, rate, core_ref, bits_ref, *rest):
    halves, ins, outs = rest[:8], rest[8:11], rest[15:19]
    flat, tmp, part_ref, swap_ref, first_ref, in_buf, out_buf, in_sem, out_sem, part_sem = rest[19:29]
    refs = (ins, outs, in_buf, out_buf, in_sem, out_sem)
    tail = Extra((6916 + 11 * CHUNK) * LANES, ins, outs, rest[29:38])
    head = Extra(0, ins, outs, rest[38:])
    rule = functools.partial(update_rule, scale, rate)
    half = PART_ROWS // 2
    pieces = []
    for i in range(2):
        which = [1 - bits_ref[p] if i else bits_ref[p] for p in range(3)]

        def rows(start, p, size, which=which):
            return pl.ds(pl.multiple_of(start + which[p] * size, 16), size)

        source = halves[2 + i].at[pl.ds(half - REST_SLOT, REST_SLOT)]
        pieces.append((source, part_ref.at[rows(0, 1, REST_SLOT)]))
        pieces.append((halves[4 + i], part_ref.at[rows(2 * REST_SLOT, 2, half)]))
        pieces.append((halves[6 + i], swap_ref.at[rows(0, 2, half)]))
        pieces.append((halves[i].at[pl.ds(0, 16)], first_ref.at[rows(0, 0, 16)]))
    parts = load_parts(pieces, part_sem)

    @pl.when(core_ref[0] == 0)
    def _():
        def stage(c):
            values = []
            for t in range(Q_TILES):
                rows = pl.ds(pl.multiple_of(REST + t * D + c * 64, 16), 64)
                values.append(part_ref[rows, :].astype(F32))
            put_wide(flat, tmp, values, 64, FLAT_BASE)

        def gradient(c, start, count):
            return flat[pl.ds(pl.multiple_of(FLAT_BASE + start, 8), count), :]

        chunks = Chunks(CHUNK // 2, O_ROW, 9, rule, refs)
        chunks.start()
        for copy in parts:
            copy.wait()
        chunks.run(stage, gradient)()

    @pl.when(core_ref[0] == 1)
    def _():
        head.start()
        chunks = Chunks(CHUNK, 6916, 11, rule, refs)
        chunks.start()
        tail.start()
        for copy in parts:
            copy.wait()
        flat[0:FLAT_BASE, :] = jnp.zeros((FLAT_BASE, LANES), F32)
        flat[FLAT_BASE : FLAT_BASE + 8, :] = swap_ref[SWAP_TAIL : SWAP_TAIL + 16, :].astype(F32)[0:8]
        flat[FLAT_BASE + 5 : FLAT_BASE + 6, :] = first_ref[0:16, :].astype(F32)[0:1]
        head.finish(shifted(flat, FLAT_BASE + 1, 8), rule)
        row = FLAT_BASE + CHUNK - 1
        flat[row : row + 1, :] = part_ref[REST - 16 : REST, :].astype(F32)[15:16]

        def stage(c):
            flat[FLAT_BASE - 1 : FLAT_BASE, :] = flat[FLAT_BASE + CHUNK - 1 : FLAT_BASE + CHUNK, :]
            inside = c < DOWN_FIRST
            here = pl.ds(pl.multiple_of(SWAP_START + jnp.where(inside, c, 0) * D, 16), D)
            there = pl.ds(pl.multiple_of(REST + jnp.where(inside, 0, c - DOWN_FIRST) * D, 16), D)
            whole = jnp.where(inside, swap_ref[here, :].astype(F32), part_ref[there, :].astype(F32))
            pieces = [whole[i * LANES : (i + 1) * LANES].T for i in range(4)]
            half = jnp.concatenate([whole[4 * LANES :], jnp.zeros((LANES - HD, LANES), F32)], axis=0)
            put_wide(flat, tmp, pieces + [half.T], LANES, FLAT_BASE)

        def gradient(c, start, count):
            return shifted(flat, FLAT_BASE + start, count)

        drain = chunks.run(stage, gradient)
        stage(11)
        flat[FLAT_BASE + CHUNK :, :] = jnp.zeros((8, LANES), F32)
        tail.finish(shifted(flat, FLAT_BASE, CHUNK + 8), rule)
        head.drain()
        drain()
        tail.drain()


def update_late(scale, rate, core_ref, own_ref, other_ref, *rest):
    ins, outs = rest[:3], rest[7:11]
    flat, tmp, late_ref, in_buf, out_buf, in_sem, out_sem = rest[11:18]
    refs = (ins, outs, in_buf, out_buf, in_sem, out_sem)
    extra = Extra(LATE_CHUNKS * CHUNK * LANES, ins, outs, rest[18:])
    rule = functools.partial(update_rule, scale, rate)

    @pl.when(core_ref[0] == 0)
    def _():
        chunks = Chunks(CHUNK, 0, LATE_CHUNKS, rule, refs)
        chunks.start()
        extra.start()
        late_ref[:LATE_HALF, :] = own_ref[...]
        late_ref[LATE_HALF:, :] = other_ref[...]

        def late(index):
            return late_ref[index * D : (index + 1) * D, :].astype(F32)

        low1 = low_half(1)
        gain_a = late_ref[8 * D : 8 * D + 16, :].astype(F32)
        gain_m = flip(late_ref[8 * D + 16 : 8 * D + 32, :].astype(F32))
        for r in range(4):
            flat[r : r + 1, :] = gain_a[r : r + 1]
        flat[4:5, :] = jnp.where(low1, gain_a[4:5], gain_m[0:1])
        for r in range(4):
            flat[5 + r : 6 + r, :] = jnp.where(low1, gain_m[r : r + 1], gain_m[r + 1 : r + 2])
        put_wide(flat, tmp, [late(t) for t in range(Q_TILES)], D, 9)
        pairs = D // 2
        for t in range(3):
            tmp[pl.ds(t * D, D), :] = late(Q_TILES + t)
        even = [tmp[pl.ds(i * D, pairs, stride=2), :] for i in range(3)]
        odd = [tmp[pl.ds(i * D + 1, pairs, stride=2), :] for i in range(3)]
        low = low_half(pairs)
        turned = [flip(odd[0]), flip(odd[1]), flip(even[1]), flip(even[2])]
        rows = (
            (2601, even[0]),
            (2602, jnp.where(low, even[1], turned[0])),
            (2603, jnp.where(low, turned[0], turned[1])),
            (3465, jnp.where(low, turned[2], turned[3])),
            (3466, jnp.where(low, turned[3], odd[1])),
            (3467, odd[2]),
        )
        for row, value in rows:
            flat[pl.ds(row, pairs, stride=3), :] = value

        def gradient(c, start, count):
            return flat[pl.ds(pl.multiple_of(c * CHUNK + start, 8), count), :]

        drain = chunks.run(lambda c: None, gradient)
        start = LATE_CHUNKS * CHUNK
        extra.finish(flat[start : start + 304, :], rule)
        drain()
        extra.drain()


def vmem():
    return pl.BlockSpec(memory_space=pltpu.VMEM)


def smem():
    return pl.BlockSpec(memory_space=pltpu.SMEM)


def hbm():
    return pl.BlockSpec(memory_space=pl.ANY)


def call(kernel, outs, in_specs, out_specs, scratch, flops, name, limit, aliases=None):
    n_bytes = sum(math.prod(shape) * jnp.dtype(kind).itemsize for shape, kind in outs)
    return pl.pallas_call(
        kernel,
        out_shape=[jax.ShapeDtypeStruct(shape, kind) for shape, kind in outs],
        in_specs=in_specs,
        out_specs=out_specs,
        scratch_shapes=scratch,
        input_output_aliases=aliases or {},
        compiler_params=pltpu.CompilerParams(vmem_limit_bytes=limit * MIB),
        cost_estimate=pl.CostEstimate(
            flops=int(flops), bytes_accessed=int(2 * n_bytes), transcendentals=0
        ),
        name=name,
    )


def rope_tables(seq_len):
    lane = jnp.arange(LANES, dtype=jnp.int32)
    which = (lane % (HD // 2)).astype(F32)
    frequency = jnp.exp(which * (-2.0 * math.log(10000.0) / HD))
    angles = jnp.arange(seq_len, dtype=F32)[:, None] * frequency[None, :]
    sign = jnp.where(lane % HD < HD // 2, -1.0, 1.0)
    return jnp.cos(angles), jnp.sin(angles) * sign[None, :]


def run_prepare(core, own, other):
    outs = [
        ((1, D), F32),
        ((1, D), F32),
        ((D, PAD_D), BF),
        ((D, KV_COLS), BF),
        ((PAD_D, D), BF),
        ((D, FF), BF),
        ((D, FF), BF),
        ((FF, D), BF),
    ]
    scratch = [
        pltpu.VMEM((2, HALF_ROWS, LANES), BF),
        pltpu.VMEM((FLAT_SCRATCH, LANES), F32),
        pltpu.VMEM((Q_TILES * D, LANES), F32),
        pltpu.SemaphoreType.DMA((2,)),
    ]
    return call(
        prepare_weights,
        outs,
        [smem()] + [hbm()] * 2,
        [vmem()] * 8,
        scratch,
        1e10,
        "prepare_weights",
        60,
    )(core, own, other)


def run_attention_forward(x, gain, wq, wkv, wo, cosine, sine):
    seq_len = x.shape[0]
    outs = [
        ((seq_len, D), F32),
        ((seq_len, PAD_D), BF),
        ((Q_TILES, seq_len, LANES), BF),
        ((6, seq_len, LANES), BF),
        ((6, seq_len, LANES), BF),
        ((16, seq_len), F32),
    ]
    return call(
        attention_forward,
        outs,
        [vmem()] * 7,
        [vmem()] * 6,
        [pltpu.VMEM((Q_TILES, BLOCK, LANES), F32)],
        1.5e10,
        "attention_forward",
        60,
    )(x, gain, wq, wkv, wo, cosine, sine)


def run_mlp(core, slot, lengths, assignment, hidden1, cot, mixed, gain, wo, wg, wu, wd):
    seq_len = hidden1.shape[0]
    outs = [
        ((seq_len, D), BF),
        ((seq_len, D), F32),
        ((Q_TILES, seq_len, LANES), BF),
        ((1, D), F32),
        ((EARLY_ROWS, LANES), BF),
        ((EARLY_ROWS, LANES), BF),
    ]
    return call(
        mlp_pass,
        outs,
        [smem()] * 4 + [hbm()] * 3 + [vmem()] + [hbm()] * 4,
        [hbm()] * 3 + [vmem()] + [hbm()] * 2,
        [
            pltpu.VMEM((seq_len, D), F32),
            pltpu.VMEM((seq_len, D), BF),
            pltpu.VMEM((seq_len, PAD_D), BF),
            pltpu.VMEM((PAD_D, D), BF),
            pltpu.VMEM((D, FF), BF),
            pltpu.VMEM((D, FF), BF),
            pltpu.VMEM((FF, D), BF),
            pltpu.VMEM((seq_len, D), BF),
            pltpu.VMEM((seq_len, D), F32),
            pltpu.VMEM((Q_TILES, seq_len, LANES), BF),
            pltpu.VMEM((PAD_D, seq_len), BF),
            pltpu.VMEM((PAD_D, seq_len), BF),
            pltpu.VMEM((seq_len, FF), BF),
            pltpu.VMEM((seq_len, FF), BF),
            pltpu.VMEM((seq_len, FF), BF),
            pltpu.VMEM((seq_len, D), BF),
            pltpu.VMEM((2, EARLY_ROWS, LANES), BF),
            pltpu.SemaphoreType.DMA((7,)),
            pltpu.SemaphoreType.DMA((seq_len // MLP_BLOCK, 3)),
            pltpu.SemaphoreType.DMA((FF_TILES // 2 + 1, 2)),
        ],
        2.5e10,
        "mlp_pass",
        60,
    )(core, slot, lengths, assignment, hidden1, cot, mixed, gain, wo, wg, wu, wd)


def run_backward_groups(first, count, q, dm, k, v, lse):
    seq_len = q.shape[1]
    fixed = pl.BlockSpec((Q_TILES, seq_len, LANES), lambda i: (0, 0, 0))
    sides = pl.BlockSpec((2, seq_len, LANES), lambda i: (first + i, 0, 0))
    single = pl.BlockSpec((1, seq_len, LANES), lambda i: (i, 0, 0))
    outs = [(count, 2, seq_len, LANES), (count, seq_len, LANES), (count, seq_len, LANES)]
    return pl.pallas_call(
        functools.partial(backward_groups, first),
        grid=(count,),
        out_shape=[jax.ShapeDtypeStruct(shape, F32) for shape in outs],
        in_specs=[
            fixed,
            fixed,
            sides,
            sides,
            pl.BlockSpec((16, seq_len), lambda i: (0, 0)),
        ],
        out_specs=[
            pl.BlockSpec((1, 2, seq_len, LANES), lambda i: (i, 0, 0, 0)),
            single,
            single,
        ],
        scratch_shapes=[pltpu.VMEM((2, seq_len, LANES), F32)] * 2,
        compiler_params=pltpu.CompilerParams(vmem_limit_bytes=60 * MIB),
        cost_estimate=pl.CostEstimate(
            flops=int(8e9) * count, bytes_accessed=int(3e6) * count, transcendentals=0
        ),
        name="backward_groups",
    )(q, dm, k, v, lse)


def run_backward_finish(x, gain, dh1, groups, wq, wkv, cosine, sine):
    seq_len = x.shape[0]
    outs = [
        ((seq_len, D), BF),
        ((seq_len, PAD_D), BF),
        ((seq_len, KV_COLS), BF),
        ((seq_len, D), BF),
        ((1, D), F32),
    ]
    return call(
        backward_finish,
        outs,
        [vmem()] * 13,
        [vmem()] * 5,
        [],
        4e9,
        "backward_finish",
        60,
    )(x, gain, dh1, *groups[0], *groups[1], wq, wkv, cosine, sine)


def run_late_weights(core, normed, d_query, d_kv, gga, ggm):
    outs = [((LATE_HALF, LANES), BF), ((LATE_HALF, LANES), BF)]
    return call(
        late_weights,
        outs,
        [smem()] + [vmem()] * 5,
        [hbm()] * 2,
        [pltpu.VMEM((2 * LATE_HALF, LANES), BF), pltpu.SemaphoreType.DMA((2,))],
        4e9,
        "late_weights",
        60,
    )(core, normed, d_query, d_kv, gga, ggm)


def run_sum(bits, kept, got, split, merge=False, n_parts=None):
    joined = n_parts is not None
    n_parts = n_parts or len(kept)
    rows = kept[0].shape[0] // (n_parts if joined else 1)
    kinds = 2 if split else 1
    n_out = 1 if merge else n_parts
    out_rows = rows // kinds * (n_parts if merge else 1)
    results = call(
        functools.partial(
            gather_sum, n_parts=n_parts, rows=rows, split=split, merge=merge, joined=joined
        ),
        [((out_rows, LANES), BF)] * (kinds * n_out),
        [smem()] + [vmem()] * (2 * len(kept)),
        [hbm()] * (kinds * n_out),
        [pltpu.VMEM((n_parts, rows, LANES), BF), pltpu.SemaphoreType.DMA((2 * n_parts,))],
        1e6,
        "gather_sum",
        12,
    )(bits, *kept, *got)
    return list(results[:n_out]), list(results[n_out:])


def run_join(bits, own, got, n_parts):
    merged = len(own) < n_parts
    rows = own[0].shape[0] // (n_parts if merged else 1)
    return call(
        functools.partial(join_halves, n_parts=n_parts, rows=rows, merged=merged),
        [((2 * rows, LANES), BF)] * n_parts,
        [smem()] + [hbm()] * (2 * len(own)),
        [hbm()] * n_parts,
        [pltpu.SemaphoreType.DMA((2 * n_parts,))],
        1e6,
        "join_halves",
        4,
    )(bits, *own, *got)


def chunk_scratch(count):
    return [
        pltpu.VMEM((3 * count * CHUNK * LANES,), F32),
        pltpu.VMEM((4 * count * CHUNK * LANES,), F32),
        pltpu.SemaphoreType.DMA((12, 3)),
        pltpu.SemaphoreType.DMA((12, 4)),
    ]


def extra_scratch(count, n_rows):
    bufs = [pltpu.VMEM((count,), F32)] * 7 + [pltpu.VMEM((n_rows * LANES,), F32)]
    return bufs + [pltpu.SemaphoreType.DMA((7,))]


def run_update_first(scale, rate, core, bits, halves, state):
    scratch = [
        pltpu.VMEM((2 * PART_ROWS, LANES), BF),
        pltpu.VMEM((FLAT_BASE + CHUNK, LANES), F32),
        *chunk_scratch(12),
        pltpu.SemaphoreType.DMA((4,)),
        *extra_scratch(TAIL_ZERO, CHUNK),
    ]
    return call(
        functools.partial(update_first, scale, rate),
        [(state[0].shape, F32)] * 4,
        [smem()] * 2 + [hbm()] * 7,
        [hbm()] * 4,
        scratch,
        1e9,
        "update_first",
        60,
    )(core, bits, *halves, *state)


def run_update_second(scale, rate, core, bits, halves, state, done):
    scratch = [
        pltpu.VMEM((FLAT_BASE + CHUNK + 8, LANES), F32),
        pltpu.VMEM((Q_TILES * D, LANES), F32),
        pltpu.VMEM((2 * REST_SLOT + PART_ROWS, LANES), BF),
        pltpu.VMEM((PART_ROWS, LANES), BF),
        pltpu.VMEM((32, LANES), BF),
        *chunk_scratch(11),
        pltpu.SemaphoreType.DMA((8,)),
        *extra_scratch(TAIL_ONE, CHUNK + 8),
        *extra_scratch(5 * LANES, 8),
    ]
    return call(
        functools.partial(update_second, scale, rate),
        [(state[0].shape, F32)] * 4,
        [smem()] * 2 + [hbm()] * 15,
        [hbm()] * 4,
        scratch,
        1e9,
        "update_second",
        60,
        {13 + i: i for i in range(4)},
    )(core, bits, *halves, *state, *done)


def run_update_late(scale, rate, core, own, other, state, done):
    last_rows = O_ROW - LATE_CHUNKS * CHUNK
    scratch = [
        pltpu.VMEM((4336, LANES), F32),
        pltpu.VMEM((Q_TILES * D, LANES), F32),
        pltpu.VMEM((2 * LATE_HALF, LANES), BF),
        *chunk_scratch(LATE_CHUNKS),
        *extra_scratch(last_rows * LANES, 304),
    ]
    return call(
        functools.partial(update_late, scale, rate),
        [(state[0].shape, F32)] * 4,
        [smem()] + [vmem()] * 2 + [hbm()] * 7,
        [hbm()] * 4,
        scratch,
        1e9,
        "update_late",
        60,
        {6 + i: i for i in range(4)},
    )(core, own, other, *state, *done)


def add_low(a, b):
    return (a.astype(F32) + b.astype(F32)).astype(BF)


def xor_swap(value, bit):
    size = lax.axis_size("dp")
    return lax.ppermute(value, "dp", [(i, i ^ (1 << bit)) for i in range(size)])


def tie(value, *others):
    return lax.optimization_barrier((value, *others))


def my_bits(orders, step):
    index = lax.axis_index("dp")
    return jnp.stack([(index >> order[step]) & 1 for order in orders]).astype(jnp.int32)


def spread(blocks, far):
    size = lax.axis_size("dp")
    near = min(size, 4)
    if far:
        groups = [[g * near + i for g in range(size // near)] for i in range(near)]
    else:
        groups = [[g * near + i for i in range(near)] for g in range(size // near)]
    return lax.all_to_all(
        blocks, "dp", split_axis=0, concat_axis=0, tiled=True, axis_index_groups=groups
    )


def group_size(far):
    size = lax.axis_size("dp")
    return size // min(size, 4) if far else min(size, 4)


def scatter_sum(value):
    count = group_size(False)
    blocks = spread(value.reshape(count, value.shape[0] // count, LANES), False)
    return jnp.sum(blocks.astype(F32), axis=0).astype(BF)


def copies(value, far):
    return spread(jnp.broadcast_to(value[None], (group_size(far), *value.shape)), far)


def bit_orders():
    n_bits = lax.axis_size("dp").bit_length() - 1
    base = list(range(n_bits))
    head = base[:3] if n_bits >= 3 else base
    return [head[r:] + head[:r] + base[len(head) :] for r in range(3)]


def on_device(inputs, cotangent, lengths, assignment, return_order, master, momentum, average):
    nseq_all, block_rows, _ = inputs.shape
    axes = ("dp", "shard")
    seq_len = block_rows * lax.axis_size("dp") * lax.axis_size("shard")
    my_slot = lax.axis_index(axes)
    core = lax.axis_index("shard")
    core_arr = core.astype(jnp.int32).reshape(1)

    seq_ids = jnp.arange(nseq_all, dtype=jnp.int32)
    inverse = jnp.sum(
        jnp.where(return_order[None, :] == seq_ids[:, None], seq_ids[None, :], 0), axis=1
    )

    def pick(array, index):
        return array.at[index].get(mode="promise_in_bounds")

    def exchange(value):
        return lax.all_to_all(value, axes, split_axis=0, concat_axis=0, tiled=True)

    sent_in, master_in = tie(pick(inputs, assignment), master)
    x = exchange(sent_in).reshape(seq_len, D)
    slot_arr = my_slot.astype(jnp.int32).reshape(1)

    own = jnp.pad(master_in.astype(BF), (0, HALF_ROWS * LANES - master.shape[0]))
    own = own.reshape(HALF_ROWS, LANES)
    other = lax.ppermute(own, "shard", [(0, 1), (1, 0)])
    gain_attn, gain_mlp, wq, wkv, wo, wg, wu, wd = run_prepare(core_arr, own, other)

    cosine, sine = rope_tables(seq_len)
    sent_cot, gain_attn, cosine = tie(pick(cotangent, inverse), gain_attn, cosine)
    cot = exchange(sent_cot).reshape(seq_len, D)
    hidden1, mixed, q, k, v, lse = run_attention_forward(x, gain_attn, wq, wkv, wo, cosine, sine)
    result, dh1, dm, ggm, early_keep, early_send = run_mlp(
        core_arr, slot_arr, lengths, assignment, hidden1, cot, mixed, gain_mlp, wo, wg, wu, wd
    )
    back_out = exchange(result.reshape(nseq_all, block_rows, D))

    orders = bit_orders()
    n_bits = len(orders[0])

    def swap_parts(parts, step):
        return [xor_swap(part, order[step]) for part, order in zip(parts, orders)]

    got = lax.ppermute(early_send, "shard", [(0, 1), (1, 0)])
    groups = [run_backward_groups(0, 1, q, dm, k, v, lse)]
    lse, got = tie(lse, got)
    sent, kept = run_sum(my_bits(orders, 0), [early_keep], [got], True, n_parts=3)
    lse, *kept = tie(lse, *kept)
    got = swap_parts(sent, 0)
    groups.append(run_backward_groups(1, KV - 1, q, dm, k, v, lse))
    sent, kept = run_sum(my_bits(orders, 1), kept, got, True)
    dh1, back_out, *kept = tie(dh1, back_out, *kept)
    got = swap_parts(sent, 1)
    d_stream, d_query, d_kv, normed, gga = run_backward_finish(
        x, gain_attn, dh1, groups, wq, wkv, cosine, sine
    )
    last_bit = n_bits - 1
    for step in range(2, n_bits):
        if step > 2:
            got = swap_parts(sent, step - 1)
        sent, kept = run_sum(my_bits(orders, step), kept, got, True, merge=step == last_bit)
        if step == 2:
            gga, *kept = tie(gga, *kept)
            late_keep, late_send = run_late_weights(core_arr, normed, d_query, d_kv, gga, ggm)
            late_send, *kept = tie(late_send, *kept)
        if step == last_bit:
            late_send, sent[0] = tie(late_send, sent[0])
    got = [xor_swap(sent[0], last_bit)]
    late_got = lax.ppermute(late_send, "shard", [(0, 1), (1, 0)])
    early, _ = run_sum(my_bits(orders, last_bit)[:1], kept, got, False)
    late, _ = run_sum(my_bits(orders, 0)[:1], [late_keep], [late_got], False)
    late, block_output, early[0] = tie(late[0], pick(back_out, return_order), early[0])
    late = scatter_sum(late)
    early = run_join(my_bits(orders, last_bit), early, [xor_swap(early[0], last_bit)], 3)
    late, *early = tie(late, *early)
    late = jnp.sum(copies(late, True).astype(F32), axis=0).astype(BF)
    for step in reversed(range(1, last_bit)):
        early = run_join(my_bits(orders, step), early, swap_parts(early, step), 3)
        if step == last_bit - 1:
            late, *early = tie(late, *early)
            late = copies(late, False).reshape(-1, LANES)
    got = swap_parts(early, 0)
    swap_own = lax.ppermute(early[2], "shard", [(0, 1)])
    bits = my_bits(orders, 0)
    scale = 1.0 / nseq_all
    rate = (nseq_all / (0.6 * seq_len)) ** 0.5 / D**0.5
    state = (master, momentum, average)
    d_stream, late, swap_own, *got = tie(d_stream, late, swap_own, *got)
    back_grad = exchange(d_stream.reshape(nseq_all, block_rows, D))
    late_other = lax.ppermute(late, "shard", [(1, 0)])
    swap_got = lax.ppermute(got[2], "shard", [(0, 1)])
    halves = [early[0], got[0], early[1], got[1], early[2], got[2], swap_own, swap_got]
    done = run_update_first(scale, rate, core_arr, bits, halves[:4], state)
    done = run_update_second(scale, rate, core_arr, bits, halves, state, done)
    weight_grad, new_momentum, new_master, new_average = run_update_late(
        scale, rate, core_arr, late, late_other, state, done
    )
    input_grad = pick(back_grad, return_order)
    return (block_output, input_grad, weight_grad, new_momentum, new_master, new_average)


def solution(mesh):
    rows = P(None, ("dp", "shard"), None)
    flat = P("shard")
    return jax.shard_map(
        on_device,
        mesh=mesh,
        in_specs=(rows, rows, P(), P(), P(), flat, flat, flat),
        out_specs=(rows, rows, flat, flat, flat, flat),
        check_vma=False,
    )
```

profile of v0, /device:TPU:1, one launch (start us, length us, event | category | flops | bytes accessed | tf_op | source)
XLA Modules:
  0.0 280.7 jit_solution(8547133014027470416)
XLA Ops:
  3.5 3.3 %convert_element_type.20 = bf16[1770048]{0:T(1024)(128)(2,1)S(1)} convert(f32[1770048]{0:T(1024)} %rest_0_.1) | non-fusion elementwise | flops 1770048 | bytes 10620288 | tf_op jit(solution)/shard_map/convert_element_type | solution.py:1332
  8.3 7.2 %all-to-all-start = ((bf16[32,24,576]{2,1,0:T(8,128)(2,1)}), bf16[32,24,576]{2,1,0:T(8,128)(2,1)}, u32[]{:S(2)}, u32[]{:S(2)}) async-start(bf16[32,24,576]{2,1,0:T(8,128)(2,1)} %gather_fusion), calls=%async_computation | async-start | bytes 1966080 | tf_op jit(solution)/shard_map/all_to_all | solution.py:1326
  20.8 10.3 %prepare_weights.1 = (f32[1,576]{1,0:T(1,128)}, f32[1,576]{1,0:T(1,128)}, bf16[576,640]{1,0:T(8,128)(2,1)}, bf16[576,384]{1,0:T(8,128)(2,1)}, bf16[640,576]{1,0:...) custom-call(s32[1]{0:T(128)} %bitcast.1.core_ref, ...), custom_call_target="tpu_custom_call" | custom-call | flops 10000000000 | bytes 14459904 | tf_op jit(solution)/shard_map/prepare_weights/pallas_call | solution.py:996
  31.2 8.4 %all-to-all-done = bf16[32,24,576]{2,1,0:T(8,128)(2,1)} async-done(((bf16[32,24,576]{2,1,0:T(8,128)(2,1)}), bf16[32,24,576]{2,1,0:T(8,128)(2,1)}, u32[]{:S(2)}, u32[]{:S(2)}) %all-to-all-start) | async-done | bytes 884768 | tf_op jit(solution)/shard_map/all_to_all | solution.py:1326
  39.5 5.1 %all-to-all-start.1 = ((bf16[32,24,576]{2,1,0:T(8,128)(2,1)}), bf16[32,24,576]{2,1,0:T(8,128)(2,1)S(1)}, u32[]{:S(2)}, u32[]{:S(2)}) async-start(bf16[32,24,576]{2,1,0:T(8,128)(2,1)} %gather_fusion.1), calls=%async_computation.1 | async-start | bytes 1966080 | tf_op jit(solution)/shard_map/all_to_all | solution.py:1326
  44.6 21.3 %attention_forward.1 = (f32[768,576]{1,0:T(8,128)}, bf16[768,640]{1,0:T(8,128)(2,1)}, bf16[5,768,128]{2,1,0:T(8,128)(2,1)}, bf16[6,768,128]{2,1,0:T(8,128)(2,1)}...) custom-call(bf16[768,576]{1,0:T(8,128)(2,1)} %bitcast.2.x_ref, f32[1,576]{1,0:T(1,128)} %get-tuple-element.126.ga_ref, ...), custom_call_target="tpu_custom_call" | custom-call | flops 15000000512 | bytes 12288000 | tf_op jit(solution)/shard_map/attention_forward/pallas_call | solution.py:1018
  69.4 28.3 %mlp_pass.1 = (bf16[768,576]{1,0:T(8,128)(2,1)}, f32[768,576]{1,0:T(8,128)}, bf16[5,768,128]{2,1,0:T(8,128)(2,1)}, f32[1,576]{1,0:T(1,128)}, bf16[12288,128]{1,0:T(8,128)(2,1)}, /*index=5*/bf16[12288,128]{1,0:T(8,128)(2,1)}) custom-call(s32[1]{0:T(128)} %bitcast.1.core_ref, s32[1]{0:T(128)} %bitcast.6.slot_ref, s32[32]{0:T(128)} %lengths_ref.1, ...), custom_call_target="tpu_custom_call" | custom-call | flops 24999999488 | bytes 19862016 | tf_op jit(solution)/shard_map/mlp_pass/pallas_call | solution.py:1040
  99.2 3.9 %all-to-all-start.2 = ((bf16[32,24,576]{2,1,0:T(8,128)(2,1)}), bf16[32,24,576]{2,1,0:T(8,128)(2,1)}, u32[]{:S(2)}, u32[]{:S(2)}) async-start(bf16[32,24,576]{2,1,0:T(8,128)(2,1)} %bitcast.21), calls=%async_computation.2 | async-start | bytes 1966080 | tf_op jit(solution)/shard_map/all_to_all | solution.py:1326
  103.1 7.6 %backward_groups.2 = (f32[1,2,768,128]{3,2,1,0:T(8,128)}, f32[1,768,128]{2,1,0:T(8,128)}, f32[1,768,128]{2,1,0:T(8,128)}) custom-call(bf16[5,768,128]{2,1,0:T(8,128)(2,1)} %get-tuple-element.158.q_ref, bf16[5,768,128]{2,1,0:T(8,128)(2,1)} %get-tuple-element.159.dm_ref, bf16[6,768,128]{2,1,0:T(8,128)(2,1)} %get-tuple-element.160.k_ref, ...), custom_call_target="tpu_custom_call" | custom-call | flops 8000000000 | bytes 3000000 | tf_op jit(solution)/shard_map/backward_groups/pallas_call | solution.py:1079
  110.7 3.6 %gather_sum.6 = (bf16[2048,128]{1,0:T(8,128)(2,1)}, bf16[2048,128]{1,0:T(8,128)(2,1)}, bf16[2048,128]{1,0:T(8,128)(2,1)}, bf16[2048,128]{1,0:T(8,128)(2,1)S(1)},...) custom-call(s32[3]{0:T(128)S(1)} %pad_add_fusion.1.bits_ref, bf16[12288,128]{1,0:T(8,128)(2,1)S(1)} %copy-done.2, ...), custom_call_target="tpu_custom_call" | custom-call | flops 1000000 | bytes 6291456 | tf_op jit(solution)/shard_map/gather_sum/pallas_call | solution.py:1146
  119.7 12.7 %backward_groups.3 = (f32[2,2,768,128]{3,2,1,0:T(8,128)}, f32[2,768,128]{2,1,0:T(8,128)}, f32[2,768,128]{2,1,0:T(8,128)}) custom-call(bf16[5,768,128]{2,1,0:T(8,128)(2,1)} %get-tuple-element.158.q_ref, bf16[5,768,128]{2,1,0:T(8,128)(2,1)} %get-tuple-element.159.dm_ref, bf16[6,768,128]{2,1,0:T(8,128)(2,1)} %get-tuple-element.160.k_ref, ...), custom_call_target="tpu_custom_call" | custom-call | flops 16000000000 | bytes 6000000 | tf_op jit(solution)/shard_map/backward_groups/pallas_call | solution.py:1079
  138.2 8.9 %backward_finish.1 = (bf16[768,576]{1,0:T(8,128)(2,1)}, bf16[768,640]{1,0:T(8,128)(2,1)}, bf16[768,384]{1,0:T(8,128)(2,1)}, bf16[768,576]{1,0:T(8,128)(2,1)}, f32[1,576]{1,0:T(1,128)}) custom-call(bf16[768,576]{1,0:T(8,128)(2,1)} %bitcast.2.x_ref, f32[1,576]{1,0:T(1,128)} %get-tuple-element.126.ga_ref, f32[768,576]{1,0:T(8,128)} %get-tuple-element.157.dh1_ref, ...), custom_call_target="tpu_custom_call" | custom-call | flops 4000000000 | bytes 6689280 | tf_op jit(solution)/shard_map/backward_finish/pallas_call | solution.py:1113
  151.6 4.1 %late_weights.1 = (bf16[2432,128]{1,0:T(8,128)(2,1)}, bf16[2432,128]{1,0:T(8,128)(2,1)}) custom-call(s32[1]{0:T(128)} %bitcast.1.core_ref, bf16[768,576]{1,0:T(8,128)(2,1)} %get-tuple-element.169.nm_s, bf16[768,640]{1,0:T(8,128)(2,1)} %get-tuple-element.170.dq_s, bf16[768,384]{1,0:T(8,128)(2,1)} %get-tuple-element.171.dkv_s, ...), custom_call_target="tpu_custom_call" | custom-call | flops 4000000000 | bytes 2490368 | tf_op jit(solution)/shard_map/late_weights/pallas_call | solution.py:1127
  156.9 3.2 %collective-permute-start.11 = (bf16[2432,128]{1,0:T(8,128)(2,1)}, bf16[2432,128]{1,0:T(8,128)(2,1)S(1)}, u32[]{:S(2)}, u32[]{:S(2)}) collective-permute-start(bf16[2432,128]{1,0:T(8,128)(2,1)} %get-tuple-element.197), channel_id=1, source_target_pairs={{0,1},{1,0},{2,3},{3,2},{4,5},{5,4},{6,7},{7,6},{8,9},{9,8},{10,11... | collective-permute-start | bytes 1867784 | tf_op jit(solution)/shard_map/ppermute | solution.py:1377
  164.0 7.9 %collective-permute-done.12.refs_1_ = bf16[768,128]{1,0:T(8,128)(2,1)S(1)} collective-permute-done((bf16[768,128]{1,0:T(8,128)(2,1)S(1)}, bf16[768,128]{1,0:T(8,128)(2,1)S(1)}, u32[]{:S(2)}, u32[]{:S(2)}) %collective-permute-start.12) | collective-permute-done | bytes 196640 | tf_op jit(solution)/shard_map/ppermute | solution.py:1263
  173.3 3.5 %all-to-all-start.3 = ((bf16[4,608,128]{2,1,0:T(8,128)(2,1)}), bf16[4,608,128]{2,1,0:T(8,128)(2,1)S(1)}, u32[]{:S(2)}, u32[]{:S(2)}) async-start(bf16[4,608,128]{2,1,0:T(8,128)(2,1)} %bitcast.12), calls=%async_computation.3 | async-start | bytes 1245184 | tf_op jit(solution)/shard_map/all_to_all | solution.py:1282
  176.9 11.7 %collective-permute-done.13.refs_1_ = bf16[768,128]{1,0:T(8,128)(2,1)S(1)} collective-permute-done((bf16[768,128]{1,0:T(8,128)(2,1)S(1)}, bf16[768,128]{1,0:T(8,128)(2,1)S(1)}, u32[]{:S(2)}, u32[]{:S(2)}) %collective-permute-start.13) | collective-permute-done | bytes 196640 | tf_op jit(solution)/shard_map/ppermute | solution.py:1263
  190.7 3.5 %all-to-all-start.4 = ((bf16[4,608,128]{2,1,0:T(8,128)(2,1)}), bf16[4,608,128]{2,1,0:T(8,128)(2,1)S(1)}, u32[]{:S(2)}, u32[]{:S(2)}) async-start(bf16[4,608,128]{2,1,0:T(8,128)(2,1)} %broadcast_in_dim.52), calls=%async_computation.4 | async-start | bytes 1245184 | tf_op jit(solution)/shard_map/all_to_all | solution.py:1282
  198.2 9.0 %collective-permute-done.14.refs_3_ = bf16[512,128]{1,0:T(8,128)(2,1)S(1)} collective-permute-done((bf16[512,128]{1,0:T(8,128)(2,1)S(1)}, bf16[512,128]{1,0:T(8,128)(2,1)S(1)}, u32[]{:S(2)}, u32[]{:S(2)}) %collective-permute-start.14) | collective-permute-done | bytes 131104 | tf_op jit(solution)/shard_map/ppermute | solution.py:1263
  213.7 3.3 %collective-permute-done.17.refs_3_ = bf16[1024,128]{1,0:T(8,128)(2,1)S(1)} collective-permute-done((bf16[1024,128]{1,0:T(8,128)(2,1)S(1)}, bf16[1024,128]{1,0:T(8,128)(2,1)S(1)}, u32[]{:S(2)}, u32[]{:S(2)}) %collective-permute-start.17) | collective-permute-done | bytes 262176 | tf_op jit(solution)/shard_map/ppermute | solution.py:1263
  223.0 15.4 %all_to_all.35 = bf16[4,608,128]{2,1,0:T(8,128)(2,1)S(1)} all-to-all(bf16[4,608,128]{2,1,0:T(8,128)(2,1)S(1)} %broadcast_in_dim.53), channel_id=1, replica_groups={{0,2,4,6},{8,10,12,14},{16,18,20,22},{24,26,28,30},{1,3,5,7},{9,11,13,1..., dimensions={0} | all-to-all | bytes 1245184 | tf_op jit(solution)/shard_map/all_to_all | solution.py:1282
  240.1 8.3 %all-to-all-start.6 = ((bf16[32,24,576]{2,1,0:T(8,128)(2,1)}), bf16[32,24,576]{2,1,0:T(8,128)(2,1)S(1)}, u32[]{:S(2)}, u32[]{:S(2)}) async-start(bf16[32,24,576]{2,1,0:T(8,128)(2,1)} %bitcast.20), calls=%async_computation.6 | async-start | bytes 1966080 | tf_op jit(solution)/shard_map/all_to_all | solution.py:1326
  252.8 11.2 %update_first.1 = (f32[1770048]{0:T(1024)}, f32[1770048]{0:T(1024)}, f32[1770048]{0:T(1024)}, f32[1770048]{0:T(1024)}) custom-call(s32[1]{0:T(128)} %bitcast.1.core_ref, s32[3]{0:T(128)} %copy-done.11, bf16[2048,128]{1,0:T(8,128)(2,1)} %copy-done.3, bf16[2048,128]{1,0:T(8,128)(2,1)} %copy-done.14, bf16[2048,128]{1,0:T(8,128)(2,1)} %copy-done.4, ...), custom_call_target="tpu_custom_call" | custom-call | flops 1000000000 | bytes 56641536 | tf_op jit(solution)/shard_map/update_first/pallas_call | solution.py:1198
  264.8 11.9 %update_second.1 = (f32[1770048]{0:T(1024)}, f32[1770048]{0:T(1024)}, f32[1770048]{0:T(1024)}, f32[1770048]{0:T(1024)}) custom-call(s32[1]{0:T(128)} %bitcast.1.core_ref, s32[3]{0:T(128)} %copy-done.11, bf16[2048,128]{1,0:T(8,128)(2,1)} %copy-done.3, ...), custom_call_target="tpu_custom_call", output_to_operand_aliasing={{0}: (13, {}), {1}: (14, {}), {2}: (15, {}), {3}: (16, {})} | custom-call | flops 1000000000 | bytes 56641536 | tf_op jit(solution)/shard_map/update_second/pallas_call | solution.py:1222
  (125 shorter events, 65.8 us)
Async XLA Ops:
  8.2 12.6 %collective-permute-start = (bf16[13832,128]{1,0:T(8,128)(2,1)S(1)}, bf16[13832,128]{1,0:T(8,128)(2,1)}, u32[]{:S(2)}, u32[]{:S(2)}) collective-permute-start(bf16[13832,128]{1,0:T(8,128)(2,1)S(1)} %pad_bitcast_fusion.own_ref), channel_id=1, source_target_pairs={{0,1},{1,0},{2,3},{3,2},{4,5},{5,4},{6,7},{7,6},{8,9},{9,8},{10,11... | collective-permute-start | bytes 10622984 | tf_op jit(solution)/shard_map/ppermute | solution.py:1334
  8.3 31.2 %all-to-all-start = ((bf16[32,24,576]{2,1,0:T(8,128)(2,1)}), bf16[32,24,576]{2,1,0:T(8,128)(2,1)}, u32[]{:S(2)}, u32[]{:S(2)}) async-start(bf16[32,24,576]{2,1,0:T(8,128)(2,1)} %gather_fusion), calls=%async_computation | async-start | bytes 1966080 | tf_op jit(solution)/shard_map/all_to_all | solution.py:1326
  39.5 28.9 %all-to-all-start.1 = ((bf16[32,24,576]{2,1,0:T(8,128)(2,1)}), bf16[32,24,576]{2,1,0:T(8,128)(2,1)S(1)}, u32[]{:S(2)}, u32[]{:S(2)}) async-start(bf16[32,24,576]{2,1,0:T(8,128)(2,1)} %gather_fusion.1), calls=%async_computation.1 | async-start | bytes 1966080 | tf_op jit(solution)/shard_map/all_to_all | solution.py:1326
  97.7 13.0 %collective-permute-start.1 = (bf16[12288,128]{1,0:T(8,128)(2,1)}, bf16[12288,128]{1,0:T(8,128)(2,1)}, u32[]{:S(2)}, u32[]{:S(2)}) collective-permute-start(bf16[12288,128]{1,0:T(8,128)(2,1)} %get-tuple-element.141), channel_id=1, source_target_pairs={{0,1},{1,0},{2,3},{3,2},{4,5},{5,4},{6,7},{7,6},{8,9},{9,8},{10,11... | collective-permute-start | bytes 9437192 | tf_op jit(solution)/shard_map/ppermute | solution.py:1352
  99.2 39.0 %all-to-all-start.2 = ((bf16[32,24,576]{2,1,0:T(8,128)(2,1)}), bf16[32,24,576]{2,1,0:T(8,128)(2,1)}, u32[]{:S(2)}, u32[]{:S(2)}) async-start(bf16[32,24,576]{2,1,0:T(8,128)(2,1)} %bitcast.21), calls=%async_computation.2 | async-start | bytes 1966080 | tf_op jit(solution)/shard_map/all_to_all | solution.py:1326
  115.9 16.5 %collective-permute-start.2 = (bf16[2048,128]{1,0:T(8,128)(2,1)}, bf16[2048,128]{1,0:T(8,128)(2,1)S(1)}, u32[]{:S(2)}, u32[]{:S(2)}) collective-permute-start(bf16[2048,128]{1,0:T(8,128)(2,1)} %get-tuple-element.151), channel_id=1, source_target_pairs={{0,2},{2,0},{4,6},{6,4},{8,10},{10,8},{12,14},{14,12},{16,18},{18,... | collective-permute-start | bytes 1572872 | tf_op jit(solution)/shard_map/ppermute | solution.py:1263
  117.3 15.3 %collective-permute-start.3 = (bf16[2048,128]{1,0:T(8,128)(2,1)}, bf16[2048,128]{1,0:T(8,128)(2,1)S(1)}, u32[]{:S(2)}, u32[]{:S(2)}) collective-permute-start(bf16[2048,128]{1,0:T(8,128)(2,1)} %get-tuple-element.152), channel_id=1, source_target_pairs={{0,4},{2,6},{4,0},{6,2},{8,12},{10,14},{12,8},{14,10},{16,20},{18,... | collective-permute-start | bytes 1572872 | tf_op jit(solution)/shard_map/ppermute | solution.py:1263
  118.5 16.0 %collective-permute-start.4 = (bf16[2048,128]{1,0:T(8,128)(2,1)}, bf16[2048,128]{1,0:T(8,128)(2,1)S(1)}, u32[]{:S(2)}, u32[]{:S(2)}) collective-permute-start(bf16[2048,128]{1,0:T(8,128)(2,1)} %get-tuple-element.153), channel_id=1, source_target_pairs={{0,8},{2,10},{4,12},{6,14},{8,0},{10,2},{12,4},{14,6},{16,24},{18,... | collective-permute-start | bytes 1572872 | tf_op jit(solution)/shard_map/ppermute | solution.py:1263
  136.2 10.9 %collective-permute-start.5 = (bf16[1024,128]{1,0:T(8,128)(2,1)}, bf16[1024,128]{1,0:T(8,128)(2,1)S(1)}, u32[]{:S(2)}, u32[]{:S(2)}) collective-permute-start(bf16[1024,128]{1,0:T(8,128)(2,1)} %get-tuple-element.176), channel_id=1, source_target_pairs={{0,4},{2,6},{4,0},{6,2},{8,12},{10,14},{12,8},{14,10},{16,20},{18,... | collective-permute-start | bytes 786440 | tf_op jit(solution)/shard_map/ppermute | solution.py:1263
  156.9 15.3 %collective-permute-start.11 = (bf16[2432,128]{1,0:T(8,128)(2,1)}, bf16[2432,128]{1,0:T(8,128)(2,1)S(1)}, u32[]{:S(2)}, u32[]{:S(2)}) collective-permute-start(bf16[2432,128]{1,0:T(8,128)(2,1)} %get-tuple-element.197), channel_id=1, source_target_pairs={{0,1},{1,0},{2,3},{3,2},{4,5},{5,4},{6,7},{7,6},{8,9},{9,8},{10,11... | collective-permute-start | bytes 1867784 | tf_op jit(solution)/shard_map/ppermute | solution.py:1377
  160.1 11.8 %collective-permute-start.12 = (bf16[768,128]{1,0:T(8,128)(2,1)S(1)}, bf16[768,128]{1,0:T(8,128)(2,1)S(1)}, u32[]{:S(2)}, u32[]{:S(2)}) collective-permute-start(bf16[768,128]{1,0:T(8,128)(2,1)S(1)} %get-tuple-element.200), channel_id=1, source_target_pairs={{0,16},{2,18},{4,20},{6,22},{8,24},{10,26},{12,28},{14,30},{16,0},... | collective-permute-start | bytes 589832 | tf_op jit(solution)/shard_map/ppermute | solution.py:1263
  173.3 16.4 %all-to-all-start.3 = ((bf16[4,608,128]{2,1,0:T(8,128)(2,1)}), bf16[4,608,128]{2,1,0:T(8,128)(2,1)S(1)}, u32[]{:S(2)}, u32[]{:S(2)}) async-start(bf16[4,608,128]{2,1,0:T(8,128)(2,1)} %bitcast.12), calls=%async_computation.3 | async-start | bytes 1245184 | tf_op jit(solution)/shard_map/all_to_all | solution.py:1282
  176.8 11.8 %collective-permute-start.13 = (bf16[768,128]{1,0:T(8,128)(2,1)S(1)}, bf16[768,128]{1,0:T(8,128)(2,1)S(1)}, u32[]{:S(2)}, u32[]{:S(2)}) collective-permute-start(bf16[768,128]{1,0:T(8,128)(2,1)S(1)} %gather_sum.11.refs_0_), channel_id=1, source_target_pairs={{0,16},{2,18},{4,20},{6,22},{8,24},{10,26},{12,28},{14,30},{16,0},... | collective-permute-start | bytes 589832 | tf_op jit(solution)/shard_map/ppermute | solution.py:1263
  190.7 19.7 %all-to-all-start.4 = ((bf16[4,608,128]{2,1,0:T(8,128)(2,1)}), bf16[4,608,128]{2,1,0:T(8,128)(2,1)S(1)}, u32[]{:S(2)}, u32[]{:S(2)}) async-start(bf16[4,608,128]{2,1,0:T(8,128)(2,1)} %broadcast_in_dim.52), calls=%async_computation.4 | async-start | bytes 1245184 | tf_op jit(solution)/shard_map/all_to_all | solution.py:1282
  194.2 12.9 %collective-permute-start.14 = (bf16[512,128]{1,0:T(8,128)(2,1)S(1)}, bf16[512,128]{1,0:T(8,128)(2,1)S(1)}, u32[]{:S(2)}, u32[]{:S(2)}) collective-permute-start(bf16[512,128]{1,0:T(8,128)(2,1)S(1)} %get-tuple-element.209.refs_0_), channel_id=1, source_target_pairs={{0,8},{2,10},{4,12},{6,14},{8,0},{10,2},{12,4},{14,6},{16,24},{18,... | collective-permute-start | bytes 393224 | tf_op jit(solution)/shard_map/ppermute | solution.py:1263
  195.6 11.5 %collective-permute-start.15 = (bf16[512,128]{1,0:T(8,128)(2,1)S(1)}, bf16[512,128]{1,0:T(8,128)(2,1)S(1)}, u32[]{:S(2)}, u32[]{:S(2)}) collective-permute-start(bf16[512,128]{1,0:T(8,128)(2,1)S(1)} %get-tuple-element.210.refs_1_), channel_id=1, source_target_pairs={{0,2},{2,0},{4,6},{6,4},{8,10},{10,8},{12,14},{14,12},{16,18},{18,... | collective-permute-start | bytes 393224 | tf_op jit(solution)/shard_map/ppermute | solution.py:1263
  197.0 10.2 %collective-permute-start.16 = (bf16[512,128]{1,0:T(8,128)(2,1)S(1)}, bf16[512,128]{1,0:T(8,128)(2,1)S(1)}, u32[]{:S(2)}, u32[]{:S(2)}) collective-permute-start(bf16[512,128]{1,0:T(8,128)(2,1)S(1)} %get-tuple-element.211.refs_2_), channel_id=1, source_target_pairs={{0,4},{2,6},{4,0},{6,2},{8,12},{10,14},{12,8},{14,10},{16,20},{18,... | collective-permute-start | bytes 393224 | tf_op jit(solution)/shard_map/ppermute | solution.py:1263
  219.5 18.9 %collective-permute-start.20 = (bf16[2048,128]{1,0:T(8,128)(2,1)S(1)}, bf16[2048,128]{1,0:T(8,128)(2,1)S(1)}, u32[]{:S(2)}, u32[]{:S(2)}) collective-permute-start(bf16[2048,128]{1,0:T(8,128)(2,1)S(1)} %get-tuple-element.219.rest_4_), channel_id=1, source_target_pairs={{0,1},{2,3},{4,5},{6,7},{8,9},{10,11},{12,13},{14,15},{16,17},{18,... | collective-permute-start | bytes 1572872 | tf_op jit(solution)/shard_map/ppermute | solution.py:1391
  220.8 17.6 %collective-permute-start.21 = (bf16[2048,128]{1,0:T(8,128)(2,1)S(1)}, bf16[2048,128]{1,0:T(8,128)(2,1)S(1)}, u32[]{:S(2)}, u32[]{:S(2)}) collective-permute-start(bf16[2048,128]{1,0:T(8,128)(2,1)S(1)} %get-tuple-element.220.rest_0_), channel_id=1, source_target_pairs={{0,2},{2,0},{4,6},{6,4},{8,10},{10,8},{12,14},{14,12},{16,18},{18,... | collective-permute-start | bytes 1572872 | tf_op jit(solution)/shard_map/ppermute | solution.py:1263
  222.1 16.4 %collective-permute-start.22 = (bf16[2048,128]{1,0:T(8,128)(2,1)S(1)}, bf16[2048,128]{1,0:T(8,128)(2,1)S(1)}, u32[]{:S(2)}, u32[]{:S(2)}) collective-permute-start(bf16[2048,128]{1,0:T(8,128)(2,1)S(1)} %get-tuple-element.221.rest_2_), channel_id=1, source_target_pairs={{0,4},{2,6},{4,0},{6,2},{8,12},{10,14},{12,8},{14,10},{16,20},{18,... | collective-permute-start | bytes 1572872 | tf_op jit(solution)/shard_map/ppermute | solution.py:1263
  222.4 16.1 %collective-permute-start.23 = (bf16[2048,128]{1,0:T(8,128)(2,1)S(1)}, bf16[2048,128]{1,0:T(8,128)(2,1)S(1)}, u32[]{:S(2)}, u32[]{:S(2)}) collective-permute-start(bf16[2048,128]{1,0:T(8,128)(2,1)S(1)} %get-tuple-element.219.rest_4_), channel_id=1, source_target_pairs={{0,8},{2,10},{4,12},{6,14},{8,0},{10,2},{12,4},{14,6},{16,24},{18,... | collective-permute-start | bytes 1572872 | tf_op jit(solution)/shard_map/ppermute | solution.py:1263
  240.1 38.7 %all-to-all-start.6 = ((bf16[32,24,576]{2,1,0:T(8,128)(2,1)}), bf16[32,24,576]{2,1,0:T(8,128)(2,1)S(1)}, u32[]{:S(2)}, u32[]{:S(2)}) async-start(bf16[32,24,576]{2,1,0:T(8,128)(2,1)} %bitcast.20), calls=%async_computation.6 | async-start | bytes 1966080 | tf_op jit(solution)/shard_map/all_to_all | solution.py:1326
  248.4 28.2 %collective-permute-start.24 = (bf16[2432,128]{1,0:T(8,128)(2,1)S(1)}, bf16[2432,128]{1,0:T(8,128)(2,1)}, u32[]{:S(2)}, u32[]{:S(2)}) collective-permute-start(bf16[2432,128]{1,0:T(8,128)(2,1)S(1)} %bitcast.18), channel_id=1, source_target_pairs={{1,0},{3,2},{5,4},{7,6},{9,8},{11,10},{13,12},{15,14},{17,16},{19,... | collective-permute-start | bytes 1867784 | tf_op jit(solution)/shard_map/ppermute | solution.py:1398
  251.4 12.5 %collective-permute-start.25 = (bf16[2048,128]{1,0:T(8,128)(2,1)}, bf16[2048,128]{1,0:T(8,128)(2,1)S(1)}, u32[]{:S(2)}, u32[]{:S(2)}) collective-permute-start(bf16[2048,128]{1,0:T(8,128)(2,1)} %copy-done.18), channel_id=1, source_target_pairs={{0,1},{2,3},{4,5},{6,7},{8,9},{10,11},{12,13},{14,15},{16,17},{18,... | collective-permute-start | bytes 1572872 | tf_op jit(solution)/shard_map/ppermute | solution.py:1399
  (29 other events, 290.9 us)
where the time goes:
time: 286 us; the launch traced here: 281 us
  Pallas kernels  132 us (46%)
  starting transfers between devices  60.4 us (21%)
  waiting for transfers between devices  48.3 us (17%)
  local copies, waits for them, and re-layouts  16.8 us (6%)
  blocking collectives  15.4 us (5%)
  other arithmetic  6.92 us (2%)
    ppermute x20, waiting for transfers between devices, xor_swap(): return lax.ppermute(value, 'dp', [(i, i ^ 1 << bit) for i in range(size)])  35.8 us
    pallas_call x1, Pallas kernels, run_mlp(): call(mlp_pass, outs, [smem()] * 4 + [hbm()] * 3 + [vmem()] + [hbm()] * 4,...  28.3 us
    all_to_all x4, starting transfers between devices, exchange(): return lax.all_to_all(value, axes, split_axis=0, concat_axis=0, tiled=True)  24.5 us
    pallas_call x1, Pallas kernels, run_attention_forward(): call(attention_forward, outs, [vmem()] * 7, [vmem()] * 6, [pltpu.VMEM((Q_...  21.3 us
    pallas_call x2, Pallas kernels, run_backward_groups(): pl.pallas_call(functools.partial(backward_groups, first), grid=(count,),...  20.3 us
    ppermute x20, starting transfers between devices, xor_swap(): return lax.ppermute(value, 'dp', [(i, i ^ 1 << bit) for i in range(size)])  18.7 us
    all_to_all x1, blocking collectives, spread(): lax.all_to_all(blocks, 'dp', split_axis=0, concat_axis=0, tiled=True, axi...  15.4 us
    pallas_call x1, Pallas kernels, run_update_second(): call(functools.partial(update_second, scale, rate), [(state[0].shape, F32...  11.9 us
  transfers between devices with their start and end apart: 32, of which 11 were waited for; matrix products, arithmetic and copies ran while one was open for 3% of the time, Pallas kernels for 35%

commit v1 on v0

--- a/solution.py
+++ b/solution.py
@@ -31,11 +31,11 @@
 REST_SLOT = REST_FIRST + 16
 REST = REST_SLOT + 16
 LATE_HALF = 2432
-HALF_ROWS = 13832
 FLAT_SCRATCH = 13848
 O_ROW = 4329
 GATE_ROW = 6921
 MLP_COLS = 256
+WIDEN = 512
 MLP_UNROLL = 6
 MLP_BLOCK = 256
 CHUNK = 576
@@ -167,26 +167,37 @@
 def prepare_weights(
     core_ref, own_ref, other_ref,
     ga_ref, gm_ref, wq_ref, wkv_ref, wo_ref, wg_ref, wu_ref, wd_ref,
-    both, flat, tmp, sem,
+    first, second, flat, tmp, rest, sem,
 ):
     core = core_ref[0]
-    copies = [
-        pltpu.make_async_copy(own_ref, both.at[core], sem.at[0]),
-        pltpu.make_async_copy(other_ref, both.at[1 - core], sem.at[1]),
-    ]
-    for copy in copies:
-        copy.start()
-    for copy in copies:
-        copy.wait()
-    step = HALF_ROWS // 13
-
-    def widen(which):
+    for which, pair in enumerate(((first, second), (second, first))):
+
+        @pl.when(core == which)
+        def _(pair=pair):
+            copies = [
+                pltpu.make_async_copy(ref, target, sem.at[i])
+                for i, (ref, target) in enumerate(zip((own_ref, other_ref), pair))
+            ]
+            for copy in copies:
+                copy.start()
+            for copy in copies:
+                copy.wait()
+
+    def widen(ref):
         def body(i, carry):
-            rows = pl.ds(pl.multiple_of(i * step, 8), step)
-            flat[rows, :] = both[which, rows, :].astype(F32)
+            start = pl.multiple_of(i * WIDEN, WIDEN)
+            span = pl.ds(pl.multiple_of(i * WIDEN * LANES, WIDEN * LANES), WIDEN * LANES)
+            flat[pl.ds(start, WIDEN), :] = ref[span].reshape(WIDEN, LANES)
             return carry
 
-        lax.fori_loop(0, 13, body, 0)
+        whole = HALF // (WIDEN * LANES)
+        lax.fori_loop(0, whole, body, 0)
+        left = HALF - whole * WIDEN * LANES
+        rest[pl.ds(0, left)] = ref[pl.ds(whole * WIDEN * LANES, left)]
+        flat[whole * WIDEN : whole * WIDEN + 8, :] = rest[...].reshape(8, LANES)
+
+    def low_precision(value):
+        return value.astype(BF).astype(F32)
 
     def interleave(even, odd, pairs, out_ref, first_row, pad):
         low = low_half(2 * pairs)
@@ -211,14 +222,16 @@
         odd = [jnp.where(low, turned[t], turned[t + 1]) for t in range(4)] + [turned[4]]
         interleave(cols[:5], odd, pairs, out_ref, 0, pad)
 
-    widen(0)
+    widen(first)
     low1 = low_half(1)
     turned = [flip(flat[4 + r : 5 + r, :]) for r in range(5)]
     for r in range(4):
-        ga_ref[:, r * LANES : (r + 1) * LANES] = flat[r : r + 1, :]
-        gm_ref[:, r * LANES : (r + 1) * LANES] = jnp.where(low1, turned[r], turned[r + 1])
-    ga_ref[:, 4 * LANES :] = flat[4:5, :HD]
-    gm_ref[:, 4 * LANES :] = turned[4][:, :HD]
+        ga_ref[:, r * LANES : (r + 1) * LANES] = low_precision(flat[r : r + 1, :])
+        gm_ref[:, r * LANES : (r + 1) * LANES] = low_precision(
+            jnp.where(low1, turned[r], turned[r + 1])
+        )
+    ga_ref[:, 4 * LANES :] = low_precision(flat[4:5, :HD])
+    gm_ref[:, 4 * LANES :] = low_precision(turned[4][:, :HD])
     wide(9, wq_ref, True)
     wide(O_ROW, wo_ref, False)
     wo_ref[D:, :] = jnp.zeros((PAD_D - D, D), BF)
@@ -241,7 +254,7 @@
     wkv_ref[:, 0:LANES] = k0.astype(BF)
     wkv_ref[:, LANES : 2 * LANES] = jnp.where(low, k1, v0).astype(BF)
     wkv_ref[:, 2 * LANES :] = jnp.where(low, v0, v1).astype(BF)
-    head = both[1, 0:16, :].astype(F32)
+    head = second[pl.ds(0, 1024)].reshape(8, LANES)
     turned = flip(head)
     for r in range(5):
         row = GATE_ROW + FF_TILES * (D - 1) + 7 + r
@@ -251,7 +264,7 @@
         wg_ref[:, t * LANES : (t + 1) * LANES] = flat[
             pl.ds(GATE_ROW + t, D, stride=FF_TILES), :
         ].astype(BF)
-    widen(1)
+    widen(second)
     here = flip(flat[pl.ds(4, D, stride=FF_TILES), :])
     for t in range(FF_TILES):
         after = flip(flat[pl.ds(5 + t, D, stride=FF_TILES), :])
@@ -885,9 +898,9 @@
 
 def update_late(scale, rate, core_ref, own_ref, other_ref, *rest):
     ins, outs = rest[:3], rest[7:11]
-    flat, tmp, late_ref, in_buf, out_buf, in_sem, out_sem = rest[11:18]
+    flat, tmp, late_ref, in_buf, out_buf, in_sem, out_sem, part_sem = rest[11:19]
     refs = (ins, outs, in_buf, out_buf, in_sem, out_sem)
-    extra = Extra(LATE_CHUNKS * CHUNK * LANES, ins, outs, rest[18:])
+    extra = Extra(LATE_CHUNKS * CHUNK * LANES, ins, outs, rest[19:])
     rule = functools.partial(update_rule, scale, rate)
 
     @pl.when(core_ref[0] == 0)
@@ -895,8 +908,12 @@
         chunks = Chunks(CHUNK, 0, LATE_CHUNKS, rule, refs)
         chunks.start()
         extra.start()
-        late_ref[:LATE_HALF, :] = own_ref[...]
-        late_ref[LATE_HALF:, :] = other_ref[...]
+        pieces = [
+            (own_ref, late_ref.at[pl.ds(0, LATE_HALF)]),
+            (other_ref, late_ref.at[pl.ds(LATE_HALF, LATE_HALF)]),
+        ]
+        for copy in load_parts(pieces, part_sem):
+            copy.wait()
 
         def late(index):
             return late_ref[index * D : (index + 1) * D, :].astype(F32)
@@ -988,9 +1005,11 @@
         ((FF, D), BF),
     ]
     scratch = [
-        pltpu.VMEM((2, HALF_ROWS, LANES), BF),
+        pltpu.VMEM((HALF,), F32),
+        pltpu.VMEM((HALF,), F32),
         pltpu.VMEM((FLAT_SCRATCH, LANES), F32),
         pltpu.VMEM((Q_TILES * D, LANES), F32),
+        pltpu.VMEM((8 * LANES,), F32),
         pltpu.SemaphoreType.DMA((2,)),
     ]
     return call(
@@ -1001,7 +1020,7 @@
         scratch,
         1e10,
         "prepare_weights",
-        60,
+        56,
     )(core, own, other)
 
 
@@ -1023,7 +1042,7 @@
         [pltpu.VMEM((Q_TILES, BLOCK, LANES), F32)],
         1.5e10,
         "attention_forward",
-        60,
+        56,
     )(x, gain, wq, wkv, wo, cosine, sine)
 
 
@@ -1066,7 +1085,7 @@
         ],
         2.5e10,
         "mlp_pass",
-        60,
+        56,
     )(core, slot, lengths, assignment, hidden1, cot, mixed, gain, wo, wg, wu, wd)
 
 
@@ -1093,7 +1112,7 @@
             single,
         ],
         scratch_shapes=[pltpu.VMEM((2, seq_len, LANES), F32)] * 2,
-        compiler_params=pltpu.CompilerParams(vmem_limit_bytes=60 * MIB),
+        compiler_params=pltpu.CompilerParams(vmem_limit_bytes=56 * MIB),
         cost_estimate=pl.CostEstimate(
             flops=int(8e9) * count, bytes_accessed=int(3e6) * count, transcendentals=0
         ),
@@ -1118,7 +1137,7 @@
         [],
         4e9,
         "backward_finish",
-        60,
+        56,
     )(x, gain, dh1, *groups[0], *groups[1], wq, wkv, cosine, sine)
 
 
@@ -1132,7 +1151,7 @@
         [pltpu.VMEM((2 * LATE_HALF, LANES), BF), pltpu.SemaphoreType.DMA((2,))],
         4e9,
         "late_weights",
-        60,
+        56,
     )(core, normed, d_query, d_kv, gga, ggm)
 
 
@@ -1203,7 +1222,7 @@
         scratch,
         1e9,
         "update_first",
-        60,
+        56,
     )(core, bits, *halves, *state)
 
 
@@ -1227,7 +1246,7 @@
         scratch,
         1e9,
         "update_second",
-        60,
+        56,
         {13 + i: i for i in range(4)},
     )(core, bits, *halves, *state, *done)
 
@@ -1239,17 +1258,18 @@
         pltpu.VMEM((Q_TILES * D, LANES), F32),
         pltpu.VMEM((2 * LATE_HALF, LANES), BF),
         *chunk_scratch(LATE_CHUNKS),
+        pltpu.SemaphoreType.DMA((2,)),
         *extra_scratch(last_rows * LANES, 304),
     ]
     return call(
         functools.partial(update_late, scale, rate),
         [(state[0].shape, F32)] * 4,
-        [smem()] + [vmem()] * 2 + [hbm()] * 7,
+        [smem()] + [hbm()] * 9,
         [hbm()] * 4,
         scratch,
         1e9,
         "update_late",
-        60,
+        56,
         {6 + i: i for i in range(4)},
     )(core, own, other, *state, *done)
 
@@ -1272,31 +1292,22 @@
     return jnp.stack([(index >> order[step]) & 1 for order in orders]).astype(jnp.int32)
 
 
-def spread(blocks, far):
-    size = lax.axis_size("dp")
-    near = min(size, 4)
-    if far:
-        groups = [[g * near + i for g in range(size // near)] for i in range(near)]
-    else:
-        groups = [[g * near + i for i in range(near)] for g in range(size // near)]
+def near_size():
+    return min(lax.axis_size("dp"), 4)
+
+
+def spread(blocks):
+    size, near = lax.axis_size("dp"), near_size()
+    groups = [[g * near + i for i in range(near)] for g in range(size // near)]
     return lax.all_to_all(
         blocks, "dp", split_axis=0, concat_axis=0, tiled=True, axis_index_groups=groups
     )
 
 
-def group_size(far):
-    size = lax.axis_size("dp")
-    return size // min(size, 4) if far else min(size, 4)
-
-
 def scatter_sum(value):
-    count = group_size(False)
-    blocks = spread(value.reshape(count, value.shape[0] // count, LANES), False)
+    count = near_size()
+    blocks = spread(value.reshape(count, value.shape[0] // count, LANES))
     return jnp.sum(blocks.astype(F32), axis=0).astype(BF)
-
-
-def copies(value, far):
-    return spread(jnp.broadcast_to(value[None], (group_size(far), *value.shape)), far)
 
 
 def bit_orders():
@@ -1325,14 +1336,11 @@
     def exchange(value):
         return lax.all_to_all(value, axes, split_axis=0, concat_axis=0, tiled=True)
 
-    sent_in, master_in = tie(pick(inputs, assignment), master)
-    x = exchange(sent_in).reshape(seq_len, D)
+    x = exchange(pick(inputs, assignment)).reshape(seq_len, D)
     slot_arr = my_slot.astype(jnp.int32).reshape(1)
 
-    own = jnp.pad(master_in.astype(BF), (0, HALF_ROWS * LANES - master.shape[0]))
-    own = own.reshape(HALF_ROWS, LANES)
-    other = lax.ppermute(own, "shard", [(0, 1), (1, 0)])
-    gain_attn, gain_mlp, wq, wkv, wo, wg, wu, wd = run_prepare(core_arr, own, other)
+    other = lax.ppermute(master, "shard", [(0, 1), (1, 0)])
+    gain_attn, gain_mlp, wq, wkv, wo, wg, wu, wd = run_prepare(core_arr, master, other)
 
     cosine, sine = rope_tables(seq_len)
     sent_cot, gain_attn, cosine = tie(pick(cotangent, inverse), gain_attn, cosine)
@@ -1375,18 +1383,34 @@
             late_send, sent[0] = tie(late_send, sent[0])
     got = [xor_swap(sent[0], last_bit)]
     late_got = lax.ppermute(late_send, "shard", [(0, 1), (1, 0)])
+    late, _ = run_sum(my_bits(orders, 0)[:1], [late_keep], [late_got], False)
+    late, block_output, *got = tie(scatter_sum(late[0]), pick(back_out, return_order), *got)
     early, _ = run_sum(my_bits(orders, last_bit)[:1], kept, got, False)
-    late, _ = run_sum(my_bits(orders, 0)[:1], [late_keep], [late_got], False)
-    late, block_output, early[0] = tie(late[0], pick(back_out, return_order), early[0])
-    late = scatter_sum(late)
-    early = run_join(my_bits(orders, last_bit), early, [xor_swap(early[0], last_bit)], 3)
-    late, *early = tie(late, *early)
-    late = jnp.sum(copies(late, True).astype(F32), axis=0).astype(BF)
+    far_bits = list(range(near_size().bit_length() - 1, n_bits))
+
+    def add_far(late, early):
+        late, *early = tie(late, *early)
+        return add_low(late, xor_swap(late, far_bits.pop(0))), early
+
+    got = xor_swap(early[0], last_bit)
+    late = add_low(late, xor_swap(late, far_bits.pop(0)))
+    late, got = tie(late, got)
+    early = run_join(my_bits(orders, last_bit), early, [got], 3)
+    whole = None
     for step in reversed(range(1, last_bit)):
-        early = run_join(my_bits(orders, step), early, swap_parts(early, step), 3)
-        if step == last_bit - 1:
+        if far_bits:
+            late, early = add_far(late, early)
+        elif whole is None:
             late, *early = tie(late, *early)
-            late = copies(late, False).reshape(-1, LANES)
+            whole = spread(jnp.broadcast_to(late[None], (near_size(), *late.shape)))
+        got = swap_parts(early, step)
+        late, *got = tie(late, *got)
+        early = run_join(my_bits(orders, step), early, got, 3)
+    while far_bits:
+        late, early = add_far(late, early)
+    if whole is None:
+        whole = spread(jnp.broadcast_to(late[None], (near_size(), *late.shape)))
+    late = whole.reshape(-1, LANES)
     got = swap_parts(early, 0)
     swap_own = lax.ppermute(early[2], "shard", [(0, 1)])
     bits = my_bits(orders, 0)

time: 286 us -> 266 us (0.930)
  waiting for transfers between devices: 48.3 us -> 41.3 us
  starting transfers between devices: 60.4 us -> 56.6 us
    ppermute x20 -> x22, waiting for transfers between devices: 35.8 us -> 26 us  [xor_swap(): return lax.ppermute(value, 'dp', [(i, i ^ 1 << bit) for i in range(size)])]
    ppermute x20 -> x22, starting transfers between devices: 18.7 us -> 22.3 us  [xor_swap(): return lax.ppermute(value, 'dp', [(i, i ^ 1 << bit) for i in range(size)])]
    all_to_all x2 -> x1, starting transfers between devices: 6.97 us -> 3.49 us  [spread(): lax.all_to_all(blocks, 'dp', split_axis=0, concat_axis=0, tiled=True, axi...]
    all_to_all x2 -> x1, waiting for transfers between devices: 1.61 us -> 5.01 us  [spread(): lax.all_to_all(blocks, 'dp', split_axis=0, concat_axis=0, tiled=True, axi...]
    convert_element_type x1 -> x2, other arithmetic: 3.27 us -> 0.09 us  [add_low(): return (a.astype(F32) + b.astype(F32)).astype(BF)]
    all_to_all x4, starting transfers between devices: 24.5 us -> 21.3 us  [exchange(): return lax.all_to_all(value, axes, split_axis=0, concat_axis=0, tiled=True)]
  transfers between devices with their start and end apart: 32 -> 33, of which waited for: 11 -> 13; matrix products, arithmetic and copies ran while one was open for 3% -> 4% of each run, Pallas kernels for 35% -> 36%
where the time goes in v1:
time: 266 us; the launch traced here: 263 us
  Pallas kernels  130 us (49%)
  starting transfers between devices  56.6 us (21%)
  waiting for transfers between devices  41.3 us (16%)
  blocking collectives  15.6 us (6%)
  local copies, waits for them, and re-layouts  14.2 us (5%)
  other arithmetic  4.23 us (2%)
    pallas_call x1, Pallas kernels, run_mlp(): call(mlp_pass, outs, [smem()] * 4 + [hbm()] * 3 + [vmem()] + [hbm()] * 4,...  28.4 us
    ppermute x22, waiting for transfers between devices, xor_swap(): return lax.ppermute(value, 'dp', [(i, i ^ 1 << bit) for i in range(size)])  26 us
    ppermute x22, starting transfers between devices, xor_swap(): return lax.ppermute(value, 'dp', [(i, i ^ 1 << bit) for i in range(size)])  22.3 us
    all_to_all x4, starting transfers between devices, exchange(): return lax.all_to_all(value, axes, split_axis=0, concat_axis=0, tiled=True)  21.3 us
    pallas_call x1, Pallas kernels, run_attention_forward(): call(attention_forward, outs, [vmem()] * 7, [vmem()] * 6, [pltpu.VMEM((Q_...  21.3 us
    pallas_call x2, Pallas kernels, run_backward_groups(): pl.pallas_call(functools.partial(backward_groups, first), grid=(count,),...  20.2 us
    all_to_all x1, blocking collectives, spread(): lax.all_to_all(blocks, 'dp', split_axis=0, concat_axis=0, tiled=True, axi...  15.6 us
    pallas_call x1, Pallas kernels, run_prepare(): call(prepare_weights, outs, [smem()] + [hbm()] * 2, [vmem()] * 8, scratch...  12.3 us
  transfers between devices with their start and end apart: 33, of which 13 were waited for; matrix products, arithmetic and copies ran while one was open for 4% of the time, Pallas kernels for 36%

profile of v1, /device:TPU:1, one launch (start us, length us, event | category | flops | bytes accessed | tf_op | source)
XLA Modules:
  0.0 262.8 jit_solution(7601484961295918824)
XLA Ops:
  3.5 7.1 %all-to-all-start = ((bf16[32,24,576]{2,1,0:T(8,128)(2,1)}), bf16[32,24,576]{2,1,0:T(8,128)(2,1)S(1)}, u32[]{:S(2)}, u32[]{:S(2)}) async-start(bf16[32,24,576]{2,1,0:T(8,128)(2,1)} %gather_fusion), calls=%async_computation | async-start | bytes 1966080 | tf_op jit(solution)/shard_map/all_to_all | solution.py:1337
  11.4 2.8 %gather_fusion.1 = bf16[32,24,576]{2,1,0:T(8,128)(2,1)} fusion(bf16[32,24,576]{2,1,0:T(8,128)(2,1)} %param.9, s32[1024]{0:T(1024)S(1)} %pad_clamp_fusion.1), kind=kCustom, calls=%fused_computation.1 | custom fusion | bytes 1769600 | tf_op jit(solution)/shard_map/gather | solution.py:1334
  16.5 12.3 %prepare_weights.1 = (f32[1,576]{1,0:T(1,128)}, f32[1,576]{1,0:T(1,128)}, bf16[576,640]{1,0:T(8,128)(2,1)}, bf16[576,384]{1,0:T(8,128)(2,1)}, bf16[640,576]{1,0:...) custom-call(s32[1]{0:T(128)} %bitcast.1.core_ref, ...), custom_call_target="tpu_custom_call" | custom-call | flops 10000000000 | bytes 14459904 | tf_op jit(solution)/shard_map/prepare_weights/pallas_call | solution.py:1015
  28.8 5.7 %all-to-all-done = bf16[32,24,576]{2,1,0:T(8,128)(2,1)S(1)} async-done(((bf16[32,24,576]{2,1,0:T(8,128)(2,1)}), bf16[32,24,576]{2,1,0:T(8,128)(2,1)S(1)}, u32[]{:S(2)}, u32[]{:S(2)}) %all-to-all-start) | async-done | bytes 884768 | tf_op jit(solution)/shard_map/all_to_all | solution.py:1337
  34.5 4.5 %all-to-all-start.1 = ((bf16[32,24,576]{2,1,0:T(8,128)(2,1)}), bf16[32,24,576]{2,1,0:T(8,128)(2,1)S(1)}, u32[]{:S(2)}, u32[]{:S(2)}) async-start(bf16[32,24,576]{2,1,0:T(8,128)(2,1)} %gather_fusion.1), calls=%async_computation.1 | async-start | bytes 1966080 | tf_op jit(solution)/shard_map/all_to_all | solution.py:1337
  39.1 21.3 %attention_forward.1 = (f32[768,576]{1,0:T(8,128)}, bf16[768,640]{1,0:T(8,128)(2,1)}, bf16[5,768,128]{2,1,0:T(8,128)(2,1)}, bf16[6,768,128]{2,1,0:T(8,128)(2,1)}...) custom-call(bf16[768,576]{1,0:T(8,128)(2,1)} %bitcast.19, f32[1,576]{1,0:T(1,128)} %get-tuple-element.131.ga_ref, ...), custom_call_target="tpu_custom_call" | custom-call | flops 15000000512 | bytes 12288000 | tf_op jit(solution)/shard_map/attention_forward/pallas_call | solution.py:1037
  63.9 28.4 %mlp_pass.1 = (bf16[768,576]{1,0:T(8,128)(2,1)}, f32[768,576]{1,0:T(8,128)}, bf16[5,768,128]{2,1,0:T(8,128)(2,1)}, f32[1,576]{1,0:T(1,128)}, bf16[12288,128]{1,0:T(8,128)(2,1)}, /*index=5*/bf16[12288,128]{1,0:T(8,128)(2,1)}) custom-call(s32[1]{0:T(128)} %bitcast.1.core_ref, s32[1]{0:T(128)} %bitcast.5.slot_ref, s32[32]{0:T(128)} %lengths_ref.1, ...), custom_call_target="tpu_custom_call" | custom-call | flops 24999999488 | bytes 19862016 | tf_op jit(solution)/shard_map/mlp_pass/pallas_call | solution.py:1059
  93.8 3.5 %all-to-all-start.2 = ((bf16[32,24,576]{2,1,0:T(8,128)(2,1)}), bf16[32,24,576]{2,1,0:T(8,128)(2,1)}, u32[]{:S(2)}, u32[]{:S(2)}) async-start(bf16[32,24,576]{2,1,0:T(8,128)(2,1)} %bitcast.21), calls=%async_computation.2 | async-start | bytes 1966080 | tf_op jit(solution)/shard_map/all_to_all | solution.py:1337
  97.3 7.6 %backward_groups.2 = (f32[1,2,768,128]{3,2,1,0:T(8,128)}, f32[1,768,128]{2,1,0:T(8,128)}, f32[1,768,128]{2,1,0:T(8,128)}) custom-call(bf16[5,768,128]{2,1,0:T(8,128)(2,1)} %get-tuple-element.163.q_ref, bf16[5,768,128]{2,1,0:T(8,128)(2,1)} %get-tuple-element.164.dm_ref, bf16[6,768,128]{2,1,0:T(8,128)(2,1)} %get-tuple-element.165.k_ref, ...), custom_call_target="tpu_custom_call" | custom-call | flops 8000000000 | bytes 3000000 | tf_op jit(solution)/shard_map/backward_groups/pallas_call | solution.py:1098
  110.9 12.6 %backward_groups.3 = (f32[2,2,768,128]{3,2,1,0:T(8,128)}, f32[2,768,128]{2,1,0:T(8,128)}, f32[2,768,128]{2,1,0:T(8,128)}) custom-call(bf16[5,768,128]{2,1,0:T(8,128)(2,1)} %get-tuple-element.163.q_ref, bf16[5,768,128]{2,1,0:T(8,128)(2,1)} %get-tuple-element.164.dm_ref, bf16[6,768,128]{2,1,0:T(8,128)(2,1)} %get-tuple-element.165.k_ref, ...), custom_call_target="tpu_custom_call" | custom-call | flops 16000000000 | bytes 6000000 | tf_op jit(solution)/shard_map/backward_groups/pallas_call | solution.py:1098
  130.4 8.7 %backward_finish.1 = (bf16[768,576]{1,0:T(8,128)(2,1)}, bf16[768,640]{1,0:T(8,128)(2,1)}, bf16[768,384]{1,0:T(8,128)(2,1)}, bf16[768,576]{1,0:T(8,128)(2,1)}, f32[1,576]{1,0:T(1,128)}) custom-call(bf16[768,576]{1,0:T(8,128)(2,1)} %bitcast.20, f32[1,576]{1,0:T(1,128)} %get-tuple-element.131.ga_ref, f32[768,576]{1,0:T(8,128)} %get-tuple-element.162.dh1_ref, ...), custom_call_target="tpu_custom_call" | custom-call | flops 4000000000 | bytes 6689280 | tf_op jit(solution)/shard_map/backward_finish/pallas_call | solution.py:1132
  143.8 4.1 %late_weights.1 = (bf16[2432,128]{1,0:T(8,128)(2,1)}, bf16[2432,128]{1,0:T(8,128)(2,1)}) custom-call(s32[1]{0:T(128)} %bitcast.1.core_ref, bf16[768,576]{1,0:T(8,128)(2,1)} %get-tuple-element.174.nm_s, bf16[768,640]{1,0:T(8,128)(2,1)} %get-tuple-element.175.dq_s, bf16[768,384]{1,0:T(8,128)(2,1)} %get-tuple-element.176.dkv_s, ...), custom_call_target="tpu_custom_call" | custom-call | flops 4000000000 | bytes 2490368 | tf_op jit(solution)/shard_map/late_weights/pallas_call | solution.py:1146
  149.1 3.1 %collective-permute-start.11 = (bf16[2432,128]{1,0:T(8,128)(2,1)}, bf16[2432,128]{1,0:T(8,128)(2,1)S(1)}, u32[]{:S(2)}, u32[]{:S(2)}) collective-permute-start(bf16[2432,128]{1,0:T(8,128)(2,1)} %get-tuple-element.202), channel_id=1, source_target_pairs={{0,1},{1,0},{2,3},{3,2},{4,5},{5,4},{6,7},{7,6},{8,9},{9,8},{10,11... | collective-permute-start | bytes 1867784 | tf_op jit(solution)/shard_map/ppermute | solution.py:1385
  156.3 3.5 %all-to-all-start.3 = ((bf16[4,608,128]{2,1,0:T(8,128)(2,1)}), bf16[4,608,128]{2,1,0:T(8,128)(2,1)S(1)}, u32[]{:S(2)}, u32[]{:S(2)}) async-start(bf16[4,608,128]{2,1,0:T(8,128)(2,1)} %bitcast.10), calls=%async_computation.3 | async-start | bytes 1245184 | tf_op jit(solution)/shard_map/all_to_all | solution.py:1302
  160.7 2.8 %gather_fusion.2 = bf16[32,24,576]{2,1,0:T(8,128)(2,1)} fusion(bf16[32,24,576]{2,1,0:T(8,128)(2,1)} %all-to-all-done.2, s32[1024]{0:T(1024)S(1)} %pad_clamp_fusion), kind=kCustom, calls=%fused_computation.2 | custom fusion | bytes 1769600 | tf_op jit(solution)/shard_map/gather | solution.py:1334
  163.5 5.0 %all-to-all-done.3 = bf16[4,608,128]{2,1,0:T(8,128)(2,1)S(1)} async-done(((bf16[4,608,128]{2,1,0:T(8,128)(2,1)}), bf16[4,608,128]{2,1,0:T(8,128)(2,1)S(1)}, u32[]{:S(2)}, u32[]{:S(2)}) %all-to-all-start.3) | async-done | bytes 622624 | tf_op jit(solution)/shard_map/all_to_all | solution.py:1302
  174.2 5.1 %collective-permute-done.13 = bf16[608,128]{1,0:T(8,128)(2,1)S(1)} collective-permute-done((bf16[608,128]{1,0:T(8,128)(2,1)S(1)}, bf16[608,128]{1,0:T(8,128)(2,1)S(1)}, u32[]{:S(2)}, u32[]{:S(2)}) %collective-permute-start.13) | collective-permute-done | bytes 155680 | tf_op jit(solution)/shard_map/ppermute | solution.py:1283
  179.3 3.7 %collective-permute-done.14.refs_1_ = bf16[768,128]{1,0:T(8,128)(2,1)S(1)} collective-permute-done((bf16[768,128]{1,0:T(8,128)(2,1)S(1)}, bf16[768,128]{1,0:T(8,128)(2,1)S(1)}, u32[]{:S(2)}, u32[]{:S(2)}) %collective-permute-start.14) | collective-permute-done | bytes 196640 | tf_op jit(solution)/shard_map/ppermute | solution.py:1283
  189.1 5.0 %collective-permute-done.15 = bf16[608,128]{1,0:T(8,128)(2,1)S(1)} collective-permute-done((bf16[608,128]{1,0:T(8,128)(2,1)S(1)}, bf16[608,128]{1,0:T(8,128)(2,1)S(1)}, u32[]{:S(2)}, u32[]{:S(2)}) %collective-permute-start.15) | collective-permute-done | bytes 155680 | tf_op jit(solution)/shard_map/ppermute | solution.py:1283
  198.4 4.4 %collective-permute-done.19.refs_3_ = bf16[1024,128]{1,0:T(8,128)(2,1)S(1)} collective-permute-done((bf16[1024,128]{1,0:T(8,128)(2,1)S(1)}, bf16[1024,128]{1,0:T(8,128)(2,1)S(1)}, u32[]{:S(2)}, u32[]{:S(2)}) %collective-permute-start.19) | collective-permute-done | bytes 262176 | tf_op jit(solution)/shard_map/ppermute | solution.py:1283
  209.0 15.6 %all_to_all.30 = bf16[4,608,128]{2,1,0:T(8,128)(2,1)S(1)} all-to-all(bf16[4,608,128]{2,1,0:T(8,128)(2,1)S(1)} %broadcast_in_dim.46), channel_id=1, replica_groups={{0,2,4,6},{8,10,12,14},{16,18,20,22},{24,26,28,30},{1,3,5,7},{9,11,13,1..., dimensions={0} | all-to-all | bytes 1245184 | tf_op jit(solution)/shard_map/all_to_all | solution.py:1302
  225.7 6.2 %all-to-all-start.5 = ((bf16[32,24,576]{2,1,0:T(8,128)(2,1)}), bf16[32,24,576]{2,1,0:T(8,128)(2,1)S(1)}, u32[]{:S(2)}, u32[]{:S(2)}) async-start(bf16[32,24,576]{2,1,0:T(8,128)(2,1)} %bitcast.18), calls=%async_computation.5 | async-start | bytes 1966080 | tf_op jit(solution)/shard_map/all_to_all | solution.py:1337
  235.6 11.2 %update_first.1 = (f32[1770048]{0:T(1024)}, f32[1770048]{0:T(1024)}, f32[1770048]{0:T(1024)}, f32[1770048]{0:T(1024)}) custom-call(s32[1]{0:T(128)} %bitcast.1.core_ref, s32[3]{0:T(128)} %copy-done.7, bf16[2048,128]{1,0:T(8,128)(2,1)} %copy-done.3, bf16[2048,128]{1,0:T(8,128)(2,1)} %copy-done.9, bf16[2048,128]{1,0:T(8,128)(2,1)} %copy-done.4, ...), custom_call_target="tpu_custom_call" | custom-call | flops 1000000000 | bytes 56641536 | tf_op jit(solution)/shard_map/update_first/pallas_call | solution.py:1217
  247.6 11.9 %update_second.1 = (f32[1770048]{0:T(1024)}, f32[1770048]{0:T(1024)}, f32[1770048]{0:T(1024)}, f32[1770048]{0:T(1024)}) custom-call(s32[1]{0:T(128)} %bitcast.1.core_ref, s32[3]{0:T(128)} %copy-done.7, bf16[2048,128]{1,0:T(8,128)(2,1)} %copy-done.3, ...), custom_call_target="tpu_custom_call", output_to_operand_aliasing={{0}: (13, {}), {1}: (14, {}), {2}: (15, {}), {3}: (16, {})} | custom-call | flops 1000000000 | bytes 56641536 | tf_op jit(solution)/shard_map/update_second/pallas_call | solution.py:1241
  (117 shorter events, 65.7 us)
Async XLA Ops:
  0.6 15.8 %collective-permute-start = (f32[1770048]{0:T(1024)}, f32[1770048]{0:T(1024)}, u32[]{:S(2)}, u32[]{:S(2)}) collective-permute-start(f32[1770048]{0:T(1024)} %rest_0_.1), channel_id=1, source_target_pairs={{0,1},{1,0},{2,3},{3,2},{4,5},{5,4},{6,7},{7,6},{8,9},{9,8},{10,11... | collective-permute-start | bytes 21240584 | tf_op jit(solution)/shard_map/ppermute | solution.py:1342
  3.5 31.0 %all-to-all-start = ((bf16[32,24,576]{2,1,0:T(8,128)(2,1)}), bf16[32,24,576]{2,1,0:T(8,128)(2,1)S(1)}, u32[]{:S(2)}, u32[]{:S(2)}) async-start(bf16[32,24,576]{2,1,0:T(8,128)(2,1)} %gather_fusion), calls=%async_computation | async-start | bytes 1966080 | tf_op jit(solution)/shard_map/all_to_all | solution.py:1337
  34.5 28.5 %all-to-all-start.1 = ((bf16[32,24,576]{2,1,0:T(8,128)(2,1)}), bf16[32,24,576]{2,1,0:T(8,128)(2,1)S(1)}, u32[]{:S(2)}, u32[]{:S(2)}) async-start(bf16[32,24,576]{2,1,0:T(8,128)(2,1)} %gather_fusion.1), calls=%async_computation.1 | async-start | bytes 1966080 | tf_op jit(solution)/shard_map/all_to_all | solution.py:1337
  92.3 12.6 %collective-permute-start.1 = (bf16[12288,128]{1,0:T(8,128)(2,1)}, bf16[12288,128]{1,0:T(8,128)(2,1)S(1)}, u32[]{:S(2)}, u32[]{:S(2)}) collective-permute-start(bf16[12288,128]{1,0:T(8,128)(2,1)} %get-tuple-element.146), channel_id=1, source_target_pairs={{0,1},{1,0},{2,3},{3,2},{4,5},{5,4},{6,7},{7,6},{8,9},{9,8},{10,11... | collective-permute-start | bytes 9437192 | tf_op jit(solution)/shard_map/ppermute | solution.py:1360
  93.8 36.6 %all-to-all-start.2 = ((bf16[32,24,576]{2,1,0:T(8,128)(2,1)}), bf16[32,24,576]{2,1,0:T(8,128)(2,1)}, u32[]{:S(2)}, u32[]{:S(2)}) async-start(bf16[32,24,576]{2,1,0:T(8,128)(2,1)} %bitcast.21), calls=%async_computation.2 | async-start | bytes 1966080 | tf_op jit(solution)/shard_map/all_to_all | solution.py:1337
  107.1 16.7 %collective-permute-start.2 = (bf16[2048,128]{1,0:T(8,128)(2,1)}, bf16[2048,128]{1,0:T(8,128)(2,1)S(1)}, u32[]{:S(2)}, u32[]{:S(2)}) collective-permute-start(bf16[2048,128]{1,0:T(8,128)(2,1)} %get-tuple-element.156), channel_id=1, source_target_pairs={{0,2},{2,0},{4,6},{6,4},{8,10},{10,8},{12,14},{14,12},{16,18},{18,... | collective-permute-start | bytes 1572872 | tf_op jit(solution)/shard_map/ppermute | solution.py:1283
  108.6 16.6 %collective-permute-start.3 = (bf16[2048,128]{1,0:T(8,128)(2,1)}, bf16[2048,128]{1,0:T(8,128)(2,1)S(1)}, u32[]{:S(2)}, u32[]{:S(2)}) collective-permute-start(bf16[2048,128]{1,0:T(8,128)(2,1)} %get-tuple-element.157), channel_id=1, source_target_pairs={{0,4},{2,6},{4,0},{6,2},{8,12},{10,14},{12,8},{14,10},{16,20},{18,... | collective-permute-start | bytes 1572872 | tf_op jit(solution)/shard_map/ppermute | solution.py:1283
  109.8 17.6 %collective-permute-start.4 = (bf16[2048,128]{1,0:T(8,128)(2,1)}, bf16[2048,128]{1,0:T(8,128)(2,1)S(1)}, u32[]{:S(2)}, u32[]{:S(2)}) collective-permute-start(bf16[2048,128]{1,0:T(8,128)(2,1)} %get-tuple-element.158), channel_id=1, source_target_pairs={{0,8},{2,10},{4,12},{6,14},{8,0},{10,2},{12,4},{14,6},{16,24},{18,... | collective-permute-start | bytes 1572872 | tf_op jit(solution)/shard_map/ppermute | solution.py:1283
  128.5 10.6 %collective-permute-start.5 = (bf16[1024,128]{1,0:T(8,128)(2,1)S(1)}, bf16[1024,128]{1,0:T(8,128)(2,1)S(1)}, u32[]{:S(2)}, u32[]{:S(2)}) collective-permute-start(bf16[1024,128]{1,0:T(8,128)(2,1)S(1)} %get-tuple-element.181), channel_id=1, source_target_pairs={{0,4},{2,6},{4,0},{6,2},{8,12},{10,14},{12,8},{14,10},{16,20},{18,... | collective-permute-start | bytes 786440 | tf_op jit(solution)/shard_map/ppermute | solution.py:1283
  129.6 9.5 %collective-permute-start.6 = (bf16[1024,128]{1,0:T(8,128)(2,1)S(1)}, bf16[1024,128]{1,0:T(8,128)(2,1)S(1)}, u32[]{:S(2)}, u32[]{:S(2)}) collective-permute-start(bf16[1024,128]{1,0:T(8,128)(2,1)S(1)} %get-tuple-element.182), channel_id=1, source_target_pairs={{0,8},{2,10},{4,12},{6,14},{8,0},{10,2},{12,4},{14,6},{16,24},{18,... | collective-permute-start | bytes 786440 | tf_op jit(solution)/shard_map/ppermute | solution.py:1283
  129.6 9.5 %collective-permute-start.7 = (bf16[1024,128]{1,0:T(8,128)(2,1)S(1)}, bf16[1024,128]{1,0:T(8,128)(2,1)S(1)}, u32[]{:S(2)}, u32[]{:S(2)}) collective-permute-start(bf16[1024,128]{1,0:T(8,128)(2,1)S(1)} %get-tuple-element.183), channel_id=1, source_target_pairs={{0,2},{2,0},{4,6},{6,4},{8,10},{10,8},{12,14},{14,12},{16,18},{18,... | collective-permute-start | bytes 786440 | tf_op jit(solution)/shard_map/ppermute | solution.py:1283
  156.3 12.3 %all-to-all-start.3 = ((bf16[4,608,128]{2,1,0:T(8,128)(2,1)}), bf16[4,608,128]{2,1,0:T(8,128)(2,1)S(1)}, u32[]{:S(2)}, u32[]{:S(2)}) async-start(bf16[4,608,128]{2,1,0:T(8,128)(2,1)} %bitcast.10), calls=%async_computation.3 | async-start | bytes 1245184 | tf_op jit(solution)/shard_map/all_to_all | solution.py:1302
  159.8 11.7 %collective-permute-start.12 = (bf16[768,128]{1,0:T(8,128)(2,1)S(1)}, bf16[768,128]{1,0:T(8,128)(2,1)S(1)}, u32[]{:S(2)}, u32[]{:S(2)}) collective-permute-start(bf16[768,128]{1,0:T(8,128)(2,1)S(1)} %get-tuple-element.204), channel_id=1, source_target_pairs={{0,16},{2,18},{4,20},{6,22},{8,24},{10,26},{12,28},{14,30},{16,0},... | collective-permute-start | bytes 589832 | tf_op jit(solution)/shard_map/ppermute | solution.py:1283
  171.5 7.8 %collective-permute-start.13 = (bf16[608,128]{1,0:T(8,128)(2,1)S(1)}, bf16[608,128]{1,0:T(8,128)(2,1)S(1)}, u32[]{:S(2)}, u32[]{:S(2)}) collective-permute-start(bf16[608,128]{1,0:T(8,128)(2,1)S(1)} %reduce_sum.25), channel_id=1, source_target_pairs={{0,8},{2,10},{4,12},{6,14},{8,0},{10,2},{12,4},{14,6},{16,24},{18,... | collective-permute-start | bytes 466952 | tf_op jit(solution)/shard_map/ppermute | solution.py:1283
  171.8 11.2 %collective-permute-start.14 = (bf16[768,128]{1,0:T(8,128)(2,1)S(1)}, bf16[768,128]{1,0:T(8,128)(2,1)S(1)}, u32[]{:S(2)}, u32[]{:S(2)}) collective-permute-start(bf16[768,128]{1,0:T(8,128)(2,1)S(1)} %gather_sum.11.refs_0_), channel_id=1, source_target_pairs={{0,16},{2,18},{4,20},{6,22},{8,24},{10,26},{12,28},{14,30},{16,0},... | collective-permute-start | bytes 589832 | tf_op jit(solution)/shard_map/ppermute | solution.py:1283
  184.2 9.9 %collective-permute-start.15 = (bf16[608,128]{1,0:T(8,128)(2,1)S(1)}, bf16[608,128]{1,0:T(8,128)(2,1)S(1)}, u32[]{:S(2)}, u32[]{:S(2)}) collective-permute-start(bf16[608,128]{1,0:T(8,128)(2,1)S(1)} %add_convert_fusion.1), channel_id=1, source_target_pairs={{0,16},{2,18},{4,20},{6,22},{8,24},{10,26},{12,28},{14,30},{16,0},... | collective-permute-start | bytes 466952 | tf_op jit(solution)/shard_map/ppermute | solution.py:1283
  184.2 9.9 %collective-permute-start.16 = (bf16[512,128]{1,0:T(8,128)(2,1)S(1)}, bf16[512,128]{1,0:T(8,128)(2,1)S(1)}, u32[]{:S(2)}, u32[]{:S(2)}) collective-permute-start(bf16[512,128]{1,0:T(8,128)(2,1)S(1)} %get-tuple-element.216.refs_0_), channel_id=1, source_target_pairs={{0,8},{2,10},{4,12},{6,14},{8,0},{10,2},{12,4},{14,6},{16,24},{18,... | collective-permute-start | bytes 393224 | tf_op jit(solution)/shard_map/ppermute | solution.py:1283
  204.7 19.9 %collective-permute-start.22 = (bf16[2048,128]{1,0:T(8,128)(2,1)S(1)}, bf16[2048,128]{1,0:T(8,128)(2,1)S(1)}, u32[]{:S(2)}, u32[]{:S(2)}) collective-permute-start(bf16[2048,128]{1,0:T(8,128)(2,1)S(1)} %get-tuple-element.233.rest_4_), channel_id=1, source_target_pairs={{0,1},{2,3},{4,5},{6,7},{8,9},{10,11},{12,13},{14,15},{16,17},{18,... | collective-permute-start | bytes 1572872 | tf_op jit(solution)/shard_map/ppermute | solution.py:1415
  206.0 18.6 %collective-permute-start.23 = (bf16[2048,128]{1,0:T(8,128)(2,1)S(1)}, bf16[2048,128]{1,0:T(8,128)(2,1)S(1)}, u32[]{:S(2)}, u32[]{:S(2)}) collective-permute-start(bf16[2048,128]{1,0:T(8,128)(2,1)S(1)} %get-tuple-element.234.rest_0_), channel_id=1, source_target_pairs={{0,2},{2,0},{4,6},{6,4},{8,10},{10,8},{12,14},{14,12},{16,18},{18,... | collective-permute-start | bytes 1572872 | tf_op jit(solution)/shard_map/ppermute | solution.py:1283
  207.5 17.1 %collective-permute-start.24 = (bf16[2048,128]{1,0:T(8,128)(2,1)S(1)}, bf16[2048,128]{1,0:T(8,128)(2,1)S(1)}, u32[]{:S(2)}, u32[]{:S(2)}) collective-permute-start(bf16[2048,128]{1,0:T(8,128)(2,1)S(1)} %get-tuple-element.235.rest_2_), channel_id=1, source_target_pairs={{0,4},{2,6},{4,0},{6,2},{8,12},{10,14},{12,8},{14,10},{16,20},{18,... | collective-permute-start | bytes 1572872 | tf_op jit(solution)/shard_map/ppermute | solution.py:1283
  207.8 16.8 %collective-permute-start.25 = (bf16[2048,128]{1,0:T(8,128)(2,1)S(1)}, bf16[2048,128]{1,0:T(8,128)(2,1)}, u32[]{:S(2)}, u32[]{:S(2)}) collective-permute-start(bf16[2048,128]{1,0:T(8,128)(2,1)S(1)} %get-tuple-element.233.rest_4_), channel_id=1, source_target_pairs={{0,8},{2,10},{4,12},{6,14},{8,0},{10,2},{12,4},{14,6},{16,24},{18,... | collective-permute-start | bytes 1572872 | tf_op jit(solution)/shard_map/ppermute | solution.py:1283
  225.7 35.5 %all-to-all-start.5 = ((bf16[32,24,576]{2,1,0:T(8,128)(2,1)}), bf16[32,24,576]{2,1,0:T(8,128)(2,1)S(1)}, u32[]{:S(2)}, u32[]{:S(2)}) async-start(bf16[32,24,576]{2,1,0:T(8,128)(2,1)} %bitcast.18), calls=%async_computation.5 | async-start | bytes 1966080 | tf_op jit(solution)/shard_map/all_to_all | solution.py:1337
  231.9 27.6 %collective-permute-start.26 = (bf16[2432,128]{1,0:T(8,128)(2,1)S(1)}, bf16[2432,128]{1,0:T(8,128)(2,1)S(1)}, u32[]{:S(2)}, u32[]{:S(2)}) collective-permute-start(bf16[2432,128]{1,0:T(8,128)(2,1)S(1)} %bitcast.16), channel_id=1, source_target_pairs={{1,0},{3,2},{5,4},{7,6},{9,8},{11,10},{13,12},{15,14},{17,16},{19,... | collective-permute-start | bytes 1867784 | tf_op jit(solution)/shard_map/ppermute | solution.py:1422
  234.2 12.5 %collective-permute-start.27 = (bf16[2048,128]{1,0:T(8,128)(2,1)}, bf16[2048,128]{1,0:T(8,128)(2,1)S(1)}, u32[]{:S(2)}, u32[]{:S(2)}) collective-permute-start(bf16[2048,128]{1,0:T(8,128)(2,1)} %collective-permute-done.25.rest_5_), channel_id=1, source_target_pairs={{0,1},{2,3},{4,5},{6,7},{8,9},{10,11},{12,13},{14,15},{16,17},{18,... | collective-permute-start | bytes 1572872 | tf_op jit(solution)/shard_map/ppermute | solution.py:1423
  (26 other events, 232.6 us)

commit v2 on v1

--- a/solution.py
+++ b/solution.py
@@ -86,8 +86,9 @@
 
 
 def attention_forward(
-    x_ref, ga_ref, wq_ref, wkv_ref, wo_ref, cos_ref, sin_ref,
-    h1_ref, mixed_ref, q_ref, k_ref, v_ref, lse_ref, o_acc,
+    x_ref, ga_ref, wq_ref, wkv_ref, wo_hbm, cos_ref, sin_ref,
+    h1_hbm, mixed_hbm, q_hbm, k_hbm, v_hbm, lse_ref,
+    h1_ref, mixed_ref, q_ref, k_ref, v_ref, wo_ref, o_acc, sem, block_sem,
 ):
     seq_len = x_ref.shape[0]
     low = low_half(BLOCK)
@@ -128,7 +129,15 @@
         put(v_ref, 5, jnp.where(low, 0.0, third))
         return carry
 
+    load = pltpu.make_async_copy(wo_hbm, wo_ref, sem.at[3])
+    load.start()
     lax.fori_loop(0, seq_len // BLOCK, project, 0)
+    stores = [
+        pltpu.make_async_copy(source, target, sem.at[i])
+        for i, (source, target) in enumerate(((q_ref, q_hbm), (k_ref, k_hbm), (v_ref, v_hbm)))
+    ]
+    for copy in stores:
+        copy.start()
     lane = lax.broadcasted_iota(jnp.int32, (BLOCK, LANES), 1)
     keep = lax.broadcasted_iota(jnp.int32, (BLOCK, BLOCK), 1) <= lax.broadcasted_iota(
         jnp.int32, (BLOCK, BLOCK), 0
@@ -152,8 +161,8 @@
                 row_max = jnp.max(scores, axis=-1, keepdims=True)
                 exponent = jnp.exp(scores - row_max)
                 total = jnp.sum(exponent, axis=-1, keepdims=True)
-                prob = (exponent * (1.0 / total)).astype(BF)
-                o_acc[j] += nn(prob, v_ref[side, 0:n_keys, :])
+                mixed = nn(exponent.astype(BF), v_ref[side, 0:n_keys, :])
+                o_acc[j] += mixed * (1.0 / total)
                 lse = jnp.where(lane == head, row_max + jnp.log(total), lse)
             return lse
 
@@ -161,7 +170,16 @@
         lse_ref[:, rows] = lse.T[:16]
         mixed = jnp.concatenate([o_acc[j].astype(BF) for j in range(Q_TILES)], axis=1)
         mixed_ref[rows, :] = mixed
+        if b == 0:
+            load.wait()
         h1_ref[rows, :] = x_ref[rows, :].astype(F32) + nn(mixed, wo_ref[...])
+        for i, (source, target) in enumerate(((mixed_ref, mixed_hbm), (h1_ref, h1_hbm))):
+            stores.append(
+                pltpu.make_async_copy(source.at[rows], target.at[rows], block_sem.at[b, i])
+            )
+            stores[-1].start()
+    for copy in stores:
+        copy.wait()
 
 
 def prepare_weights(
@@ -294,7 +312,7 @@
 
 
 def mlp_pass(
-    core_ref, slot_ref, lengths_ref, assignment_ref,
+    core_ref, slot_ref, lengths_ref, assignment_ref, return_ref,
     h1_hbm, cot_hbm, mixed_hbm, gm_ref, wo_hbm, wg_hbm, wu_hbm, wd_hbm,
     out_hbm, dh1_hbm, dm_hbm, ggm_ref, keep_ref, send_ref,
     h1_ref, cot_ref, mixed_ref, wo_ref, wg_ref, wu_ref, wd_ref, out_ref, dh1_ref, dm_ref,
@@ -302,7 +320,7 @@
 ):
     seq_len = h1_ref.shape[0]
     core = core_ref[0]
-    live_len = lengths_ref[assignment_ref[slot_ref[0]]]
+    live_len = lengths_ref[assignment_ref[return_ref[slot_ref[0]]]]
     n_cols = FF // MLP_COLS
     loads = [
         pltpu.make_async_copy(source, target, in_sem.at[i])
@@ -634,6 +652,12 @@
         flat[pl.ds(row + 5 + c, pairs, stride=9), :] = jnp.where(low, odd[c], odd[c + 1])
 
 
+def copy_array(source_ref, target_ref, sem):
+    copy = pltpu.make_async_copy(source_ref, target_ref, sem)
+    copy.start()
+    copy.wait()
+
+
 def update_rule(scale, rate, grad, master, momentum, average):
     weight_grad = grad * scale
     new_momentum = MOMENTUM_DECAY * momentum + weight_grad
@@ -819,12 +843,46 @@
         extra.drain()
 
 
+def lay_out_late(flat, tmp, late_ref):
+    def late(index):
+        return late_ref[index * D : (index + 1) * D, :].astype(F32)
+
+    low1 = low_half(1)
+    gain_a = late_ref[8 * D : 8 * D + 16, :].astype(F32)
+    gain_m = flip(late_ref[8 * D + 16 : 8 * D + 32, :].astype(F32))
+    for r in range(4):
+        flat[r : r + 1, :] = gain_a[r : r + 1]
+    flat[4:5, :] = jnp.where(low1, gain_a[4:5], gain_m[0:1])
+    for r in range(4):
+        flat[5 + r : 6 + r, :] = jnp.where(low1, gain_m[r : r + 1], gain_m[r + 1 : r + 2])
+    put_wide(flat, tmp, [late(t) for t in range(Q_TILES)], D, 9)
+    pairs = D // 2
+    for t in range(3):
+        tmp[pl.ds(t * D, D), :] = late(Q_TILES + t)
+    even = [tmp[pl.ds(i * D, pairs, stride=2), :] for i in range(3)]
+    odd = [tmp[pl.ds(i * D + 1, pairs, stride=2), :] for i in range(3)]
+    low = low_half(pairs)
+    turned = [flip(odd[0]), flip(odd[1]), flip(even[1]), flip(even[2])]
+    rows = (
+        (2601, even[0]),
+        (2602, jnp.where(low, even[1], turned[0])),
+        (2603, jnp.where(low, turned[0], turned[1])),
+        (3465, jnp.where(low, turned[2], turned[3])),
+        (3466, jnp.where(low, turned[3], odd[1])),
+        (3467, odd[2]),
+    )
+    for row, value in rows:
+        flat[pl.ds(row, pairs, stride=3), :] = value
+
+
 def update_second(scale, rate, core_ref, bits_ref, *rest):
-    halves, ins, outs = rest[:8], rest[8:11], rest[15:19]
-    flat, tmp, part_ref, swap_ref, first_ref, in_buf, out_buf, in_sem, out_sem, part_sem = rest[19:29]
+    halves, late_halves, ins, outs = rest[:8], rest[8:10], rest[10:13], rest[17:21]
+    flat, tmp, part_ref, swap_ref, first_ref, in_buf, out_buf, in_sem, out_sem, part_sem = rest[21:31]
     refs = (ins, outs, in_buf, out_buf, in_sem, out_sem)
-    tail = Extra((6916 + 11 * CHUNK) * LANES, ins, outs, rest[29:38])
-    head = Extra(0, ins, outs, rest[38:])
+    tail = Extra((6916 + 11 * CHUNK) * LANES, ins, outs, rest[31:40])
+    head = Extra(0, ins, outs, rest[40:49])
+    late_flat, late_ref, late_in, late_out, late_in_sem, late_out_sem, late_sem = rest[49:56]
+    late_last = Extra(LATE_CHUNKS * CHUNK * LANES, ins, outs, rest[56:])
     rule = functools.partial(update_rule, scale, rate)
     half = PART_ROWS // 2
     pieces = []
@@ -854,10 +912,31 @@
             return flat[pl.ds(pl.multiple_of(FLAT_BASE + start, 8), count), :]
 
         chunks = Chunks(CHUNK // 2, O_ROW, 9, rule, refs)
+        late_refs = (ins, outs, late_in, late_out, late_in_sem, late_out_sem)
+        late_chunks = Chunks(CHUNK, 0, LATE_CHUNKS, rule, late_refs)
+        pieces = [
+            (ref, late_ref.at[pl.ds(i * LATE_HALF, LATE_HALF)]) for i, ref in enumerate(late_halves)
+        ]
         chunks.start()
+        late_parts = load_parts(pieces, late_sem)
+        late_chunks.start()
+        late_last.start()
         for copy in parts:
             copy.wait()
-        chunks.run(stage, gradient)()
+        drain = chunks.run(stage, gradient)
+        for copy in late_parts:
+            copy.wait()
+        lay_out_late(late_flat, tmp, late_ref)
+
+        def late_gradient(c, start, count):
+            return late_flat[pl.ds(pl.multiple_of(c * CHUNK + start, 8), count), :]
+
+        late_drain = late_chunks.run(lambda c: None, late_gradient)
+        start = LATE_CHUNKS * CHUNK
+        late_last.finish(late_flat[start : start + 304, :], rule)
+        drain()
+        late_drain()
+        late_last.drain()
 
     @pl.when(core_ref[0] == 1)
     def _():
@@ -894,65 +973,6 @@
         head.drain()
         drain()
         tail.drain()
-
-
-def update_late(scale, rate, core_ref, own_ref, other_ref, *rest):
-    ins, outs = rest[:3], rest[7:11]
-    flat, tmp, late_ref, in_buf, out_buf, in_sem, out_sem, part_sem = rest[11:19]
-    refs = (ins, outs, in_buf, out_buf, in_sem, out_sem)
-    extra = Extra(LATE_CHUNKS * CHUNK * LANES, ins, outs, rest[19:])
-    rule = functools.partial(update_rule, scale, rate)
-
-    @pl.when(core_ref[0] == 0)
-    def _():
-        chunks = Chunks(CHUNK, 0, LATE_CHUNKS, rule, refs)
-        chunks.start()
-        extra.start()
-        pieces = [
-            (own_ref, late_ref.at[pl.ds(0, LATE_HALF)]),
-            (other_ref, late_ref.at[pl.ds(LATE_HALF, LATE_HALF)]),
-        ]
-        for copy in load_parts(pieces, part_sem):
-            copy.wait()
-
-        def late(index):
-            return late_ref[index * D : (index + 1) * D, :].astype(F32)
-
-        low1 = low_half(1)
-        gain_a = late_ref[8 * D : 8 * D + 16, :].astype(F32)
-        gain_m = flip(late_ref[8 * D + 16 : 8 * D + 32, :].astype(F32))
-        for r in range(4):
-            flat[r : r + 1, :] = gain_a[r : r + 1]
-        flat[4:5, :] = jnp.where(low1, gain_a[4:5], gain_m[0:1])
-        for r in range(4):
-            flat[5 + r : 6 + r, :] = jnp.where(low1, gain_m[r : r + 1], gain_m[r + 1 : r + 2])
-        put_wide(flat, tmp, [late(t) for t in range(Q_TILES)], D, 9)
-        pairs = D // 2
-        for t in range(3):
-            tmp[pl.ds(t * D, D), :] = late(Q_TILES + t)
-        even = [tmp[pl.ds(i * D, pairs, stride=2), :] for i in range(3)]
-        odd = [tmp[pl.ds(i * D + 1, pairs, stride=2), :] for i in range(3)]
-        low = low_half(pairs)
-        turned = [flip(odd[0]), flip(odd[1]), flip(even[1]), flip(even[2])]
-        rows = (
-            (2601, even[0]),
-            (2602, jnp.where(low, even[1], turned[0])),
-            (2603, jnp.where(low, turned[0], turned[1])),
-            (3465, jnp.where(low, turned[2], turned[3])),
-            (3466, jnp.where(low, turned[3], odd[1])),
-            (3467, odd[2]),
-        )
-        for row, value in rows:
-            flat[pl.ds(row, pairs, stride=3), :] = value
-
-        def gradient(c, start, count):
-            return flat[pl.ds(pl.multiple_of(c * CHUNK + start, 8), count), :]
-
-        drain = chunks.run(lambda c: None, gradient)
-        start = LATE_CHUNKS * CHUNK
-        extra.finish(flat[start : start + 304, :], rule)
-        drain()
-        extra.drain()
 
 
 def vmem():
@@ -1037,16 +1057,22 @@
     return call(
         attention_forward,
         outs,
-        [vmem()] * 7,
-        [vmem()] * 6,
-        [pltpu.VMEM((Q_TILES, BLOCK, LANES), F32)],
+        [vmem()] * 4 + [hbm()] + [vmem()] * 2,
+        [hbm()] * 5 + [vmem()],
+        [pltpu.VMEM(shape, kind) for shape, kind in outs[:5]]
+        + [
+            pltpu.VMEM((PAD_D, D), BF),
+            pltpu.VMEM((Q_TILES, BLOCK, LANES), F32),
+            pltpu.SemaphoreType.DMA((4,)),
+            pltpu.SemaphoreType.DMA((seq_len // BLOCK, 2)),
+        ],
         1.5e10,
         "attention_forward",
         56,
     )(x, gain, wq, wkv, wo, cosine, sine)
 
 
-def run_mlp(core, slot, lengths, assignment, hidden1, cot, mixed, gain, wo, wg, wu, wd):
+def run_mlp(core, slot, lengths, assignment, return_order, hidden1, cot, mixed, gain, wo, wg, wu, wd):
     seq_len = hidden1.shape[0]
     outs = [
         ((seq_len, D), BF),
@@ -1059,7 +1085,7 @@
     return call(
         mlp_pass,
         outs,
-        [smem()] * 4 + [hbm()] * 3 + [vmem()] + [hbm()] * 4,
+        [smem()] * 5 + [hbm()] * 3 + [vmem()] + [hbm()] * 4,
         [hbm()] * 3 + [vmem()] + [hbm()] * 2,
         [
             pltpu.VMEM((seq_len, D), F32),
@@ -1086,7 +1112,7 @@
         2.5e10,
         "mlp_pass",
         56,
-    )(core, slot, lengths, assignment, hidden1, cot, mixed, gain, wo, wg, wu, wd)
+    )(core, slot, lengths, assignment, return_order, hidden1, cot, mixed, gain, wo, wg, wu, wd)
 
 
 def run_backward_groups(first, count, q, dm, k, v, lse):
@@ -1192,6 +1218,12 @@
     )(bits, *own, *got)
 
 
+def run_copy(value):
+    outs = [(value.shape, value.dtype)]
+    scratch = [pltpu.SemaphoreType.DMA]
+    return call(copy_array, outs, [hbm()], [hbm()], scratch, 1e6, "copy_array", 4)(value)[0]
+
+
 def chunk_scratch(count):
     return [
         pltpu.VMEM((3 * count * CHUNK * LANES,), F32),
@@ -1226,7 +1258,7 @@
     )(core, bits, *halves, *state)
 
 
-def run_update_second(scale, rate, core, bits, halves, state, done):
+def run_update_second(scale, rate, core, bits, halves, late_halves, state, done):
     scratch = [
         pltpu.VMEM((FLAT_BASE + CHUNK + 8, LANES), F32),
         pltpu.VMEM((Q_TILES * D, LANES), F32),
@@ -1237,41 +1269,23 @@
         pltpu.SemaphoreType.DMA((8,)),
         *extra_scratch(TAIL_ONE, CHUNK + 8),
         *extra_scratch(5 * LANES, 8),
+        pltpu.VMEM((4336, LANES), F32),
+        pltpu.VMEM((2 * LATE_HALF, LANES), BF),
+        *chunk_scratch(LATE_CHUNKS),
+        pltpu.SemaphoreType.DMA((2,)),
+        *extra_scratch((O_ROW - LATE_CHUNKS * CHUNK) * LANES, 304),
     ]
     return call(
         functools.partial(update_second, scale, rate),
         [(state[0].shape, F32)] * 4,
-        [smem()] * 2 + [hbm()] * 15,
+        [smem()] * 2 + [hbm()] * 17,
         [hbm()] * 4,
         scratch,
         1e9,
         "update_second",
         56,
-        {13 + i: i for i in range(4)},
-    )(core, bits, *halves, *state, *done)
-
-
-def run_update_late(scale, rate, core, own, other, state, done):
-    last_rows = O_ROW - LATE_CHUNKS * CHUNK
-    scratch = [
-        pltpu.VMEM((4336, LANES), F32),
-        pltpu.VMEM((Q_TILES * D, LANES), F32),
-        pltpu.VMEM((2 * LATE_HALF, LANES), BF),
-        *chunk_scratch(LATE_CHUNKS),
-        pltpu.SemaphoreType.DMA((2,)),
-        *extra_scratch(last_rows * LANES, 304),
-    ]
-    return call(
-        functools.partial(update_late, scale, rate),
-        [(state[0].shape, F32)] * 4,
-        [smem()] + [hbm()] * 9,
-        [hbm()] * 4,
-        scratch,
-        1e9,
-        "update_late",
-        56,
-        {6 + i: i for i in range(4)},
-    )(core, own, other, *state, *done)
+        {15 + i: i for i in range(4)},
+    )(core, bits, *halves, *late_halves, *state, *done)
 
 
 def add_low(a, b):
@@ -1326,8 +1340,8 @@
     core_arr = core.astype(jnp.int32).reshape(1)
 
     seq_ids = jnp.arange(nseq_all, dtype=jnp.int32)
-    inverse = jnp.sum(
-        jnp.where(return_order[None, :] == seq_ids[:, None], seq_ids[None, :], 0), axis=1
+    sequence = jnp.sum(
+        jnp.where(return_order[:, None] == seq_ids[None, :], assignment[None, :], 0), axis=1
     )
 
     def pick(array, index):
@@ -1336,18 +1350,18 @@
     def exchange(value):
         return lax.all_to_all(value, axes, split_axis=0, concat_axis=0, tiled=True)
 
-    x = exchange(pick(inputs, assignment)).reshape(seq_len, D)
+    x = exchange(pick(inputs, sequence)).reshape(seq_len, D)
     slot_arr = my_slot.astype(jnp.int32).reshape(1)
 
     other = lax.ppermute(master, "shard", [(0, 1), (1, 0)])
     gain_attn, gain_mlp, wq, wkv, wo, wg, wu, wd = run_prepare(core_arr, master, other)
 
     cosine, sine = rope_tables(seq_len)
-    sent_cot, gain_attn, cosine = tie(pick(cotangent, inverse), gain_attn, cosine)
+    sent_cot, gain_attn, cosine = tie(cotangent, gain_attn, cosine)
     cot = exchange(sent_cot).reshape(seq_len, D)
     hidden1, mixed, q, k, v, lse = run_attention_forward(x, gain_attn, wq, wkv, wo, cosine, sine)
     result, dh1, dm, ggm, early_keep, early_send = run_mlp(
-        core_arr, slot_arr, lengths, assignment, hidden1, cot, mixed, gain_mlp, wo, wg, wu, wd
+        core_arr, slot_arr, lengths, assignment, return_order, hidden1, cot, mixed, gain_mlp, wo, wg, wu, wd
     )
     back_out = exchange(result.reshape(nseq_all, block_rows, D))
 
@@ -1384,33 +1398,28 @@
     got = [xor_swap(sent[0], last_bit)]
     late_got = lax.ppermute(late_send, "shard", [(0, 1), (1, 0)])
     late, _ = run_sum(my_bits(orders, 0)[:1], [late_keep], [late_got], False)
-    late, block_output, *got = tie(scatter_sum(late[0]), pick(back_out, return_order), *got)
+    late, block_output, *got = tie(late[0], run_copy(back_out), *got)
     early, _ = run_sum(my_bits(orders, last_bit)[:1], kept, got, False)
+    late = scatter_sum(late)
+    got = xor_swap(early[0], last_bit)
+    late, got = tie(late, got)
+    early = run_join(my_bits(orders, last_bit), early, [got], 3)
     far_bits = list(range(near_size().bit_length() - 1, n_bits))
 
     def add_far(late, early):
         late, *early = tie(late, *early)
         return add_low(late, xor_swap(late, far_bits.pop(0))), early
 
-    got = xor_swap(early[0], last_bit)
-    late = add_low(late, xor_swap(late, far_bits.pop(0)))
-    late, got = tie(late, got)
-    early = run_join(my_bits(orders, last_bit), early, [got], 3)
-    whole = None
     for step in reversed(range(1, last_bit)):
         if far_bits:
             late, early = add_far(late, early)
-        elif whole is None:
-            late, *early = tie(late, *early)
-            whole = spread(jnp.broadcast_to(late[None], (near_size(), *late.shape)))
         got = swap_parts(early, step)
         late, *got = tie(late, *got)
         early = run_join(my_bits(orders, step), early, got, 3)
     while far_bits:
         late, early = add_far(late, early)
-    if whole is None:
-        whole = spread(jnp.broadcast_to(late[None], (near_size(), *late.shape)))
-    late = whole.reshape(-1, LANES)
+    late, *early = tie(late, *early)
+    late = spread(jnp.broadcast_to(late[None], (near_size(), *late.shape))).reshape(-1, LANES)
     got = swap_parts(early, 0)
     swap_own = lax.ppermute(early[2], "shard", [(0, 1)])
     bits = my_bits(orders, 0)
@@ -1423,12 +1432,10 @@
     swap_got = lax.ppermute(got[2], "shard", [(0, 1)])
     halves = [early[0], got[0], early[1], got[1], early[2], got[2], swap_own, swap_got]
     done = run_update_first(scale, rate, core_arr, bits, halves[:4], state)
-    done = run_update_second(scale, rate, core_arr, bits, halves, state, done)
-    weight_grad, new_momentum, new_master, new_average = run_update_late(
-        scale, rate, core_arr, late, late_other, state, done
+    weight_grad, new_momentum, new_master, new_average = run_update_second(
+        scale, rate, core_arr, bits, halves, (late, late_other), state, done
     )
-    input_grad = pick(back_grad, return_order)
-    return (block_output, input_grad, weight_grad, new_momentum, new_master, new_average)
+    return (block_output, back_grad, weight_grad, new_momentum, new_master, new_average)
 
 
 def solution(mesh):

time: 266 us -> 262 us (0.985)
  waiting for transfers between devices: 41.3 us -> 49.5 us
  local copies, waits for them, and re-layouts: 14.2 us -> 7.54 us
    gather x4 -> x1, local copies, waits for them, and re-layouts: 8.86 us -> 1.61 us  [pick(): return array.at[index].get(mode='promise_in_bounds')]
    all_to_all x4, waiting for transfers between devices: 8.39 us -> 15.6 us  [exchange(): return lax.all_to_all(value, axes, split_axis=0, concat_axis=0, tiled=True)]
    pallas_call x3, Pallas kernels: 50.4 us -> 47.1 us  [the longest x1 28.5 us: run_mlp(): call(mlp_pass, outs, [smem()] * 5 + [hbm()] * 3 + [vmem()] + [hbm()] * 4,...]
    all_to_all x1, waiting for transfers between devices: 5.01 us -> 8.3 us  [spread(): lax.all_to_all(blocks, 'dp', split_axis=0, concat_axis=0, tiled=True, axi...]
    unnamed x34 -> x33, local copies, waits for them, and re-layouts: 5.21 us -> 5.85 us
  transfers between devices with their start and end apart: 33 -> 33, of which waited for: 13 -> 12; matrix products, arithmetic and copies ran while one was open for 4% -> 2% of each run, Pallas kernels for 36% -> 36%
where the time goes in v2:
time: 262 us; the launch traced here: 261 us
  Pallas kernels  128 us (49%)
  starting transfers between devices  55.2 us (21%)
  waiting for transfers between devices  49.5 us (19%)
  blocking collectives  15.9 us (6%)
  local copies, waits for them, and re-layouts  7.54 us (3%)
  other arithmetic  3.66 us (1%)
    pallas_call x1, Pallas kernels, run_mlp(): call(mlp_pass, outs, [smem()] * 5 + [hbm()] * 3 + [vmem()] + [hbm()] * 4,...  28.5 us
    ppermute x22, waiting for transfers between devices, xor_swap(): return lax.ppermute(value, 'dp', [(i, i ^ 1 << bit) for i in range(size)])  25.4 us
    all_to_all x4, starting transfers between devices, exchange(): return lax.all_to_all(value, axes, split_axis=0, concat_axis=0, tiled=True)  23 us
    pallas_call x2, Pallas kernels, run_backward_groups(): pl.pallas_call(functools.partial(backward_groups, first), grid=(count,),...  20.2 us
    ppermute x22, starting transfers between devices, xor_swap(): return lax.ppermute(value, 'dp', [(i, i ^ 1 << bit) for i in range(size)])  19.8 us
    pallas_call x1, Pallas kernels, run_attention_forward(): call(attention_forward, outs, [vmem()] * 4 + [hbm()] + [vmem()] * 2, [hbm...  17.6 us
    all_to_all x1, blocking collectives, spread(): lax.all_to_all(blocks, 'dp', split_axis=0, concat_axis=0, tiled=True, axi...  15.9 us
    all_to_all x4, waiting for transfers between devices, exchange(): return lax.all_to_all(value, axes, split_axis=0, concat_axis=0, tiled=True)  15.6 us
  transfers between devices with their start and end apart: 33, of which 12 were waited for; matrix products, arithmetic and copies ran while one was open for 2% of the time, Pallas kernels for 36%

profile of v2, /device:TPU:1, one launch (start us, length us, event | category | flops | bytes accessed | tf_op | source)
XLA Modules:
  0.0 261.1 jit_solution(3523704837705013858)
XLA Ops:
  3.5 7.1 %all-to-all-start = ((bf16[32,24,576]{2,1,0:T(8,128)(2,1)}), bf16[32,24,576]{2,1,0:T(8,128)(2,1)S(1)}, u32[]{:S(2)}, u32[]{:S(2)}) async-start(bf16[32,24,576]{2,1,0:T(8,128)(2,1)} %gather_fusion), calls=%async_computation | async-start | bytes 1966080 | tf_op jit(solution)/shard_map/all_to_all | solution.py:1351
  12.9 12.3 %prepare_weights.1 = (f32[1,576]{1,0:T(1,128)}, f32[1,576]{1,0:T(1,128)}, bf16[576,640]{1,0:T(8,128)(2,1)}, bf16[576,384]{1,0:T(8,128)(2,1)}, bf16[640,576]{1,0:...) custom-call(s32[1]{0:T(128)} %bitcast.1.core_ref, ...), custom_call_target="tpu_custom_call" | custom-call | flops 10000000000 | bytes 14459904 | tf_op jit(solution)/shard_map/prepare_weights/pallas_call | solution.py:1035
  25.2 9.3 %all-to-all-done = bf16[32,24,576]{2,1,0:T(8,128)(2,1)S(1)} async-done(((bf16[32,24,576]{2,1,0:T(8,128)(2,1)}), bf16[32,24,576]{2,1,0:T(8,128)(2,1)S(1)}, u32[]{:S(2)}, u32[]{:S(2)}) %all-to-all-start) | async-done | bytes 884768 | tf_op jit(solution)/shard_map/all_to_all | solution.py:1351
  34.5 4.5 %all-to-all-start.1 = ((bf16[32,24,576]{2,1,0:T(8,128)(2,1)}), bf16[32,24,576]{2,1,0:T(8,128)(2,1)S(1)}, u32[]{:S(2)}, u32[]{:S(2)}) async-start(bf16[32,24,576]{2,1,0:T(8,128)(2,1)} %param.9), calls=%async_computation.1 | async-start | bytes 1966080 | tf_op jit(solution)/shard_map/all_to_all | solution.py:1351
  39.1 17.6 %attention_forward.1 = (f32[768,576]{1,0:T(8,128)}, bf16[768,640]{1,0:T(8,128)(2,1)}, bf16[5,768,128]{2,1,0:T(8,128)(2,1)}, bf16[6,768,128]{2,1,0:T(8,128)(2,1)}...) custom-call(bf16[768,576]{1,0:T(8,128)(2,1)} %bitcast.19, f32[1,576]{1,0:T(1,128)} %get-tuple-element.132.ga_ref, ...), custom_call_target="tpu_custom_call" | custom-call | flops 15000000512 | bytes 12288000 | tf_op jit(solution)/shard_map/attention_forward/pallas_call | solution.py:1057
  56.7 6.2 %all-to-all-done.1 = bf16[32,24,576]{2,1,0:T(8,128)(2,1)S(1)} async-done(((bf16[32,24,576]{2,1,0:T(8,128)(2,1)}), bf16[32,24,576]{2,1,0:T(8,128)(2,1)S(1)}, u32[]{:S(2)}, u32[]{:S(2)}) %all-to-all-start.1) | async-done | bytes 884768 | tf_op jit(solution)/shard_map/all_to_all | solution.py:1351
  64.0 28.5 %mlp_pass.1 = (bf16[768,576]{1,0:T(8,128)(2,1)}, f32[768,576]{1,0:T(8,128)}, bf16[5,768,128]{2,1,0:T(8,128)(2,1)}, f32[1,576]{1,0:T(1,128)}, bf16[12288,128]{1,0:T(8,128)(2,1)}, /*index=5*/bf16[12288,128]{1,0:T(8,128)(2,1)}) custom-call(s32[1]{0:T(128)} %bitcast.1.core_ref, s32[1]{0:T(128)} %bitcast.5.slot_ref, s32[32]{0:T(128)} %lengths_ref.1, ...), custom_call_target="tpu_custom_call" | custom-call | flops 24999999488 | bytes 19862016 | tf_op jit(solution)/shard_map/mlp_pass/pallas_call | solution.py:1085
  93.9 3.5 %all-to-all-start.2 = ((bf16[32,24,576]{2,1,0:T(8,128)(2,1)}), bf16[32,24,576]{2,1,0:T(8,128)(2,1)S(1)}, u32[]{:S(2)}, u32[]{:S(2)}) async-start(bf16[32,24,576]{2,1,0:T(8,128)(2,1)} %bitcast.21), calls=%async_computation.2 | async-start | bytes 1966080 | tf_op jit(solution)/shard_map/all_to_all | solution.py:1351
  97.4 7.6 %backward_groups.2 = (f32[1,2,768,128]{3,2,1,0:T(8,128)}, f32[1,768,128]{2,1,0:T(8,128)}, f32[1,768,128]{2,1,0:T(8,128)}) custom-call(bf16[5,768,128]{2,1,0:T(8,128)(2,1)} %get-tuple-element.164.q_ref, bf16[5,768,128]{2,1,0:T(8,128)(2,1)} %get-tuple-element.165.dm_ref, bf16[6,768,128]{2,1,0:T(8,128)(2,1)} %get-tuple-element.166.k_ref, ...), custom_call_target="tpu_custom_call" | custom-call | flops 8000000000 | bytes 3000000 | tf_op jit(solution)/shard_map/backward_groups/pallas_call | solution.py:1124
  105.0 2.9 %gather_sum.6 = (bf16[2048,128]{1,0:T(8,128)(2,1)S(1)}, bf16[2048,128]{1,0:T(8,128)(2,1)S(1)}, bf16[2048,128]{1,0:T(8,128)(2,1)S(1)}, bf16[2048,128]{1,0:T(8,128...) custom-call(s32[3]{0:T(128)S(1)} %pad_add_fusion.1.bits_ref, bf16[12288,128]{1,0:T(8,128)(2,1)S(1)} %copy-done.2, ...), custom_call_target="tpu_custom_call" | custom-call | flops 1000000 | bytes 6291456 | tf_op jit(solution)/shard_map/gather_sum/pallas_call | solution.py:1191
  111.8 12.6 %backward_groups.3 = (f32[2,2,768,128]{3,2,1,0:T(8,128)}, f32[2,768,128]{2,1,0:T(8,128)}, f32[2,768,128]{2,1,0:T(8,128)}) custom-call(bf16[5,768,128]{2,1,0:T(8,128)(2,1)} %get-tuple-element.164.q_ref, bf16[5,768,128]{2,1,0:T(8,128)(2,1)} %get-tuple-element.165.dm_ref, bf16[6,768,128]{2,1,0:T(8,128)(2,1)} %get-tuple-element.166.k_ref, ...), custom_call_target="tpu_custom_call" | custom-call | flops 16000000000 | bytes 6000000 | tf_op jit(solution)/shard_map/backward_groups/pallas_call | solution.py:1124
  131.1 8.7 %backward_finish.1 = (bf16[768,576]{1,0:T(8,128)(2,1)}, bf16[768,640]{1,0:T(8,128)(2,1)}, bf16[768,384]{1,0:T(8,128)(2,1)}, bf16[768,576]{1,0:T(8,128)(2,1)}, f32[1,576]{1,0:T(1,128)}) custom-call(bf16[768,576]{1,0:T(8,128)(2,1)} %bitcast.20, f32[1,576]{1,0:T(1,128)} %get-tuple-element.132.ga_ref, f32[768,576]{1,0:T(8,128)} %get-tuple-element.163.dh1_ref, ...), custom_call_target="tpu_custom_call" | custom-call | flops 4000000000 | bytes 6689280 | tf_op jit(solution)/shard_map/backward_finish/pallas_call | solution.py:1158
  144.5 4.1 %late_weights.1 = (bf16[2432,128]{1,0:T(8,128)(2,1)}, bf16[2432,128]{1,0:T(8,128)(2,1)}) custom-call(s32[1]{0:T(128)} %bitcast.1.core_ref, bf16[768,576]{1,0:T(8,128)(2,1)} %get-tuple-element.175.nm_s, bf16[768,640]{1,0:T(8,128)(2,1)} %get-tuple-element.176.dq_s, bf16[768,384]{1,0:T(8,128)(2,1)} %get-tuple-element.177.dkv_s, ...), custom_call_target="tpu_custom_call" | custom-call | flops 4000000000 | bytes 2490368 | tf_op jit(solution)/shard_map/late_weights/pallas_call | solution.py:1172
  149.8 2.8 %collective-permute-start.11 = (bf16[2432,128]{1,0:T(8,128)(2,1)}, bf16[2432,128]{1,0:T(8,128)(2,1)S(1)}, u32[]{:S(2)}, u32[]{:S(2)}) collective-permute-start(bf16[2432,128]{1,0:T(8,128)(2,1)} %get-tuple-element.203), channel_id=1, source_target_pairs={{0,1},{1,0},{2,3},{3,2},{4,5},{5,4},{6,7},{7,6},{8,9},{9,8},{10,11... | collective-permute-start | bytes 1867784 | tf_op jit(solution)/shard_map/ppermute | solution.py:1399
  156.6 7.7 %collective-permute-done.12.refs_1_ = bf16[768,128]{1,0:T(8,128)(2,1)S(1)} collective-permute-done((bf16[768,128]{1,0:T(8,128)(2,1)S(1)}, bf16[768,128]{1,0:T(8,128)(2,1)S(1)}, u32[]{:S(2)}, u32[]{:S(2)}) %collective-permute-start.12) | collective-permute-done | bytes 196640 | tf_op jit(solution)/shard_map/ppermute | solution.py:1297
  164.4 3.5 %all-to-all-start.3 = ((bf16[4,608,128]{2,1,0:T(8,128)(2,1)}), bf16[4,608,128]{2,1,0:T(8,128)(2,1)S(1)}, u32[]{:S(2)}, u32[]{:S(2)}) async-start(bf16[4,608,128]{2,1,0:T(8,128)(2,1)} %bitcast.10), calls=%async_computation.3 | async-start | bytes 1245184 | tf_op jit(solution)/shard_map/all_to_all | solution.py:1316
  168.2 8.3 %all-to-all-done.3 = bf16[4,608,128]{2,1,0:T(8,128)(2,1)S(1)} async-done(((bf16[4,608,128]{2,1,0:T(8,128)(2,1)}), bf16[4,608,128]{2,1,0:T(8,128)(2,1)S(1)}, u32[]{:S(2)}, u32[]{:S(2)}) %all-to-all-start.3) | async-done | bytes 622624 | tf_op jit(solution)/shard_map/all_to_all | solution.py:1316
  176.7 3.1 %collective-permute-done.13.refs_1_ = bf16[768,128]{1,0:T(8,128)(2,1)S(1)} collective-permute-done((bf16[768,128]{1,0:T(8,128)(2,1)S(1)}, bf16[768,128]{1,0:T(8,128)(2,1)S(1)}, u32[]{:S(2)}, u32[]{:S(2)}) %collective-permute-start.13) | collective-permute-done | bytes 196640 | tf_op jit(solution)/shard_map/ppermute | solution.py:1297
  186.1 2.8 %collective-permute-done.15.refs_3_ = bf16[512,128]{1,0:T(8,128)(2,1)S(1)} collective-permute-done((bf16[512,128]{1,0:T(8,128)(2,1)S(1)}, bf16[512,128]{1,0:T(8,128)(2,1)S(1)}, u32[]{:S(2)}, u32[]{:S(2)}) %collective-permute-start.15) | collective-permute-done | bytes 131104 | tf_op jit(solution)/shard_map/ppermute | solution.py:1297
  194.8 5.9 %collective-permute-done.18 = bf16[608,128]{1,0:T(8,128)(2,1)S(1)} collective-permute-done((bf16[608,128]{1,0:T(8,128)(2,1)S(1)}, bf16[608,128]{1,0:T(8,128)(2,1)S(1)}, u32[]{:S(2)}, u32[]{:S(2)}) %collective-permute-start.18) | collective-permute-done | bytes 155680 | tf_op jit(solution)/shard_map/ppermute | solution.py:1297
  206.1 15.9 %all_to_all.30 = bf16[4,608,128]{2,1,0:T(8,128)(2,1)S(1)} all-to-all(bf16[4,608,128]{2,1,0:T(8,128)(2,1)S(1)} %broadcast_in_dim.37), channel_id=1, replica_groups={{0,2,4,6},{8,10,12,14},{16,18,20,22},{24,26,28,30},{1,3,5,7},{9,11,13,1..., dimensions={0} | all-to-all | bytes 1245184 | tf_op jit(solution)/shard_map/all_to_all | solution.py:1316
  223.7 7.9 %all-to-all-start.5 = ((bf16[32,24,576]{2,1,0:T(8,128)(2,1)}), bf16[32,24,576]{2,1,0:T(8,128)(2,1)S(1)}, u32[]{:S(2)}, u32[]{:S(2)}) async-start(bf16[32,24,576]{2,1,0:T(8,128)(2,1)} %bitcast.18), calls=%async_computation.5 | async-start | bytes 1966080 | tf_op jit(solution)/shard_map/all_to_all | solution.py:1351
  235.1 11.2 %update_first.1 = (f32[1770048]{0:T(1024)}, f32[1770048]{0:T(1024)}, f32[1770048]{0:T(1024)}, f32[1770048]{0:T(1024)}) custom-call(s32[1]{0:T(128)} %bitcast.1.core_ref, s32[3]{0:T(128)} %copy-done.7, bf16[2048,128]{1,0:T(8,128)(2,1)} %copy-done.3, bf16[2048,128]{1,0:T(8,128)(2,1)} %copy-done.9, bf16[2048,128]{1,0:T(8,128)(2,1)} %copy-done.4, ...), custom_call_target="tpu_custom_call" | custom-call | flops 1000000000 | bytes 56641536 | tf_op jit(solution)/shard_map/update_first/pallas_call | solution.py:1249
  247.3 12.8 %update_second.1 = (f32[1770048]{0:T(1024)}, f32[1770048]{0:T(1024)}, f32[1770048]{0:T(1024)}, f32[1770048]{0:T(1024)}) custom-call(s32[1]{0:T(128)} %bitcast.1.core_ref, s32[3]{0:T(128)} %copy-done.7, bf16[2048,128]{1,0:T(8,128)(2,1)} %copy-done.3, ...), custom_call_target="tpu_custom_call", output_to_operand_aliasing={{0}: (15, {}), {1}: (16, {}), {2}: (17, {}), {3}: (18, {})} | custom-call | flops 1000000000 | bytes 56641536 | tf_op jit(solution)/shard_map/update_second/pallas_call | solution.py:1278
  (109 shorter events, 53.2 us)
Async XLA Ops:
  0.6 12.3 %collective-permute-start = (f32[1770048]{0:T(1024)}, f32[1770048]{0:T(1024)}, u32[]{:S(2)}, u32[]{:S(2)}) collective-permute-start(f32[1770048]{0:T(1024)} %rest_10_.1), channel_id=1, source_target_pairs={{0,1},{1,0},{2,3},{3,2},{4,5},{5,4},{6,7},{7,6},{8,9},{9,8},{10,11... | collective-permute-start | bytes 21240584 | tf_op jit(solution)/shard_map/ppermute | solution.py:1356
  3.5 31.0 %all-to-all-start = ((bf16[32,24,576]{2,1,0:T(8,128)(2,1)}), bf16[32,24,576]{2,1,0:T(8,128)(2,1)S(1)}, u32[]{:S(2)}, u32[]{:S(2)}) async-start(bf16[32,24,576]{2,1,0:T(8,128)(2,1)} %gather_fusion), calls=%async_computation | async-start | bytes 1966080 | tf_op jit(solution)/shard_map/all_to_all | solution.py:1351
  34.5 28.5 %all-to-all-start.1 = ((bf16[32,24,576]{2,1,0:T(8,128)(2,1)}), bf16[32,24,576]{2,1,0:T(8,128)(2,1)S(1)}, u32[]{:S(2)}, u32[]{:S(2)}) async-start(bf16[32,24,576]{2,1,0:T(8,128)(2,1)} %param.9), calls=%async_computation.1 | async-start | bytes 1966080 | tf_op jit(solution)/shard_map/all_to_all | solution.py:1351
  92.5 12.6 %collective-permute-start.1 = (bf16[12288,128]{1,0:T(8,128)(2,1)}, bf16[12288,128]{1,0:T(8,128)(2,1)}, u32[]{:S(2)}, u32[]{:S(2)}) collective-permute-start(bf16[12288,128]{1,0:T(8,128)(2,1)} %get-tuple-element.147), channel_id=1, source_target_pairs={{0,1},{1,0},{2,3},{3,2},{4,5},{5,4},{6,7},{7,6},{8,9},{9,8},{10,11... | collective-permute-start | bytes 9437192 | tf_op jit(solution)/shard_map/ppermute | solution.py:1374
  93.9 35.1 %all-to-all-start.2 = ((bf16[32,24,576]{2,1,0:T(8,128)(2,1)}), bf16[32,24,576]{2,1,0:T(8,128)(2,1)S(1)}, u32[]{:S(2)}, u32[]{:S(2)}) async-start(bf16[32,24,576]{2,1,0:T(8,128)(2,1)} %bitcast.21), calls=%async_computation.2 | async-start | bytes 1966080 | tf_op jit(solution)/shard_map/all_to_all | solution.py:1351
  108.0 16.4 %collective-permute-start.2 = (bf16[2048,128]{1,0:T(8,128)(2,1)S(1)}, bf16[2048,128]{1,0:T(8,128)(2,1)S(1)}, u32[]{:S(2)}, u32[]{:S(2)}) collective-permute-start(bf16[2048,128]{1,0:T(8,128)(2,1)S(1)} %get-tuple-element.157), channel_id=1, source_target_pairs={{0,2},{2,0},{4,6},{6,4},{8,10},{10,8},{12,14},{14,12},{16,18},{18,... | collective-permute-start | bytes 1572872 | tf_op jit(solution)/shard_map/ppermute | solution.py:1297
  109.4 16.4 %collective-permute-start.3 = (bf16[2048,128]{1,0:T(8,128)(2,1)S(1)}, bf16[2048,128]{1,0:T(8,128)(2,1)S(1)}, u32[]{:S(2)}, u32[]{:S(2)}) collective-permute-start(bf16[2048,128]{1,0:T(8,128)(2,1)S(1)} %get-tuple-element.158), channel_id=1, source_target_pairs={{0,4},{2,6},{4,0},{6,2},{8,12},{10,14},{12,8},{14,10},{16,20},{18,... | collective-permute-start | bytes 1572872 | tf_op jit(solution)/shard_map/ppermute | solution.py:1297
  110.6 17.3 %collective-permute-start.4 = (bf16[2048,128]{1,0:T(8,128)(2,1)S(1)}, bf16[2048,128]{1,0:T(8,128)(2,1)S(1)}, u32[]{:S(2)}, u32[]{:S(2)}) collective-permute-start(bf16[2048,128]{1,0:T(8,128)(2,1)S(1)} %get-tuple-element.159), channel_id=1, source_target_pairs={{0,8},{2,10},{4,12},{6,14},{8,0},{10,2},{12,4},{14,6},{16,24},{18,... | collective-permute-start | bytes 1572872 | tf_op jit(solution)/shard_map/ppermute | solution.py:1297
  129.1 10.7 %collective-permute-start.5 = (bf16[1024,128]{1,0:T(8,128)(2,1)S(1)}, bf16[1024,128]{1,0:T(8,128)(2,1)S(1)}, u32[]{:S(2)}, u32[]{:S(2)}) collective-permute-start(bf16[1024,128]{1,0:T(8,128)(2,1)S(1)} %get-tuple-element.182), channel_id=1, source_target_pairs={{0,4},{2,6},{4,0},{6,2},{8,12},{10,14},{12,8},{14,10},{16,20},{18,... | collective-permute-start | bytes 786440 | tf_op jit(solution)/shard_map/ppermute | solution.py:1297
  129.9 9.8 %collective-permute-start.6 = (bf16[1024,128]{1,0:T(8,128)(2,1)S(1)}, bf16[1024,128]{1,0:T(8,128)(2,1)S(1)}, u32[]{:S(2)}, u32[]{:S(2)}) collective-permute-start(bf16[1024,128]{1,0:T(8,128)(2,1)S(1)} %get-tuple-element.183), channel_id=1, source_target_pairs={{0,8},{2,10},{4,12},{6,14},{8,0},{10,2},{12,4},{14,6},{16,24},{18,... | collective-permute-start | bytes 786440 | tf_op jit(solution)/shard_map/ppermute | solution.py:1297
  130.0 9.8 %collective-permute-start.7 = (bf16[1024,128]{1,0:T(8,128)(2,1)S(1)}, bf16[1024,128]{1,0:T(8,128)(2,1)S(1)}, u32[]{:S(2)}, u32[]{:S(2)}) collective-permute-start(bf16[1024,128]{1,0:T(8,128)(2,1)S(1)} %get-tuple-element.184), channel_id=1, source_target_pairs={{0,2},{2,0},{4,6},{6,4},{8,10},{10,8},{12,14},{14,12},{16,18},{18,... | collective-permute-start | bytes 786440 | tf_op jit(solution)/shard_map/ppermute | solution.py:1297
  152.6 11.7 %collective-permute-start.12 = (bf16[768,128]{1,0:T(8,128)(2,1)S(1)}, bf16[768,128]{1,0:T(8,128)(2,1)S(1)}, u32[]{:S(2)}, u32[]{:S(2)}) collective-permute-start(bf16[768,128]{1,0:T(8,128)(2,1)S(1)} %get-tuple-element.205), channel_id=1, source_target_pairs={{0,16},{2,18},{4,20},{6,22},{8,24},{10,26},{12,28},{14,30},{16,0},... | collective-permute-start | bytes 589832 | tf_op jit(solution)/shard_map/ppermute | solution.py:1297
  164.4 12.2 %all-to-all-start.3 = ((bf16[4,608,128]{2,1,0:T(8,128)(2,1)}), bf16[4,608,128]{2,1,0:T(8,128)(2,1)S(1)}, u32[]{:S(2)}, u32[]{:S(2)}) async-start(bf16[4,608,128]{2,1,0:T(8,128)(2,1)} %bitcast.10), calls=%async_computation.3 | async-start | bytes 1245184 | tf_op jit(solution)/shard_map/all_to_all | solution.py:1316
  168.2 11.5 %collective-permute-start.13 = (bf16[768,128]{1,0:T(8,128)(2,1)S(1)}, bf16[768,128]{1,0:T(8,128)(2,1)S(1)}, u32[]{:S(2)}, u32[]{:S(2)}) collective-permute-start(bf16[768,128]{1,0:T(8,128)(2,1)S(1)} %gather_sum.11.refs_0_), channel_id=1, source_target_pairs={{0,16},{2,18},{4,20},{6,22},{8,24},{10,26},{12,28},{14,30},{16,0},... | collective-permute-start | bytes 589832 | tf_op jit(solution)/shard_map/ppermute | solution.py:1297
  190.5 10.2 %collective-permute-start.18 = (bf16[608,128]{1,0:T(8,128)(2,1)S(1)}, bf16[608,128]{1,0:T(8,128)(2,1)S(1)}, u32[]{:S(2)}, u32[]{:S(2)}) collective-permute-start(bf16[608,128]{1,0:T(8,128)(2,1)S(1)} %add_convert_fusion.1), channel_id=1, source_target_pairs={{0,16},{2,18},{4,20},{6,22},{8,24},{10,26},{12,28},{14,30},{16,0},... | collective-permute-start | bytes 466952 | tf_op jit(solution)/shard_map/ppermute | solution.py:1297
  191.1 9.7 %collective-permute-start.19 = (bf16[1024,128]{1,0:T(8,128)(2,1)S(1)}, bf16[1024,128]{1,0:T(8,128)(2,1)S(1)}, u32[]{:S(2)}, u32[]{:S(2)}) collective-permute-start(bf16[1024,128]{1,0:T(8,128)(2,1)S(1)} %get-tuple-element.228.refs_0_), channel_id=1, source_target_pairs={{0,4},{2,6},{4,0},{6,2},{8,12},{10,14},{12,8},{14,10},{16,20},{18,... | collective-permute-start | bytes 786440 | tf_op jit(solution)/shard_map/ppermute | solution.py:1297
  192.5 9.6 %collective-permute-start.20 = (bf16[1024,128]{1,0:T(8,128)(2,1)S(1)}, bf16[1024,128]{1,0:T(8,128)(2,1)S(1)}, u32[]{:S(2)}, u32[]{:S(2)}) collective-permute-start(bf16[1024,128]{1,0:T(8,128)(2,1)S(1)} %get-tuple-element.229.refs_1_), channel_id=1, source_target_pairs={{0,8},{2,10},{4,12},{6,14},{8,0},{10,2},{12,4},{14,6},{16,24},{18,... | collective-permute-start | bytes 786440 | tf_op jit(solution)/shard_map/ppermute | solution.py:1297
  202.8 19.2 %collective-permute-start.25 = (bf16[2048,128]{1,0:T(8,128)(2,1)S(1)}, bf16[2048,128]{1,0:T(8,128)(2,1)}, u32[]{:S(2)}, u32[]{:S(2)}) collective-permute-start(bf16[2048,128]{1,0:T(8,128)(2,1)S(1)} %get-tuple-element.239.rest_4_), channel_id=1, source_target_pairs={{0,8},{2,10},{4,12},{6,14},{8,0},{10,2},{12,4},{14,6},{16,24},{18,... | collective-permute-start | bytes 1572872 | tf_op jit(solution)/shard_map/ppermute | solution.py:1297
  202.9 19.1 %collective-permute-start.22 = (bf16[2048,128]{1,0:T(8,128)(2,1)S(1)}, bf16[2048,128]{1,0:T(8,128)(2,1)S(1)}, u32[]{:S(2)}, u32[]{:S(2)}) collective-permute-start(bf16[2048,128]{1,0:T(8,128)(2,1)S(1)} %get-tuple-element.239.rest_4_), channel_id=1, source_target_pairs={{0,1},{2,3},{4,5},{6,7},{8,9},{10,11},{12,13},{14,15},{16,17},{18,... | collective-permute-start | bytes 1572872 | tf_op jit(solution)/shard_map/ppermute | solution.py:1424
  204.2 17.8 %collective-permute-start.23 = (bf16[2048,128]{1,0:T(8,128)(2,1)S(1)}, bf16[2048,128]{1,0:T(8,128)(2,1)S(1)}, u32[]{:S(2)}, u32[]{:S(2)}) collective-permute-start(bf16[2048,128]{1,0:T(8,128)(2,1)S(1)} %get-tuple-element.240.rest_0_), channel_id=1, source_target_pairs={{0,2},{2,0},{4,6},{6,4},{8,10},{10,8},{12,14},{14,12},{16,18},{18,... | collective-permute-start | bytes 1572872 | tf_op jit(solution)/shard_map/ppermute | solution.py:1297
  205.5 16.6 %collective-permute-start.24 = (bf16[2048,128]{1,0:T(8,128)(2,1)S(1)}, bf16[2048,128]{1,0:T(8,128)(2,1)S(1)}, u32[]{:S(2)}, u32[]{:S(2)}) collective-permute-start(bf16[2048,128]{1,0:T(8,128)(2,1)S(1)} %get-tuple-element.241.rest_2_), channel_id=1, source_target_pairs={{0,4},{2,6},{4,0},{6,2},{8,12},{10,14},{12,8},{14,10},{16,20},{18,... | collective-permute-start | bytes 1572872 | tf_op jit(solution)/shard_map/ppermute | solution.py:1297
  223.7 36.5 %all-to-all-start.5 = ((bf16[32,24,576]{2,1,0:T(8,128)(2,1)}), bf16[32,24,576]{2,1,0:T(8,128)(2,1)S(1)}, u32[]{:S(2)}, u32[]{:S(2)}) async-start(bf16[32,24,576]{2,1,0:T(8,128)(2,1)} %bitcast.18), calls=%async_computation.5 | async-start | bytes 1966080 | tf_op jit(solution)/shard_map/all_to_all | solution.py:1351
  231.6 14.8 %collective-permute-start.27 = (bf16[2432,128]{1,0:T(8,128)(2,1)S(1)}, bf16[2432,128]{1,0:T(8,128)(2,1)S(1)}, u32[]{:S(2)}, u32[]{:S(2)}) collective-permute-start(bf16[2432,128]{1,0:T(8,128)(2,1)S(1)} %bitcast.16), channel_id=1, source_target_pairs={{1,0},{3,2},{5,4},{7,6},{9,8},{11,10},{13,12},{15,14},{17,16},{19,... | collective-permute-start | bytes 1867784 | tf_op jit(solution)/shard_map/ppermute | solution.py:1431
  233.8 12.5 %collective-permute-start.26 = (bf16[2048,128]{1,0:T(8,128)(2,1)}, bf16[2048,128]{1,0:T(8,128)(2,1)S(1)}, u32[]{:S(2)}, u32[]{:S(2)}) collective-permute-start(bf16[2048,128]{1,0:T(8,128)(2,1)} %collective-permute-done.25.rest_5_), channel_id=1, source_target_pairs={{0,1},{2,3},{4,5},{6,7},{8,9},{10,11},{12,13},{14,15},{16,17},{18,... | collective-permute-start | bytes 1572872 | tf_op jit(solution)/shard_map/ppermute | solution.py:1432
  (25 other events, 233.3 us)

commit v3 on v2

--- a/solution.py
+++ b/solution.py
@@ -1028,7 +1028,7 @@
         pltpu.VMEM((HALF,), F32),
         pltpu.VMEM((HALF,), F32),
         pltpu.VMEM((FLAT_SCRATCH, LANES), F32),
-        pltpu.VMEM((Q_TILES * D, LANES), F32),
+        pltpu.VMEM((Q_TILES * D + 8, LANES), F32),
         pltpu.VMEM((8 * LANES,), F32),
         pltpu.SemaphoreType.DMA((2,)),
     ]
@@ -1241,7 +1241,7 @@
 def run_update_first(scale, rate, core, bits, halves, state):
     scratch = [
         pltpu.VMEM((2 * PART_ROWS, LANES), BF),
-        pltpu.VMEM((FLAT_BASE + CHUNK, LANES), F32),
+        pltpu.VMEM((FLAT_BASE + CHUNK + 16, LANES), F32),
         *chunk_scratch(12),
         pltpu.SemaphoreType.DMA((4,)),
         *extra_scratch(TAIL_ZERO, CHUNK),
@@ -1261,7 +1261,7 @@
 def run_update_second(scale, rate, core, bits, halves, late_halves, state, done):
     scratch = [
         pltpu.VMEM((FLAT_BASE + CHUNK + 8, LANES), F32),
-        pltpu.VMEM((Q_TILES * D, LANES), F32),
+        pltpu.VMEM((Q_TILES * D + 8, LANES), F32),
         pltpu.VMEM((2 * REST_SLOT + PART_ROWS, LANES), BF),
         pltpu.VMEM((PART_ROWS, LANES), BF),
         pltpu.VMEM((32, LANES), BF),

time: 262 us -> 262 us (level)
  no operation moved by 1% of the time
where the time goes in v3:
time: 262 us; the launch traced here: 261 us
  Pallas kernels  128 us (49%)
  starting transfers between devices  55.2 us (21%)
  waiting for transfers between devices  49.5 us (19%)
  blocking collectives  15.9 us (6%)
  local copies, waits for them, and re-layouts  7.54 us (3%)
  other arithmetic  3.66 us (1%)
    pallas_call x1, Pallas kernels, run_mlp(): call(mlp_pass, outs, [smem()] * 5 + [hbm()] * 3 + [vmem()] + [hbm()] * 4,...  28.5 us
    ppermute x22, waiting for transfers between devices, xor_swap(): return lax.ppermute(value, 'dp', [(i, i ^ 1 << bit) for i in range(size)])  25.4 us
    all_to_all x4, starting transfers between devices, exchange(): return lax.all_to_all(value, axes, split_axis=0, concat_axis=0, tiled=True)  23 us
    pallas_call x2, Pallas kernels, run_backward_groups(): pl.pallas_call(functools.partial(backward_groups, first), grid=(count,),...  20.2 us
    ppermute x22, starting transfers between devices, xor_swap(): return lax.ppermute(value, 'dp', [(i, i ^ 1 << bit) for i in range(size)])  19.8 us
    pallas_call x1, Pallas kernels, run_attention_forward(): call(attention_forward, outs, [vmem()] * 4 + [hbm()] + [vmem()] * 2, [hbm...  17.6 us
    all_to_all x1, blocking collectives, spread(): lax.all_to_all(blocks, 'dp', split_axis=0, concat_axis=0, tiled=True, axi...  15.9 us
    all_to_all x4, waiting for transfers between devices, exchange(): return lax.all_to_all(value, axes, split_axis=0, concat_axis=0, tiled=True)  15.6 us
  transfers between devices with their start and end apart: 33, of which 12 were waited for; matrix products, arithmetic and copies ran while one was open for 2% of the time, Pallas kernels for 36%

profile of v3, /device:TPU:1, one launch (start us, length us, event | category | flops | bytes accessed | tf_op | source)
XLA Modules:
  0.0 261.1 jit_solution(13578743147958156339)
XLA Ops:
  3.5 7.1 %all-to-all-start = ((bf16[32,24,576]{2,1,0:T(8,128)(2,1)}), bf16[32,24,576]{2,1,0:T(8,128)(2,1)S(1)}, u32[]{:S(2)}, u32[]{:S(2)}) async-start(bf16[32,24,576]{2,1,0:T(8,128)(2,1)} %gather_fusion), calls=%async_computation | async-start | bytes 1966080 | tf_op jit(solution)/shard_map/all_to_all | solution.py:1351
  12.9 12.3 %prepare_weights.1 = (f32[1,576]{1,0:T(1,128)}, f32[1,576]{1,0:T(1,128)}, bf16[576,640]{1,0:T(8,128)(2,1)}, bf16[576,384]{1,0:T(8,128)(2,1)}, bf16[640,576]{1,0:...) custom-call(s32[1]{0:T(128)} %bitcast.1.core_ref, ...), custom_call_target="tpu_custom_call" | custom-call | flops 10000000000 | bytes 14459904 | tf_op jit(solution)/shard_map/prepare_weights/pallas_call | solution.py:1035
  25.2 9.3 %all-to-all-done = bf16[32,24,576]{2,1,0:T(8,128)(2,1)S(1)} async-done(((bf16[32,24,576]{2,1,0:T(8,128)(2,1)}), bf16[32,24,576]{2,1,0:T(8,128)(2,1)S(1)}, u32[]{:S(2)}, u32[]{:S(2)}) %all-to-all-start) | async-done | bytes 884768 | tf_op jit(solution)/shard_map/all_to_all | solution.py:1351
  34.5 4.5 %all-to-all-start.1 = ((bf16[32,24,576]{2,1,0:T(8,128)(2,1)}), bf16[32,24,576]{2,1,0:T(8,128)(2,1)S(1)}, u32[]{:S(2)}, u32[]{:S(2)}) async-start(bf16[32,24,576]{2,1,0:T(8,128)(2,1)} %param.9), calls=%async_computation.1 | async-start | bytes 1966080 | tf_op jit(solution)/shard_map/all_to_all | solution.py:1351
  39.1 17.6 %attention_forward.1 = (f32[768,576]{1,0:T(8,128)}, bf16[768,640]{1,0:T(8,128)(2,1)}, bf16[5,768,128]{2,1,0:T(8,128)(2,1)}, bf16[6,768,128]{2,1,0:T(8,128)(2,1)}...) custom-call(bf16[768,576]{1,0:T(8,128)(2,1)} %bitcast.19, f32[1,576]{1,0:T(1,128)} %get-tuple-element.132.ga_ref, ...), custom_call_target="tpu_custom_call" | custom-call | flops 15000000512 | bytes 12288000 | tf_op jit(solution)/shard_map/attention_forward/pallas_call | solution.py:1057
  56.7 6.2 %all-to-all-done.1 = bf16[32,24,576]{2,1,0:T(8,128)(2,1)S(1)} async-done(((bf16[32,24,576]{2,1,0:T(8,128)(2,1)}), bf16[32,24,576]{2,1,0:T(8,128)(2,1)S(1)}, u32[]{:S(2)}, u32[]{:S(2)}) %all-to-all-start.1) | async-done | bytes 884768 | tf_op jit(solution)/shard_map/all_to_all | solution.py:1351
  64.0 28.5 %mlp_pass.1 = (bf16[768,576]{1,0:T(8,128)(2,1)}, f32[768,576]{1,0:T(8,128)}, bf16[5,768,128]{2,1,0:T(8,128)(2,1)}, f32[1,576]{1,0:T(1,128)}, bf16[12288,128]{1,0:T(8,128)(2,1)}, /*index=5*/bf16[12288,128]{1,0:T(8,128)(2,1)}) custom-call(s32[1]{0:T(128)} %bitcast.1.core_ref, s32[1]{0:T(128)} %bitcast.5.slot_ref, s32[32]{0:T(128)} %lengths_ref.1, ...), custom_call_target="tpu_custom_call" | custom-call | flops 24999999488 | bytes 19862016 | tf_op jit(solution)/shard_map/mlp_pass/pallas_call | solution.py:1085
  93.9 3.5 %all-to-all-start.2 = ((bf16[32,24,576]{2,1,0:T(8,128)(2,1)}), bf16[32,24,576]{2,1,0:T(8,128)(2,1)S(1)}, u32[]{:S(2)}, u32[]{:S(2)}) async-start(bf16[32,24,576]{2,1,0:T(8,128)(2,1)} %bitcast.21), calls=%async_computation.2 | async-start | bytes 1966080 | tf_op jit(solution)/shard_map/all_to_all | solution.py:1351
  97.4 7.6 %backward_groups.2 = (f32[1,2,768,128]{3,2,1,0:T(8,128)}, f32[1,768,128]{2,1,0:T(8,128)}, f32[1,768,128]{2,1,0:T(8,128)}) custom-call(bf16[5,768,128]{2,1,0:T(8,128)(2,1)} %get-tuple-element.164.q_ref, bf16[5,768,128]{2,1,0:T(8,128)(2,1)} %get-tuple-element.165.dm_ref, bf16[6,768,128]{2,1,0:T(8,128)(2,1)} %get-tuple-element.166.k_ref, ...), custom_call_target="tpu_custom_call" | custom-call | flops 8000000000 | bytes 3000000 | tf_op jit(solution)/shard_map/backward_groups/pallas_call | solution.py:1124
  105.0 2.9 %gather_sum.6 = (bf16[2048,128]{1,0:T(8,128)(2,1)S(1)}, bf16[2048,128]{1,0:T(8,128)(2,1)S(1)}, bf16[2048,128]{1,0:T(8,128)(2,1)S(1)}, bf16[2048,128]{1,0:T(8,128...) custom-call(s32[3]{0:T(128)S(1)} %pad_add_fusion.1.bits_ref, bf16[12288,128]{1,0:T(8,128)(2,1)S(1)} %copy-done.2, ...), custom_call_target="tpu_custom_call" | custom-call | flops 1000000 | bytes 6291456 | tf_op jit(solution)/shard_map/gather_sum/pallas_call | solution.py:1191
  111.8 12.6 %backward_groups.3 = (f32[2,2,768,128]{3,2,1,0:T(8,128)}, f32[2,768,128]{2,1,0:T(8,128)}, f32[2,768,128]{2,1,0:T(8,128)}) custom-call(bf16[5,768,128]{2,1,0:T(8,128)(2,1)} %get-tuple-element.164.q_ref, bf16[5,768,128]{2,1,0:T(8,128)(2,1)} %get-tuple-element.165.dm_ref, bf16[6,768,128]{2,1,0:T(8,128)(2,1)} %get-tuple-element.166.k_ref, ...), custom_call_target="tpu_custom_call" | custom-call | flops 16000000000 | bytes 6000000 | tf_op jit(solution)/shard_map/backward_groups/pallas_call | solution.py:1124
  131.1 8.7 %backward_finish.1 = (bf16[768,576]{1,0:T(8,128)(2,1)}, bf16[768,640]{1,0:T(8,128)(2,1)}, bf16[768,384]{1,0:T(8,128)(2,1)}, bf16[768,576]{1,0:T(8,128)(2,1)}, f32[1,576]{1,0:T(1,128)}) custom-call(bf16[768,576]{1,0:T(8,128)(2,1)} %bitcast.20, f32[1,576]{1,0:T(1,128)} %get-tuple-element.132.ga_ref, f32[768,576]{1,0:T(8,128)} %get-tuple-element.163.dh1_ref, ...), custom_call_target="tpu_custom_call" | custom-call | flops 4000000000 | bytes 6689280 | tf_op jit(solution)/shard_map/backward_finish/pallas_call | solution.py:1158
  144.5 4.1 %late_weights.1 = (bf16[2432,128]{1,0:T(8,128)(2,1)}, bf16[2432,128]{1,0:T(8,128)(2,1)}) custom-call(s32[1]{0:T(128)} %bitcast.1.core_ref, bf16[768,576]{1,0:T(8,128)(2,1)} %get-tuple-element.175.nm_s, bf16[768,640]{1,0:T(8,128)(2,1)} %get-tuple-element.176.dq_s, bf16[768,384]{1,0:T(8,128)(2,1)} %get-tuple-element.177.dkv_s, ...), custom_call_target="tpu_custom_call" | custom-call | flops 4000000000 | bytes 2490368 | tf_op jit(solution)/shard_map/late_weights/pallas_call | solution.py:1172
  149.8 2.8 %collective-permute-start.11 = (bf16[2432,128]{1,0:T(8,128)(2,1)}, bf16[2432,128]{1,0:T(8,128)(2,1)S(1)}, u32[]{:S(2)}, u32[]{:S(2)}) collective-permute-start(bf16[2432,128]{1,0:T(8,128)(2,1)} %get-tuple-element.203), channel_id=1, source_target_pairs={{0,1},{1,0},{2,3},{3,2},{4,5},{5,4},{6,7},{7,6},{8,9},{9,8},{10,11... | collective-permute-start | bytes 1867784 | tf_op jit(solution)/shard_map/ppermute | solution.py:1399
  156.6 7.7 %collective-permute-done.12.refs_1_ = bf16[768,128]{1,0:T(8,128)(2,1)S(1)} collective-permute-done((bf16[768,128]{1,0:T(8,128)(2,1)S(1)}, bf16[768,128]{1,0:T(8,128)(2,1)S(1)}, u32[]{:S(2)}, u32[]{:S(2)}) %collective-permute-start.12) | collective-permute-done | bytes 196640 | tf_op jit(solution)/shard_map/ppermute | solution.py:1297
  164.4 3.5 %all-to-all-start.3 = ((bf16[4,608,128]{2,1,0:T(8,128)(2,1)}), bf16[4,608,128]{2,1,0:T(8,128)(2,1)S(1)}, u32[]{:S(2)}, u32[]{:S(2)}) async-start(bf16[4,608,128]{2,1,0:T(8,128)(2,1)} %bitcast.10), calls=%async_computation.3 | async-start | bytes 1245184 | tf_op jit(solution)/shard_map/all_to_all | solution.py:1316
  168.2 8.3 %all-to-all-done.3 = bf16[4,608,128]{2,1,0:T(8,128)(2,1)S(1)} async-done(((bf16[4,608,128]{2,1,0:T(8,128)(2,1)}), bf16[4,608,128]{2,1,0:T(8,128)(2,1)S(1)}, u32[]{:S(2)}, u32[]{:S(2)}) %all-to-all-start.3) | async-done | bytes 622624 | tf_op jit(solution)/shard_map/all_to_all | solution.py:1316
  176.7 3.1 %collective-permute-done.13.refs_1_ = bf16[768,128]{1,0:T(8,128)(2,1)S(1)} collective-permute-done((bf16[768,128]{1,0:T(8,128)(2,1)S(1)}, bf16[768,128]{1,0:T(8,128)(2,1)S(1)}, u32[]{:S(2)}, u32[]{:S(2)}) %collective-permute-start.13) | collective-permute-done | bytes 196640 | tf_op jit(solution)/shard_map/ppermute | solution.py:1297
  186.1 2.8 %collective-permute-done.15.refs_3_ = bf16[512,128]{1,0:T(8,128)(2,1)S(1)} collective-permute-done((bf16[512,128]{1,0:T(8,128)(2,1)S(1)}, bf16[512,128]{1,0:T(8,128)(2,1)S(1)}, u32[]{:S(2)}, u32[]{:S(2)}) %collective-permute-start.15) | collective-permute-done | bytes 131104 | tf_op jit(solution)/shard_map/ppermute | solution.py:1297
  194.8 5.9 %collective-permute-done.18 = bf16[608,128]{1,0:T(8,128)(2,1)S(1)} collective-permute-done((bf16[608,128]{1,0:T(8,128)(2,1)S(1)}, bf16[608,128]{1,0:T(8,128)(2,1)S(1)}, u32[]{:S(2)}, u32[]{:S(2)}) %collective-permute-start.18) | collective-permute-done | bytes 155680 | tf_op jit(solution)/shard_map/ppermute | solution.py:1297
  206.1 15.9 %all_to_all.30 = bf16[4,608,128]{2,1,0:T(8,128)(2,1)S(1)} all-to-all(bf16[4,608,128]{2,1,0:T(8,128)(2,1)S(1)} %broadcast_in_dim.37), channel_id=1, replica_groups={{0,2,4,6},{8,10,12,14},{16,18,20,22},{24,26,28,30},{1,3,5,7},{9,11,13,1..., dimensions={0} | all-to-all | bytes 1245184 | tf_op jit(solution)/shard_map/all_to_all | solution.py:1316
  223.7 7.9 %all-to-all-start.5 = ((bf16[32,24,576]{2,1,0:T(8,128)(2,1)}), bf16[32,24,576]{2,1,0:T(8,128)(2,1)S(1)}, u32[]{:S(2)}, u32[]{:S(2)}) async-start(bf16[32,24,576]{2,1,0:T(8,128)(2,1)} %bitcast.18), calls=%async_computation.5 | async-start | bytes 1966080 | tf_op jit(solution)/shard_map/all_to_all | solution.py:1351
  235.1 11.2 %update_first.1 = (f32[1770048]{0:T(1024)}, f32[1770048]{0:T(1024)}, f32[1770048]{0:T(1024)}, f32[1770048]{0:T(1024)}) custom-call(s32[1]{0:T(128)} %bitcast.1.core_ref, s32[3]{0:T(128)} %copy-done.7, bf16[2048,128]{1,0:T(8,128)(2,1)} %copy-done.3, bf16[2048,128]{1,0:T(8,128)(2,1)} %copy-done.9, bf16[2048,128]{1,0:T(8,128)(2,1)} %copy-done.4, ...), custom_call_target="tpu_custom_call" | custom-call | flops 1000000000 | bytes 56641536 | tf_op jit(solution)/shard_map/update_first/pallas_call | solution.py:1249
  247.3 12.8 %update_second.1 = (f32[1770048]{0:T(1024)}, f32[1770048]{0:T(1024)}, f32[1770048]{0:T(1024)}, f32[1770048]{0:T(1024)}) custom-call(s32[1]{0:T(128)} %bitcast.1.core_ref, s32[3]{0:T(128)} %copy-done.7, bf16[2048,128]{1,0:T(8,128)(2,1)} %copy-done.3, ...), custom_call_target="tpu_custom_call", output_to_operand_aliasing={{0}: (15, {}), {1}: (16, {}), {2}: (17, {}), {3}: (18, {})} | custom-call | flops 1000000000 | bytes 56641536 | tf_op jit(solution)/shard_map/update_second/pallas_call | solution.py:1278
  (109 shorter events, 53.2 us)
Async XLA Ops:
  0.6 12.3 %collective-permute-start = (f32[1770048]{0:T(1024)}, f32[1770048]{0:T(1024)}, u32[]{:S(2)}, u32[]{:S(2)}) collective-permute-start(f32[1770048]{0:T(1024)} %rest_10_.1), channel_id=1, source_target_pairs={{0,1},{1,0},{2,3},{3,2},{4,5},{5,4},{6,7},{7,6},{8,9},{9,8},{10,11... | collective-permute-start | bytes 21240584 | tf_op jit(solution)/shard_map/ppermute | solution.py:1356
  3.5 31.0 %all-to-all-start = ((bf16[32,24,576]{2,1,0:T(8,128)(2,1)}), bf16[32,24,576]{2,1,0:T(8,128)(2,1)S(1)}, u32[]{:S(2)}, u32[]{:S(2)}) async-start(bf16[32,24,576]{2,1,0:T(8,128)(2,1)} %gather_fusion), calls=%async_computation | async-start | bytes 1966080 | tf_op jit(solution)/shard_map/all_to_all | solution.py:1351
  34.5 28.5 %all-to-all-start.1 = ((bf16[32,24,576]{2,1,0:T(8,128)(2,1)}), bf16[32,24,576]{2,1,0:T(8,128)(2,1)S(1)}, u32[]{:S(2)}, u32[]{:S(2)}) async-start(bf16[32,24,576]{2,1,0:T(8,128)(2,1)} %param.9), calls=%async_computation.1 | async-start | bytes 1966080 | tf_op jit(solution)/shard_map/all_to_all | solution.py:1351
  92.5 12.6 %collective-permute-start.1 = (bf16[12288,128]{1,0:T(8,128)(2,1)}, bf16[12288,128]{1,0:T(8,128)(2,1)}, u32[]{:S(2)}, u32[]{:S(2)}) collective-permute-start(bf16[12288,128]{1,0:T(8,128)(2,1)} %get-tuple-element.147), channel_id=1, source_target_pairs={{0,1},{1,0},{2,3},{3,2},{4,5},{5,4},{6,7},{7,6},{8,9},{9,8},{10,11... | collective-permute-start | bytes 9437192 | tf_op jit(solution)/shard_map/ppermute | solution.py:1374
  93.9 35.1 %all-to-all-start.2 = ((bf16[32,24,576]{2,1,0:T(8,128)(2,1)}), bf16[32,24,576]{2,1,0:T(8,128)(2,1)S(1)}, u32[]{:S(2)}, u32[]{:S(2)}) async-start(bf16[32,24,576]{2,1,0:T(8,128)(2,1)} %bitcast.21), calls=%async_computation.2 | async-start | bytes 1966080 | tf_op jit(solution)/shard_map/all_to_all | solution.py:1351
  108.0 16.4 %collective-permute-start.2 = (bf16[2048,128]{1,0:T(8,128)(2,1)S(1)}, bf16[2048,128]{1,0:T(8,128)(2,1)S(1)}, u32[]{:S(2)}, u32[]{:S(2)}) collective-permute-start(bf16[2048,128]{1,0:T(8,128)(2,1)S(1)} %get-tuple-element.157), channel_id=1, source_target_pairs={{0,2},{2,0},{4,6},{6,4},{8,10},{10,8},{12,14},{14,12},{16,18},{18,... | collective-permute-start | bytes 1572872 | tf_op jit(solution)/shard_map/ppermute | solution.py:1297
  109.4 16.4 %collective-permute-start.3 = (bf16[2048,128]{1,0:T(8,128)(2,1)S(1)}, bf16[2048,128]{1,0:T(8,128)(2,1)S(1)}, u32[]{:S(2)}, u32[]{:S(2)}) collective-permute-start(bf16[2048,128]{1,0:T(8,128)(2,1)S(1)} %get-tuple-element.158), channel_id=1, source_target_pairs={{0,4},{2,6},{4,0},{6,2},{8,12},{10,14},{12,8},{14,10},{16,20},{18,... | collective-permute-start | bytes 1572872 | tf_op jit(solution)/shard_map/ppermute | solution.py:1297
  110.6 17.3 %collective-permute-start.4 = (bf16[2048,128]{1,0:T(8,128)(2,1)S(1)}, bf16[2048,128]{1,0:T(8,128)(2,1)S(1)}, u32[]{:S(2)}, u32[]{:S(2)}) collective-permute-start(bf16[2048,128]{1,0:T(8,128)(2,1)S(1)} %get-tuple-element.159), channel_id=1, source_target_pairs={{0,8},{2,10},{4,12},{6,14},{8,0},{10,2},{12,4},{14,6},{16,24},{18,... | collective-permute-start | bytes 1572872 | tf_op jit(solution)/shard_map/ppermute | solution.py:1297
  129.1 10.7 %collective-permute-start.5 = (bf16[1024,128]{1,0:T(8,128)(2,1)S(1)}, bf16[1024,128]{1,0:T(8,128)(2,1)S(1)}, u32[]{:S(2)}, u32[]{:S(2)}) collective-permute-start(bf16[1024,128]{1,0:T(8,128)(2,1)S(1)} %get-tuple-element.182), channel_id=1, source_target_pairs={{0,4},{2,6},{4,0},{6,2},{8,12},{10,14},{12,8},{14,10},{16,20},{18,... | collective-permute-start | bytes 786440 | tf_op jit(solution)/shard_map/ppermute | solution.py:1297
  129.9 9.8 %collective-permute-start.6 = (bf16[1024,128]{1,0:T(8,128)(2,1)S(1)}, bf16[1024,128]{1,0:T(8,128)(2,1)S(1)}, u32[]{:S(2)}, u32[]{:S(2)}) collective-permute-start(bf16[1024,128]{1,0:T(8,128)(2,1)S(1)} %get-tuple-element.183), channel_id=1, source_target_pairs={{0,8},{2,10},{4,12},{6,14},{8,0},{10,2},{12,4},{14,6},{16,24},{18,... | collective-permute-start | bytes 786440 | tf_op jit(solution)/shard_map/ppermute | solution.py:1297
  130.0 9.8 %collective-permute-start.7 = (bf16[1024,128]{1,0:T(8,128)(2,1)S(1)}, bf16[1024,128]{1,0:T(8,128)(2,1)S(1)}, u32[]{:S(2)}, u32[]{:S(2)}) collective-permute-start(bf16[1024,128]{1,0:T(8,128)(2,1)S(1)} %get-tuple-element.184), channel_id=1, source_target_pairs={{0,2},{2,0},{4,6},{6,4},{8,10},{10,8},{12,14},{14,12},{16,18},{18,... | collective-permute-start | bytes 786440 | tf_op jit(solution)/shard_map/ppermute | solution.py:1297
  152.6 11.7 %collective-permute-start.12 = (bf16[768,128]{1,0:T(8,128)(2,1)S(1)}, bf16[768,128]{1,0:T(8,128)(2,1)S(1)}, u32[]{:S(2)}, u32[]{:S(2)}) collective-permute-start(bf16[768,128]{1,0:T(8,128)(2,1)S(1)} %get-tuple-element.205), channel_id=1, source_target_pairs={{0,16},{2,18},{4,20},{6,22},{8,24},{10,26},{12,28},{14,30},{16,0},... | collective-permute-start | bytes 589832 | tf_op jit(solution)/shard_map/ppermute | solution.py:1297
  164.4 12.2 %all-to-all-start.3 = ((bf16[4,608,128]{2,1,0:T(8,128)(2,1)}), bf16[4,608,128]{2,1,0:T(8,128)(2,1)S(1)}, u32[]{:S(2)}, u32[]{:S(2)}) async-start(bf16[4,608,128]{2,1,0:T(8,128)(2,1)} %bitcast.10), calls=%async_computation.3 | async-start | bytes 1245184 | tf_op jit(solution)/shard_map/all_to_all | solution.py:1316
  168.2 11.5 %collective-permute-start.13 = (bf16[768,128]{1,0:T(8,128)(2,1)S(1)}, bf16[768,128]{1,0:T(8,128)(2,1)S(1)}, u32[]{:S(2)}, u32[]{:S(2)}) collective-permute-start(bf16[768,128]{1,0:T(8,128)(2,1)S(1)} %gather_sum.11.refs_0_), channel_id=1, source_target_pairs={{0,16},{2,18},{4,20},{6,22},{8,24},{10,26},{12,28},{14,30},{16,0},... | collective-permute-start | bytes 589832 | tf_op jit(solution)/shard_map/ppermute | solution.py:1297
  190.5 10.2 %collective-permute-start.18 = (bf16[608,128]{1,0:T(8,128)(2,1)S(1)}, bf16[608,128]{1,0:T(8,128)(2,1)S(1)}, u32[]{:S(2)}, u32[]{:S(2)}) collective-permute-start(bf16[608,128]{1,0:T(8,128)(2,1)S(1)} %add_convert_fusion.1), channel_id=1, source_target_pairs={{0,16},{2,18},{4,20},{6,22},{8,24},{10,26},{12,28},{14,30},{16,0},... | collective-permute-start | bytes 466952 | tf_op jit(solution)/shard_map/ppermute | solution.py:1297
  191.1 9.7 %collective-permute-start.19 = (bf16[1024,128]{1,0:T(8,128)(2,1)S(1)}, bf16[1024,128]{1,0:T(8,128)(2,1)S(1)}, u32[]{:S(2)}, u32[]{:S(2)}) collective-permute-start(bf16[1024,128]{1,0:T(8,128)(2,1)S(1)} %get-tuple-element.228.refs_0_), channel_id=1, source_target_pairs={{0,4},{2,6},{4,0},{6,2},{8,12},{10,14},{12,8},{14,10},{16,20},{18,... | collective-permute-start | bytes 786440 | tf_op jit(solution)/shard_map/ppermute | solution.py:1297
  192.5 9.6 %collective-permute-start.20 = (bf16[1024,128]{1,0:T(8,128)(2,1)S(1)}, bf16[1024,128]{1,0:T(8,128)(2,1)S(1)}, u32[]{:S(2)}, u32[]{:S(2)}) collective-permute-start(bf16[1024,128]{1,0:T(8,128)(2,1)S(1)} %get-tuple-element.229.refs_1_), channel_id=1, source_target_pairs={{0,8},{2,10},{4,12},{6,14},{8,0},{10,2},{12,4},{14,6},{16,24},{18,... | collective-permute-start | bytes 786440 | tf_op jit(solution)/shard_map/ppermute | solution.py:1297
  202.8 19.2 %collective-permute-start.25 = (bf16[2048,128]{1,0:T(8,128)(2,1)S(1)}, bf16[2048,128]{1,0:T(8,128)(2,1)}, u32[]{:S(2)}, u32[]{:S(2)}) collective-permute-start(bf16[2048,128]{1,0:T(8,128)(2,1)S(1)} %get-tuple-element.239.rest_4_), channel_id=1, source_target_pairs={{0,8},{2,10},{4,12},{6,14},{8,0},{10,2},{12,4},{14,6},{16,24},{18,... | collective-permute-start | bytes 1572872 | tf_op jit(solution)/shard_map/ppermute | solution.py:1297
  202.9 19.1 %collective-permute-start.22 = (bf16[2048,128]{1,0:T(8,128)(2,1)S(1)}, bf16[2048,128]{1,0:T(8,128)(2,1)S(1)}, u32[]{:S(2)}, u32[]{:S(2)}) collective-permute-start(bf16[2048,128]{1,0:T(8,128)(2,1)S(1)} %get-tuple-element.239.rest_4_), channel_id=1, source_target_pairs={{0,1},{2,3},{4,5},{6,7},{8,9},{10,11},{12,13},{14,15},{16,17},{18,... | collective-permute-start | bytes 1572872 | tf_op jit(solution)/shard_map/ppermute | solution.py:1424
  204.2 17.8 %collective-permute-start.23 = (bf16[2048,128]{1,0:T(8,128)(2,1)S(1)}, bf16[2048,128]{1,0:T(8,128)(2,1)S(1)}, u32[]{:S(2)}, u32[]{:S(2)}) collective-permute-start(bf16[2048,128]{1,0:T(8,128)(2,1)S(1)} %get-tuple-element.240.rest_0_), channel_id=1, source_target_pairs={{0,2},{2,0},{4,6},{6,4},{8,10},{10,8},{12,14},{14,12},{16,18},{18,... | collective-permute-start | bytes 1572872 | tf_op jit(solution)/shard_map/ppermute | solution.py:1297
  205.5 16.6 %collective-permute-start.24 = (bf16[2048,128]{1,0:T(8,128)(2,1)S(1)}, bf16[2048,128]{1,0:T(8,128)(2,1)S(1)}, u32[]{:S(2)}, u32[]{:S(2)}) collective-permute-start(bf16[2048,128]{1,0:T(8,128)(2,1)S(1)} %get-tuple-element.241.rest_2_), channel_id=1, source_target_pairs={{0,4},{2,6},{4,0},{6,2},{8,12},{10,14},{12,8},{14,10},{16,20},{18,... | collective-permute-start | bytes 1572872 | tf_op jit(solution)/shard_map/ppermute | solution.py:1297
  223.7 36.5 %all-to-all-start.5 = ((bf16[32,24,576]{2,1,0:T(8,128)(2,1)}), bf16[32,24,576]{2,1,0:T(8,128)(2,1)S(1)}, u32[]{:S(2)}, u32[]{:S(2)}) async-start(bf16[32,24,576]{2,1,0:T(8,128)(2,1)} %bitcast.18), calls=%async_computation.5 | async-start | bytes 1966080 | tf_op jit(solution)/shard_map/all_to_all | solution.py:1351
  231.6 14.7 %collective-permute-start.27 = (bf16[2432,128]{1,0:T(8,128)(2,1)S(1)}, bf16[2432,128]{1,0:T(8,128)(2,1)S(1)}, u32[]{:S(2)}, u32[]{:S(2)}) collective-permute-start(bf16[2432,128]{1,0:T(8,128)(2,1)S(1)} %bitcast.16), channel_id=1, source_target_pairs={{1,0},{3,2},{5,4},{7,6},{9,8},{11,10},{13,12},{15,14},{17,16},{19,... | collective-permute-start | bytes 1867784 | tf_op jit(solution)/shard_map/ppermute | solution.py:1431
  233.8 12.5 %collective-permute-start.26 = (bf16[2048,128]{1,0:T(8,128)(2,1)}, bf16[2048,128]{1,0:T(8,128)(2,1)S(1)}, u32[]{:S(2)}, u32[]{:S(2)}) collective-permute-start(bf16[2048,128]{1,0:T(8,128)(2,1)} %collective-permute-done.25.rest_5_), channel_id=1, source_target_pairs={{0,1},{2,3},{4,5},{6,7},{8,9},{10,11},{12,13},{14,15},{16,17},{18,... | collective-permute-start | bytes 1572872 | tf_op jit(solution)/shard_map/ppermute | solution.py:1432
  (25 other events, 233.3 us)

commit v4 on v3

--- a/solution.py
+++ b/solution.py
@@ -523,14 +523,39 @@
 
 
 def backward_finish(
-    x_ref, ga_ref, dh1_ref, dqa_ref, dka_ref, dva_ref, dqb_ref, dkb_ref, dvb_ref,
-    wq_ref, wkv_ref, cos_ref, sin_ref,
-    dx_ref, dq_s, dkv_s, nm_s, gga_ref,
+    x_hbm, ga_ref, dh1_hbm, dqa_hbm, dka_hbm, dva_hbm, dqb_hbm, dkb_hbm, dvb_hbm,
+    wq_ref, wkv_ref, cos_hbm, sin_hbm,
+    dx_hbm, dq_hbm, dkv_hbm, nm_hbm, gga_ref,
+    x_ref, dh1_ref, cos_ref, sin_ref, dqa_ref, dka_ref, dva_ref, dqb_ref, dkb_ref, dvb_ref,
+    dx_ref, dq_s, dkv_s, nm_s, in_sem, out_sem,
 ):
     seq_len = x_ref.shape[0]
     low = low_half(BLOCK)
 
+    def rows_of(ref, b):
+        rows = pl.ds(pl.multiple_of(b * BLOCK, BLOCK), BLOCK)
+        return ref.at[(slice(None),) * (len(ref.shape) - 2) + (rows,)]
+
+    def moves(pairs, b, sem):
+        return [
+            pltpu.make_async_copy(rows_of(source, b), rows_of(target, b), sem.at[b, i])
+            for i, (source, target) in enumerate(pairs)
+        ]
+
+    inward = (
+        (x_hbm, x_ref), (dh1_hbm, dh1_ref), (cos_hbm, cos_ref), (sin_hbm, sin_ref),
+        (dqa_hbm, dqa_ref), (dka_hbm, dka_ref), (dva_hbm, dva_ref),
+        (dqb_hbm, dqb_ref), (dkb_hbm, dkb_ref), (dvb_hbm, dvb_ref),
+    )
+    outward = ((dx_ref, dx_hbm), (dq_s, dq_hbm), (dkv_s, dkv_hbm), (nm_s, nm_hbm))
+    n_blocks = seq_len // BLOCK
+    for b in range(n_blocks):
+        for copy in moves(inward, b, in_sem):
+            copy.start()
+
     def block(b, gga):
+        for copy in moves(inward, b, in_sem):
+            copy.wait()
         rows = pl.ds(pl.multiple_of(b * BLOCK, BLOCK), BLOCK)
         cosine = cos_ref[rows, :]
         sine = sin_ref[rows, :]
@@ -567,9 +592,14 @@
             + r1 * scaled
             - stream * (r1 * r1 * r1) * jnp.mean(scaled * stream, axis=-1, keepdims=True)
         ).astype(BF)
+        for copy in moves(outward, b, out_sem):
+            copy.start()
         return gga + jnp.sum(d_normed * stream * r1, axis=0, keepdims=True)
 
     gga_ref[...] = lax.fori_loop(0, seq_len // BLOCK, block, jnp.zeros((1, D), F32))
+    for b in range(n_blocks):
+        for copy in moves(outward, b, out_sem):
+            copy.wait()
 
 
 def late_weights(
@@ -1158,9 +1188,17 @@
     return call(
         backward_finish,
         outs,
-        [vmem()] * 13,
-        [vmem()] * 5,
-        [],
+        [hbm(), vmem()] + [hbm()] * 7 + [vmem()] * 2 + [hbm()] * 2,
+        [hbm()] * 4 + [vmem()],
+        [
+            pltpu.VMEM(value.shape, value.dtype)
+            for value in (x, dh1, cosine, sine, *groups[0], *groups[1])
+        ]
+        + [pltpu.VMEM(shape, kind) for shape, kind in outs[:4]]
+        + [
+            pltpu.SemaphoreType.DMA((seq_len // BLOCK, 10)),
+            pltpu.SemaphoreType.DMA((seq_len // BLOCK, 4)),
+        ],
         4e9,
         "backward_finish",
         56,

time: 262 us -> 262 us (level)
  no operation moved by 1% of the time
where the time goes in v4:
time: 262 us; the launch traced here: 261 us
  Pallas kernels  128 us (49%)
  starting transfers between devices  55.2 us (21%)
  waiting for transfers between devices  49.5 us (19%)
  blocking collectives  15.9 us (6%)
  local copies, waits for them, and re-layouts  7.54 us (3%)
  other arithmetic  3.66 us (1%)
    pallas_call x1, Pallas kernels, run_mlp(): call(mlp_pass, outs, [smem()] * 5 + [hbm()] * 3 + [vmem()] + [hbm()] * 4,...  28.5 us
    ppermute x22, waiting for transfers between devices, xor_swap(): return lax.ppermute(value, 'dp', [(i, i ^ 1 << bit) for i in range(size)])  25.4 us
    all_to_all x4, starting transfers between devices, exchange(): return lax.all_to_all(value, axes, split_axis=0, concat_axis=0, tiled=True)  23 us
    pallas_call x2, Pallas kernels, run_backward_groups(): pl.pallas_call(functools.partial(backward_groups, first), grid=(count,),...  20.2 us
    ppermute x22, starting transfers between devices, xor_swap(): return lax.ppermute(value, 'dp', [(i, i ^ 1 << bit) for i in range(size)])  19.8 us
    pallas_call x1, Pallas kernels, run_attention_forward(): call(attention_forward, outs, [vmem()] * 4 + [hbm()] + [vmem()] * 2, [hbm...  17.6 us
    all_to_all x1, blocking collectives, spread(): lax.all_to_all(blocks, 'dp', split_axis=0, concat_axis=0, tiled=True, axi...  15.9 us
    all_to_all x4, waiting for transfers between devices, exchange(): return lax.all_to_all(value, axes, split_axis=0, concat_axis=0, tiled=True)  15.6 us
  transfers between devices with their start and end apart: 33, of which 12 were waited for; matrix products, arithmetic and copies ran while one was open for 2% of the time, Pallas kernels for 36%

profile of v4, /device:TPU:1, one launch (start us, length us, event | category | flops | bytes accessed | tf_op | source)
XLA Modules:
  0.0 260.8 jit_solution(8764918317236528091)
XLA Ops:
  3.5 7.1 %all-to-all-start = ((bf16[32,24,576]{2,1,0:T(8,128)(2,1)}), bf16[32,24,576]{2,1,0:T(8,128)(2,1)S(1)}, u32[]{:S(2)}, u32[]{:S(2)}) async-start(bf16[32,24,576]{2,1,0:T(8,128)(2,1)} %gather_fusion), calls=%async_computation | async-start | bytes 1966080 | tf_op jit(solution)/shard_map/all_to_all | solution.py:1389
  12.9 12.3 %prepare_weights.1 = (f32[1,576]{1,0:T(1,128)}, f32[1,576]{1,0:T(1,128)}, bf16[576,640]{1,0:T(8,128)(2,1)}, bf16[576,384]{1,0:T(8,128)(2,1)}, bf16[640,576]{1,0:...) custom-call(s32[1]{0:T(128)} %bitcast.1.core_ref, ...), custom_call_target="tpu_custom_call" | custom-call | flops 10000000000 | bytes 14459904 | tf_op jit(solution)/shard_map/prepare_weights/pallas_call | solution.py:1065
  25.2 9.3 %all-to-all-done = bf16[32,24,576]{2,1,0:T(8,128)(2,1)S(1)} async-done(((bf16[32,24,576]{2,1,0:T(8,128)(2,1)}), bf16[32,24,576]{2,1,0:T(8,128)(2,1)S(1)}, u32[]{:S(2)}, u32[]{:S(2)}) %all-to-all-start) | async-done | bytes 884768 | tf_op jit(solution)/shard_map/all_to_all | solution.py:1389
  34.5 4.5 %all-to-all-start.1 = ((bf16[32,24,576]{2,1,0:T(8,128)(2,1)}), bf16[32,24,576]{2,1,0:T(8,128)(2,1)S(1)}, u32[]{:S(2)}, u32[]{:S(2)}) async-start(bf16[32,24,576]{2,1,0:T(8,128)(2,1)} %param.9), calls=%async_computation.1 | async-start | bytes 1966080 | tf_op jit(solution)/shard_map/all_to_all | solution.py:1389
  39.1 17.6 %attention_forward.1 = (f32[768,576]{1,0:T(8,128)}, bf16[768,640]{1,0:T(8,128)(2,1)}, bf16[5,768,128]{2,1,0:T(8,128)(2,1)}, bf16[6,768,128]{2,1,0:T(8,128)(2,1)}...) custom-call(bf16[768,576]{1,0:T(8,128)(2,1)} %bitcast.19, f32[1,576]{1,0:T(1,128)} %get-tuple-element.132.ga_ref, ...), custom_call_target="tpu_custom_call" | custom-call | flops 15000000512 | bytes 12288000 | tf_op jit(solution)/shard_map/attention_forward/pallas_call | solution.py:1087
  56.7 6.2 %all-to-all-done.1 = bf16[32,24,576]{2,1,0:T(8,128)(2,1)S(1)} async-done(((bf16[32,24,576]{2,1,0:T(8,128)(2,1)}), bf16[32,24,576]{2,1,0:T(8,128)(2,1)S(1)}, u32[]{:S(2)}, u32[]{:S(2)}) %all-to-all-start.1) | async-done | bytes 884768 | tf_op jit(solution)/shard_map/all_to_all | solution.py:1389
  64.0 28.5 %mlp_pass.1 = (bf16[768,576]{1,0:T(8,128)(2,1)}, f32[768,576]{1,0:T(8,128)}, bf16[5,768,128]{2,1,0:T(8,128)(2,1)}, f32[1,576]{1,0:T(1,128)}, bf16[12288,128]{1,0:T(8,128)(2,1)}, /*index=5*/bf16[12288,128]{1,0:T(8,128)(2,1)}) custom-call(s32[1]{0:T(128)} %bitcast.1.core_ref, s32[1]{0:T(128)} %bitcast.5.slot_ref, s32[32]{0:T(128)} %lengths_ref.1, ...), custom_call_target="tpu_custom_call" | custom-call | flops 24999999488 | bytes 19862016 | tf_op jit(solution)/shard_map/mlp_pass/pallas_call | solution.py:1115
  93.9 3.5 %all-to-all-start.2 = ((bf16[32,24,576]{2,1,0:T(8,128)(2,1)}), bf16[32,24,576]{2,1,0:T(8,128)(2,1)S(1)}, u32[]{:S(2)}, u32[]{:S(2)}) async-start(bf16[32,24,576]{2,1,0:T(8,128)(2,1)} %bitcast.21), calls=%async_computation.2 | async-start | bytes 1966080 | tf_op jit(solution)/shard_map/all_to_all | solution.py:1389
  97.4 7.6 %backward_groups.2 = (f32[1,2,768,128]{3,2,1,0:T(8,128)}, f32[1,768,128]{2,1,0:T(8,128)}, f32[1,768,128]{2,1,0:T(8,128)}) custom-call(bf16[5,768,128]{2,1,0:T(8,128)(2,1)} %get-tuple-element.164.q_ref, bf16[5,768,128]{2,1,0:T(8,128)(2,1)} %get-tuple-element.165.dm_ref, bf16[6,768,128]{2,1,0:T(8,128)(2,1)} %get-tuple-element.166.k_ref, ...), custom_call_target="tpu_custom_call" | custom-call | flops 8000000000 | bytes 3000000 | tf_op jit(solution)/shard_map/backward_groups/pallas_call | solution.py:1154
  105.0 2.9 %gather_sum.6 = (bf16[2048,128]{1,0:T(8,128)(2,1)S(1)}, bf16[2048,128]{1,0:T(8,128)(2,1)S(1)}, bf16[2048,128]{1,0:T(8,128)(2,1)S(1)}, bf16[2048,128]{1,0:T(8,128...) custom-call(s32[3]{0:T(128)S(1)} %pad_add_fusion.1.bits_ref, bf16[12288,128]{1,0:T(8,128)(2,1)S(1)} %copy-done.2, ...), custom_call_target="tpu_custom_call" | custom-call | flops 1000000 | bytes 6291456 | tf_op jit(solution)/shard_map/gather_sum/pallas_call | solution.py:1229
  111.8 12.6 %backward_groups.3 = (f32[2,2,768,128]{3,2,1,0:T(8,128)}, f32[2,768,128]{2,1,0:T(8,128)}, f32[2,768,128]{2,1,0:T(8,128)}) custom-call(bf16[5,768,128]{2,1,0:T(8,128)(2,1)} %get-tuple-element.164.q_ref, bf16[5,768,128]{2,1,0:T(8,128)(2,1)} %get-tuple-element.165.dm_ref, bf16[6,768,128]{2,1,0:T(8,128)(2,1)} %get-tuple-element.166.k_ref, ...), custom_call_target="tpu_custom_call" | custom-call | flops 16000000000 | bytes 6000000 | tf_op jit(solution)/shard_map/backward_groups/pallas_call | solution.py:1154
  131.0 8.4 %backward_finish.1 = (bf16[768,576]{1,0:T(8,128)(2,1)}, bf16[768,640]{1,0:T(8,128)(2,1)}, bf16[768,384]{1,0:T(8,128)(2,1)}, bf16[768,576]{1,0:T(8,128)(2,1)}, f32[1,576]{1,0:T(1,128)}) custom-call(bf16[768,576]{1,0:T(8,128)(2,1)} %bitcast.20, f32[1,576]{1,0:T(1,128)} %get-tuple-element.132.ga_ref, f32[768,576]{1,0:T(8,128)} %get-tuple-element.163.dh1_hbm, ...), custom_call_target="tpu_custom_call" | custom-call | flops 4000000000 | bytes 6689280 | tf_op jit(solution)/shard_map/backward_finish/pallas_call | solution.py:1188
  144.1 4.1 %late_weights.1 = (bf16[2432,128]{1,0:T(8,128)(2,1)}, bf16[2432,128]{1,0:T(8,128)(2,1)}) custom-call(s32[1]{0:T(128)} %bitcast.1.core_ref, bf16[768,576]{1,0:T(8,128)(2,1)} %get-tuple-element.175.nm_s, bf16[768,640]{1,0:T(8,128)(2,1)} %get-tuple-element.176.dq_s, bf16[768,384]{1,0:T(8,128)(2,1)} %get-tuple-element.177.dkv_s, ...), custom_call_target="tpu_custom_call" | custom-call | flops 4000000000 | bytes 2490368 | tf_op jit(solution)/shard_map/late_weights/pallas_call | solution.py:1210
  149.5 2.8 %collective-permute-start.11 = (bf16[2432,128]{1,0:T(8,128)(2,1)}, bf16[2432,128]{1,0:T(8,128)(2,1)S(1)}, u32[]{:S(2)}, u32[]{:S(2)}) collective-permute-start(bf16[2432,128]{1,0:T(8,128)(2,1)} %get-tuple-element.203), channel_id=1, source_target_pairs={{0,1},{1,0},{2,3},{3,2},{4,5},{5,4},{6,7},{7,6},{8,9},{9,8},{10,11... | collective-permute-start | bytes 1867784 | tf_op jit(solution)/shard_map/ppermute | solution.py:1437
  156.3 7.7 %collective-permute-done.12.refs_1_ = bf16[768,128]{1,0:T(8,128)(2,1)S(1)} collective-permute-done((bf16[768,128]{1,0:T(8,128)(2,1)S(1)}, bf16[768,128]{1,0:T(8,128)(2,1)S(1)}, u32[]{:S(2)}, u32[]{:S(2)}) %collective-permute-start.12) | collective-permute-done | bytes 196640 | tf_op jit(solution)/shard_map/ppermute | solution.py:1335
  164.0 3.5 %all-to-all-start.3 = ((bf16[4,608,128]{2,1,0:T(8,128)(2,1)}), bf16[4,608,128]{2,1,0:T(8,128)(2,1)S(1)}, u32[]{:S(2)}, u32[]{:S(2)}) async-start(bf16[4,608,128]{2,1,0:T(8,128)(2,1)} %bitcast.10), calls=%async_computation.3 | async-start | bytes 1245184 | tf_op jit(solution)/shard_map/all_to_all | solution.py:1354
  167.9 8.3 %all-to-all-done.3 = bf16[4,608,128]{2,1,0:T(8,128)(2,1)S(1)} async-done(((bf16[4,608,128]{2,1,0:T(8,128)(2,1)}), bf16[4,608,128]{2,1,0:T(8,128)(2,1)S(1)}, u32[]{:S(2)}, u32[]{:S(2)}) %all-to-all-start.3) | async-done | bytes 622624 | tf_op jit(solution)/shard_map/all_to_all | solution.py:1354
  176.3 3.1 %collective-permute-done.13.refs_1_ = bf16[768,128]{1,0:T(8,128)(2,1)S(1)} collective-permute-done((bf16[768,128]{1,0:T(8,128)(2,1)S(1)}, bf16[768,128]{1,0:T(8,128)(2,1)S(1)}, u32[]{:S(2)}, u32[]{:S(2)}) %collective-permute-start.13) | collective-permute-done | bytes 196640 | tf_op jit(solution)/shard_map/ppermute | solution.py:1335
  185.8 2.8 %collective-permute-done.15.refs_3_ = bf16[512,128]{1,0:T(8,128)(2,1)S(1)} collective-permute-done((bf16[512,128]{1,0:T(8,128)(2,1)S(1)}, bf16[512,128]{1,0:T(8,128)(2,1)S(1)}, u32[]{:S(2)}, u32[]{:S(2)}) %collective-permute-start.15) | collective-permute-done | bytes 131104 | tf_op jit(solution)/shard_map/ppermute | solution.py:1335
  194.5 5.9 %collective-permute-done.18 = bf16[608,128]{1,0:T(8,128)(2,1)S(1)} collective-permute-done((bf16[608,128]{1,0:T(8,128)(2,1)S(1)}, bf16[608,128]{1,0:T(8,128)(2,1)S(1)}, u32[]{:S(2)}, u32[]{:S(2)}) %collective-permute-start.18) | collective-permute-done | bytes 155680 | tf_op jit(solution)/shard_map/ppermute | solution.py:1335
  205.8 15.9 %all_to_all.30 = bf16[4,608,128]{2,1,0:T(8,128)(2,1)S(1)} all-to-all(bf16[4,608,128]{2,1,0:T(8,128)(2,1)S(1)} %broadcast_in_dim.37), channel_id=1, replica_groups={{0,2,4,6},{8,10,12,14},{16,18,20,22},{24,26,28,30},{1,3,5,7},{9,11,13,1..., dimensions={0} | all-to-all | bytes 1245184 | tf_op jit(solution)/shard_map/all_to_all | solution.py:1354
  223.4 7.9 %all-to-all-start.5 = ((bf16[32,24,576]{2,1,0:T(8,128)(2,1)}), bf16[32,24,576]{2,1,0:T(8,128)(2,1)S(1)}, u32[]{:S(2)}, u32[]{:S(2)}) async-start(bf16[32,24,576]{2,1,0:T(8,128)(2,1)} %bitcast.18), calls=%async_computation.5 | async-start | bytes 1966080 | tf_op jit(solution)/shard_map/all_to_all | solution.py:1389
  234.8 11.2 %update_first.1 = (f32[1770048]{0:T(1024)}, f32[1770048]{0:T(1024)}, f32[1770048]{0:T(1024)}, f32[1770048]{0:T(1024)}) custom-call(s32[1]{0:T(128)} %bitcast.1.core_ref, s32[3]{0:T(128)} %copy-done.7, bf16[2048,128]{1,0:T(8,128)(2,1)} %copy-done.3, bf16[2048,128]{1,0:T(8,128)(2,1)} %copy-done.9, bf16[2048,128]{1,0:T(8,128)(2,1)} %copy-done.4, ...), custom_call_target="tpu_custom_call" | custom-call | flops 1000000000 | bytes 56641536 | tf_op jit(solution)/shard_map/update_first/pallas_call | solution.py:1287
  247.0 12.8 %update_second.1 = (f32[1770048]{0:T(1024)}, f32[1770048]{0:T(1024)}, f32[1770048]{0:T(1024)}, f32[1770048]{0:T(1024)}) custom-call(s32[1]{0:T(128)} %bitcast.1.core_ref, s32[3]{0:T(128)} %copy-done.7, bf16[2048,128]{1,0:T(8,128)(2,1)} %copy-done.3, ...), custom_call_target="tpu_custom_call", output_to_operand_aliasing={{0}: (15, {}), {1}: (16, {}), {2}: (17, {}), {3}: (18, {})} | custom-call | flops 1000000000 | bytes 56641536 | tf_op jit(solution)/shard_map/update_second/pallas_call | solution.py:1316
  (109 shorter events, 53.2 us)
Async XLA Ops:
  0.6 12.3 %collective-permute-start = (f32[1770048]{0:T(1024)}, f32[1770048]{0:T(1024)}, u32[]{:S(2)}, u32[]{:S(2)}) collective-permute-start(f32[1770048]{0:T(1024)} %rest_10_.1), channel_id=1, source_target_pairs={{0,1},{1,0},{2,3},{3,2},{4,5},{5,4},{6,7},{7,6},{8,9},{9,8},{10,11... | collective-permute-start | bytes 21240584 | tf_op jit(solution)/shard_map/ppermute | solution.py:1394
  3.5 31.0 %all-to-all-start = ((bf16[32,24,576]{2,1,0:T(8,128)(2,1)}), bf16[32,24,576]{2,1,0:T(8,128)(2,1)S(1)}, u32[]{:S(2)}, u32[]{:S(2)}) async-start(bf16[32,24,576]{2,1,0:T(8,128)(2,1)} %gather_fusion), calls=%async_computation | async-start | bytes 1966080 | tf_op jit(solution)/shard_map/all_to_all | solution.py:1389
  34.5 28.5 %all-to-all-start.1 = ((bf16[32,24,576]{2,1,0:T(8,128)(2,1)}), bf16[32,24,576]{2,1,0:T(8,128)(2,1)S(1)}, u32[]{:S(2)}, u32[]{:S(2)}) async-start(bf16[32,24,576]{2,1,0:T(8,128)(2,1)} %param.9), calls=%async_computation.1 | async-start | bytes 1966080 | tf_op jit(solution)/shard_map/all_to_all | solution.py:1389
  92.5 12.6 %collective-permute-start.1 = (bf16[12288,128]{1,0:T(8,128)(2,1)}, bf16[12288,128]{1,0:T(8,128)(2,1)}, u32[]{:S(2)}, u32[]{:S(2)}) collective-permute-start(bf16[12288,128]{1,0:T(8,128)(2,1)} %get-tuple-element.147), channel_id=1, source_target_pairs={{0,1},{1,0},{2,3},{3,2},{4,5},{5,4},{6,7},{7,6},{8,9},{9,8},{10,11... | collective-permute-start | bytes 9437192 | tf_op jit(solution)/shard_map/ppermute | solution.py:1412
  93.9 35.1 %all-to-all-start.2 = ((bf16[32,24,576]{2,1,0:T(8,128)(2,1)}), bf16[32,24,576]{2,1,0:T(8,128)(2,1)S(1)}, u32[]{:S(2)}, u32[]{:S(2)}) async-start(bf16[32,24,576]{2,1,0:T(8,128)(2,1)} %bitcast.21), calls=%async_computation.2 | async-start | bytes 1966080 | tf_op jit(solution)/shard_map/all_to_all | solution.py:1389
  108.0 16.4 %collective-permute-start.2 = (bf16[2048,128]{1,0:T(8,128)(2,1)S(1)}, bf16[2048,128]{1,0:T(8,128)(2,1)S(1)}, u32[]{:S(2)}, u32[]{:S(2)}) collective-permute-start(bf16[2048,128]{1,0:T(8,128)(2,1)S(1)} %get-tuple-element.157), channel_id=1, source_target_pairs={{0,2},{2,0},{4,6},{6,4},{8,10},{10,8},{12,14},{14,12},{16,18},{18,... | collective-permute-start | bytes 1572872 | tf_op jit(solution)/shard_map/ppermute | solution.py:1335
  109.4 16.4 %collective-permute-start.3 = (bf16[2048,128]{1,0:T(8,128)(2,1)S(1)}, bf16[2048,128]{1,0:T(8,128)(2,1)S(1)}, u32[]{:S(2)}, u32[]{:S(2)}) collective-permute-start(bf16[2048,128]{1,0:T(8,128)(2,1)S(1)} %get-tuple-element.158), channel_id=1, source_target_pairs={{0,4},{2,6},{4,0},{6,2},{8,12},{10,14},{12,8},{14,10},{16,20},{18,... | collective-permute-start | bytes 1572872 | tf_op jit(solution)/shard_map/ppermute | solution.py:1335
  110.6 17.3 %collective-permute-start.4 = (bf16[2048,128]{1,0:T(8,128)(2,1)S(1)}, bf16[2048,128]{1,0:T(8,128)(2,1)S(1)}, u32[]{:S(2)}, u32[]{:S(2)}) collective-permute-start(bf16[2048,128]{1,0:T(8,128)(2,1)S(1)} %get-tuple-element.159), channel_id=1, source_target_pairs={{0,8},{2,10},{4,12},{6,14},{8,0},{10,2},{12,4},{14,6},{16,24},{18,... | collective-permute-start | bytes 1572872 | tf_op jit(solution)/shard_map/ppermute | solution.py:1335
  129.1 10.4 %collective-permute-start.5 = (bf16[1024,128]{1,0:T(8,128)(2,1)S(1)}, bf16[1024,128]{1,0:T(8,128)(2,1)S(1)}, u32[]{:S(2)}, u32[]{:S(2)}) collective-permute-start(bf16[1024,128]{1,0:T(8,128)(2,1)S(1)} %get-tuple-element.182), channel_id=1, source_target_pairs={{0,4},{2,6},{4,0},{6,2},{8,12},{10,14},{12,8},{14,10},{16,20},{18,... | collective-permute-start | bytes 786440 | tf_op jit(solution)/shard_map/ppermute | solution.py:1335
  129.9 9.5 %collective-permute-start.6 = (bf16[1024,128]{1,0:T(8,128)(2,1)S(1)}, bf16[1024,128]{1,0:T(8,128)(2,1)S(1)}, u32[]{:S(2)}, u32[]{:S(2)}) collective-permute-start(bf16[1024,128]{1,0:T(8,128)(2,1)S(1)} %get-tuple-element.183), channel_id=1, source_target_pairs={{0,8},{2,10},{4,12},{6,14},{8,0},{10,2},{12,4},{14,6},{16,24},{18,... | collective-permute-start | bytes 786440 | tf_op jit(solution)/shard_map/ppermute | solution.py:1335
  129.9 9.5 %collective-permute-start.7 = (bf16[1024,128]{1,0:T(8,128)(2,1)S(1)}, bf16[1024,128]{1,0:T(8,128)(2,1)S(1)}, u32[]{:S(2)}, u32[]{:S(2)}) collective-permute-start(bf16[1024,128]{1,0:T(8,128)(2,1)S(1)} %get-tuple-element.184), channel_id=1, source_target_pairs={{0,2},{2,0},{4,6},{6,4},{8,10},{10,8},{12,14},{14,12},{16,18},{18,... | collective-permute-start | bytes 786440 | tf_op jit(solution)/shard_map/ppermute | solution.py:1335
  152.3 11.7 %collective-permute-start.12 = (bf16[768,128]{1,0:T(8,128)(2,1)S(1)}, bf16[768,128]{1,0:T(8,128)(2,1)S(1)}, u32[]{:S(2)}, u32[]{:S(2)}) collective-permute-start(bf16[768,128]{1,0:T(8,128)(2,1)S(1)} %get-tuple-element.205), channel_id=1, source_target_pairs={{0,16},{2,18},{4,20},{6,22},{8,24},{10,26},{12,28},{14,30},{16,0},... | collective-permute-start | bytes 589832 | tf_op jit(solution)/shard_map/ppermute | solution.py:1335
  164.0 12.2 %all-to-all-start.3 = ((bf16[4,608,128]{2,1,0:T(8,128)(2,1)}), bf16[4,608,128]{2,1,0:T(8,128)(2,1)S(1)}, u32[]{:S(2)}, u32[]{:S(2)}) async-start(bf16[4,608,128]{2,1,0:T(8,128)(2,1)} %bitcast.10), calls=%async_computation.3 | async-start | bytes 1245184 | tf_op jit(solution)/shard_map/all_to_all | solution.py:1354
  167.8 11.5 %collective-permute-start.13 = (bf16[768,128]{1,0:T(8,128)(2,1)S(1)}, bf16[768,128]{1,0:T(8,128)(2,1)S(1)}, u32[]{:S(2)}, u32[]{:S(2)}) collective-permute-start(bf16[768,128]{1,0:T(8,128)(2,1)S(1)} %gather_sum.11.refs_0_), channel_id=1, source_target_pairs={{0,16},{2,18},{4,20},{6,22},{8,24},{10,26},{12,28},{14,30},{16,0},... | collective-permute-start | bytes 589832 | tf_op jit(solution)/shard_map/ppermute | solution.py:1335
  190.2 10.2 %collective-permute-start.18 = (bf16[608,128]{1,0:T(8,128)(2,1)S(1)}, bf16[608,128]{1,0:T(8,128)(2,1)S(1)}, u32[]{:S(2)}, u32[]{:S(2)}) collective-permute-start(bf16[608,128]{1,0:T(8,128)(2,1)S(1)} %add_convert_fusion.1), channel_id=1, source_target_pairs={{0,16},{2,18},{4,20},{6,22},{8,24},{10,26},{12,28},{14,30},{16,0},... | collective-permute-start | bytes 466952 | tf_op jit(solution)/shard_map/ppermute | solution.py:1335
  190.7 9.7 %collective-permute-start.19 = (bf16[1024,128]{1,0:T(8,128)(2,1)S(1)}, bf16[1024,128]{1,0:T(8,128)(2,1)S(1)}, u32[]{:S(2)}, u32[]{:S(2)}) collective-permute-start(bf16[1024,128]{1,0:T(8,128)(2,1)S(1)} %get-tuple-element.228.refs_0_), channel_id=1, source_target_pairs={{0,4},{2,6},{4,0},{6,2},{8,12},{10,14},{12,8},{14,10},{16,20},{18,... | collective-permute-start | bytes 786440 | tf_op jit(solution)/shard_map/ppermute | solution.py:1335
  192.1 9.6 %collective-permute-start.20 = (bf16[1024,128]{1,0:T(8,128)(2,1)S(1)}, bf16[1024,128]{1,0:T(8,128)(2,1)S(1)}, u32[]{:S(2)}, u32[]{:S(2)}) collective-permute-start(bf16[1024,128]{1,0:T(8,128)(2,1)S(1)} %get-tuple-element.229.refs_1_), channel_id=1, source_target_pairs={{0,8},{2,10},{4,12},{6,14},{8,0},{10,2},{12,4},{14,6},{16,24},{18,... | collective-permute-start | bytes 786440 | tf_op jit(solution)/shard_map/ppermute | solution.py:1335
  202.5 19.2 %collective-permute-start.25 = (bf16[2048,128]{1,0:T(8,128)(2,1)S(1)}, bf16[2048,128]{1,0:T(8,128)(2,1)}, u32[]{:S(2)}, u32[]{:S(2)}) collective-permute-start(bf16[2048,128]{1,0:T(8,128)(2,1)S(1)} %get-tuple-element.239.rest_4_), channel_id=1, source_target_pairs={{0,8},{2,10},{4,12},{6,14},{8,0},{10,2},{12,4},{14,6},{16,24},{18,... | collective-permute-start | bytes 1572872 | tf_op jit(solution)/shard_map/ppermute | solution.py:1335
  202.6 19.1 %collective-permute-start.22 = (bf16[2048,128]{1,0:T(8,128)(2,1)S(1)}, bf16[2048,128]{1,0:T(8,128)(2,1)S(1)}, u32[]{:S(2)}, u32[]{:S(2)}) collective-permute-start(bf16[2048,128]{1,0:T(8,128)(2,1)S(1)} %get-tuple-element.239.rest_4_), channel_id=1, source_target_pairs={{0,1},{2,3},{4,5},{6,7},{8,9},{10,11},{12,13},{14,15},{16,17},{18,... | collective-permute-start | bytes 1572872 | tf_op jit(solution)/shard_map/ppermute | solution.py:1462
  203.9 17.8 %collective-permute-start.23 = (bf16[2048,128]{1,0:T(8,128)(2,1)S(1)}, bf16[2048,128]{1,0:T(8,128)(2,1)S(1)}, u32[]{:S(2)}, u32[]{:S(2)}) collective-permute-start(bf16[2048,128]{1,0:T(8,128)(2,1)S(1)} %get-tuple-element.240.rest_0_), channel_id=1, source_target_pairs={{0,2},{2,0},{4,6},{6,4},{8,10},{10,8},{12,14},{14,12},{16,18},{18,... | collective-permute-start | bytes 1572872 | tf_op jit(solution)/shard_map/ppermute | solution.py:1335
  205.2 16.6 %collective-permute-start.24 = (bf16[2048,128]{1,0:T(8,128)(2,1)S(1)}, bf16[2048,128]{1,0:T(8,128)(2,1)S(1)}, u32[]{:S(2)}, u32[]{:S(2)}) collective-permute-start(bf16[2048,128]{1,0:T(8,128)(2,1)S(1)} %get-tuple-element.241.rest_2_), channel_id=1, source_target_pairs={{0,4},{2,6},{4,0},{6,2},{8,12},{10,14},{12,8},{14,10},{16,20},{18,... | collective-permute-start | bytes 1572872 | tf_op jit(solution)/shard_map/ppermute | solution.py:1335
  223.4 36.5 %all-to-all-start.5 = ((bf16[32,24,576]{2,1,0:T(8,128)(2,1)}), bf16[32,24,576]{2,1,0:T(8,128)(2,1)S(1)}, u32[]{:S(2)}, u32[]{:S(2)}) async-start(bf16[32,24,576]{2,1,0:T(8,128)(2,1)} %bitcast.18), calls=%async_computation.5 | async-start | bytes 1966080 | tf_op jit(solution)/shard_map/all_to_all | solution.py:1389
  231.3 14.7 %collective-permute-start.27 = (bf16[2432,128]{1,0:T(8,128)(2,1)S(1)}, bf16[2432,128]{1,0:T(8,128)(2,1)S(1)}, u32[]{:S(2)}, u32[]{:S(2)}) collective-permute-start(bf16[2432,128]{1,0:T(8,128)(2,1)S(1)} %bitcast.16), channel_id=1, source_target_pairs={{1,0},{3,2},{5,4},{7,6},{9,8},{11,10},{13,12},{15,14},{17,16},{19,... | collective-permute-start | bytes 1867784 | tf_op jit(solution)/shard_map/ppermute | solution.py:1469
  233.5 12.5 %collective-permute-start.26 = (bf16[2048,128]{1,0:T(8,128)(2,1)}, bf16[2048,128]{1,0:T(8,128)(2,1)S(1)}, u32[]{:S(2)}, u32[]{:S(2)}) collective-permute-start(bf16[2048,128]{1,0:T(8,128)(2,1)} %collective-permute-done.25.rest_5_), channel_id=1, source_target_pairs={{0,1},{2,3},{4,5},{6,7},{8,9},{10,11},{12,13},{14,15},{16,17},{18,... | collective-permute-start | bytes 1572872 | tf_op jit(solution)/shard_map/ppermute | solution.py:1470
  (25 other events, 233.3 us)

commit v5 on v4

--- a/solution.py
+++ b/solution.py
@@ -605,8 +605,10 @@
 def late_weights(
     core_ref, nm_s, dq_s, dkv_s, gga_ref, ggm_ref, keep_ref, send_ref, late, sem
 ):
-    grad_q = tn(nm_s[...], dq_s[...]).astype(BF)
-    grad_kv = tn(nm_s[...], dkv_s[...]).astype(BF)
+    both = jnp.concatenate([dq_s[...], dkv_s[...]], axis=1)
+    grads = tn(nm_s[...], both).astype(BF)
+    grad_q = grads[:, :PAD_D]
+    grad_kv = grads[:, PAD_D:]
     for t in range(Q_TILES):
         late[t * D : (t + 1) * D, :] = tile(grad_q, t)
     for t in range(3):

time: 262 us -> 262 us (level)
  transfers between devices with their start and end apart: 33 -> 33, of which waited for: 12 -> 11; matrix products, arithmetic and copies ran while one was open for 2% -> 2% of each run, Pallas kernels for 36% -> 35%
where the time goes in v5:
time: 262 us; the launch traced here: 261 us
  Pallas kernels  128 us (49%)
  starting transfers between devices  55.5 us (21%)
  waiting for transfers between devices  49.5 us (19%)
  blocking collectives  15.9 us (6%)
  local copies, waits for them, and re-layouts  7.54 us (3%)
  other arithmetic  3.66 us (1%)
    pallas_call x1, Pallas kernels, run_mlp(): call(mlp_pass, outs, [smem()] * 5 + [hbm()] * 3 + [vmem()] + [hbm()] * 4,...  28.5 us
    ppermute x22, waiting for transfers between devices, xor_swap(): return lax.ppermute(value, 'dp', [(i, i ^ 1 << bit) for i in range(size)])  25.6 us
    all_to_all x4, starting transfers between devices, exchange(): return lax.all_to_all(value, axes, split_axis=0, concat_axis=0, tiled=True)  23 us
    pallas_call x2, Pallas kernels, run_backward_groups(): pl.pallas_call(functools.partial(backward_groups, first), grid=(count,),...  20.2 us
    ppermute x22, starting transfers between devices, xor_swap(): return lax.ppermute(value, 'dp', [(i, i ^ 1 << bit) for i in range(size)])  20 us
    pallas_call x1, Pallas kernels, run_attention_forward(): call(attention_forward, outs, [vmem()] * 4 + [hbm()] + [vmem()] * 2, [hbm...  17.6 us
    all_to_all x1, blocking collectives, spread(): lax.all_to_all(blocks, 'dp', split_axis=0, concat_axis=0, tiled=True, axi...  15.9 us
    all_to_all x4, waiting for transfers between devices, exchange(): return lax.all_to_all(value, axes, split_axis=0, concat_axis=0, tiled=True)  15.6 us
  transfers between devices with their start and end apart: 33, of which 11 were waited for; matrix products, arithmetic and copies ran while one was open for 2% of the time, Pallas kernels for 35%

profile of v5, /device:TPU:1, one launch (start us, length us, event | category | flops | bytes accessed | tf_op | source)
XLA Modules:
  0.0 260.8 jit_solution(6675630060357871597)
XLA Ops:
  3.5 7.1 %all-to-all-start = ((bf16[32,24,576]{2,1,0:T(8,128)(2,1)}), bf16[32,24,576]{2,1,0:T(8,128)(2,1)S(1)}, u32[]{:S(2)}, u32[]{:S(2)}) async-start(bf16[32,24,576]{2,1,0:T(8,128)(2,1)} %gather_fusion), calls=%async_computation | async-start | bytes 1966080 | tf_op jit(solution)/shard_map/all_to_all | solution.py:1391
  12.9 12.3 %prepare_weights.1 = (f32[1,576]{1,0:T(1,128)}, f32[1,576]{1,0:T(1,128)}, bf16[576,640]{1,0:T(8,128)(2,1)}, bf16[576,384]{1,0:T(8,128)(2,1)}, bf16[640,576]{1,0:...) custom-call(s32[1]{0:T(128)} %bitcast.1.core_ref, ...), custom_call_target="tpu_custom_call" | custom-call | flops 10000000000 | bytes 14459904 | tf_op jit(solution)/shard_map/prepare_weights/pallas_call | solution.py:1067
  25.2 9.3 %all-to-all-done = bf16[32,24,576]{2,1,0:T(8,128)(2,1)S(1)} async-done(((bf16[32,24,576]{2,1,0:T(8,128)(2,1)}), bf16[32,24,576]{2,1,0:T(8,128)(2,1)S(1)}, u32[]{:S(2)}, u32[]{:S(2)}) %all-to-all-start) | async-done | bytes 884768 | tf_op jit(solution)/shard_map/all_to_all | solution.py:1391
  34.5 4.5 %all-to-all-start.1 = ((bf16[32,24,576]{2,1,0:T(8,128)(2,1)}), bf16[32,24,576]{2,1,0:T(8,128)(2,1)S(1)}, u32[]{:S(2)}, u32[]{:S(2)}) async-start(bf16[32,24,576]{2,1,0:T(8,128)(2,1)} %param.9), calls=%async_computation.1 | async-start | bytes 1966080 | tf_op jit(solution)/shard_map/all_to_all | solution.py:1391
  39.1 17.6 %attention_forward.1 = (f32[768,576]{1,0:T(8,128)}, bf16[768,640]{1,0:T(8,128)(2,1)}, bf16[5,768,128]{2,1,0:T(8,128)(2,1)}, bf16[6,768,128]{2,1,0:T(8,128)(2,1)}...) custom-call(bf16[768,576]{1,0:T(8,128)(2,1)} %bitcast.19, f32[1,576]{1,0:T(1,128)} %get-tuple-element.132.ga_ref, ...), custom_call_target="tpu_custom_call" | custom-call | flops 15000000512 | bytes 12288000 | tf_op jit(solution)/shard_map/attention_forward/pallas_call | solution.py:1089
  56.7 6.2 %all-to-all-done.1 = bf16[32,24,576]{2,1,0:T(8,128)(2,1)S(1)} async-done(((bf16[32,24,576]{2,1,0:T(8,128)(2,1)}), bf16[32,24,576]{2,1,0:T(8,128)(2,1)S(1)}, u32[]{:S(2)}, u32[]{:S(2)}) %all-to-all-start.1) | async-done | bytes 884768 | tf_op jit(solution)/shard_map/all_to_all | solution.py:1391
  64.0 28.5 %mlp_pass.1 = (bf16[768,576]{1,0:T(8,128)(2,1)}, f32[768,576]{1,0:T(8,128)}, bf16[5,768,128]{2,1,0:T(8,128)(2,1)}, f32[1,576]{1,0:T(1,128)}, bf16[12288,128]{1,0:T(8,128)(2,1)}, /*index=5*/bf16[12288,128]{1,0:T(8,128)(2,1)}) custom-call(s32[1]{0:T(128)} %bitcast.1.core_ref, s32[1]{0:T(128)} %bitcast.5.slot_ref, s32[32]{0:T(128)} %lengths_ref.1, ...), custom_call_target="tpu_custom_call" | custom-call | flops 24999999488 | bytes 19862016 | tf_op jit(solution)/shard_map/mlp_pass/pallas_call | solution.py:1117
  93.9 3.5 %all-to-all-start.2 = ((bf16[32,24,576]{2,1,0:T(8,128)(2,1)}), bf16[32,24,576]{2,1,0:T(8,128)(2,1)S(1)}, u32[]{:S(2)}, u32[]{:S(2)}) async-start(bf16[32,24,576]{2,1,0:T(8,128)(2,1)} %bitcast.21), calls=%async_computation.2 | async-start | bytes 1966080 | tf_op jit(solution)/shard_map/all_to_all | solution.py:1391
  97.4 7.6 %backward_groups.2 = (f32[1,2,768,128]{3,2,1,0:T(8,128)}, f32[1,768,128]{2,1,0:T(8,128)}, f32[1,768,128]{2,1,0:T(8,128)}) custom-call(bf16[5,768,128]{2,1,0:T(8,128)(2,1)} %get-tuple-element.164.q_ref, bf16[5,768,128]{2,1,0:T(8,128)(2,1)} %get-tuple-element.165.dm_ref, bf16[6,768,128]{2,1,0:T(8,128)(2,1)} %get-tuple-element.166.k_ref, ...), custom_call_target="tpu_custom_call" | custom-call | flops 8000000000 | bytes 3000000 | tf_op jit(solution)/shard_map/backward_groups/pallas_call | solution.py:1156
  105.0 2.9 %gather_sum.6 = (bf16[2048,128]{1,0:T(8,128)(2,1)S(1)}, bf16[2048,128]{1,0:T(8,128)(2,1)S(1)}, bf16[2048,128]{1,0:T(8,128)(2,1)S(1)}, bf16[2048,128]{1,0:T(8,128...) custom-call(s32[3]{0:T(128)S(1)} %pad_add_fusion.1.bits_ref, bf16[12288,128]{1,0:T(8,128)(2,1)S(1)} %copy-done.2, ...), custom_call_target="tpu_custom_call" | custom-call | flops 1000000 | bytes 6291456 | tf_op jit(solution)/shard_map/gather_sum/pallas_call | solution.py:1231
  111.8 12.6 %backward_groups.3 = (f32[2,2,768,128]{3,2,1,0:T(8,128)}, f32[2,768,128]{2,1,0:T(8,128)}, f32[2,768,128]{2,1,0:T(8,128)}) custom-call(bf16[5,768,128]{2,1,0:T(8,128)(2,1)} %get-tuple-element.164.q_ref, bf16[5,768,128]{2,1,0:T(8,128)(2,1)} %get-tuple-element.165.dm_ref, bf16[6,768,128]{2,1,0:T(8,128)(2,1)} %get-tuple-element.166.k_ref, ...), custom_call_target="tpu_custom_call" | custom-call | flops 16000000000 | bytes 6000000 | tf_op jit(solution)/shard_map/backward_groups/pallas_call | solution.py:1156
  131.0 8.4 %backward_finish.1 = (bf16[768,576]{1,0:T(8,128)(2,1)}, bf16[768,640]{1,0:T(8,128)(2,1)}, bf16[768,384]{1,0:T(8,128)(2,1)}, bf16[768,576]{1,0:T(8,128)(2,1)}, f32[1,576]{1,0:T(1,128)}) custom-call(bf16[768,576]{1,0:T(8,128)(2,1)} %bitcast.20, f32[1,576]{1,0:T(1,128)} %get-tuple-element.132.ga_ref, f32[768,576]{1,0:T(8,128)} %get-tuple-element.163.dh1_hbm, ...), custom_call_target="tpu_custom_call" | custom-call | flops 4000000000 | bytes 6689280 | tf_op jit(solution)/shard_map/backward_finish/pallas_call | solution.py:1190
  144.1 3.8 %late_weights.1 = (bf16[2432,128]{1,0:T(8,128)(2,1)}, bf16[2432,128]{1,0:T(8,128)(2,1)}) custom-call(s32[1]{0:T(128)} %bitcast.1.core_ref, bf16[768,576]{1,0:T(8,128)(2,1)} %get-tuple-element.175.nm_s, bf16[768,640]{1,0:T(8,128)(2,1)} %get-tuple-element.176.dq_s, bf16[768,384]{1,0:T(8,128)(2,1)} %get-tuple-element.177.dkv_s, ...), custom_call_target="tpu_custom_call" | custom-call | flops 4000000000 | bytes 2490368 | tf_op jit(solution)/shard_map/late_weights/pallas_call | solution.py:1212
  149.2 2.8 %collective-permute-start.11 = (bf16[2432,128]{1,0:T(8,128)(2,1)}, bf16[2432,128]{1,0:T(8,128)(2,1)S(1)}, u32[]{:S(2)}, u32[]{:S(2)}) collective-permute-start(bf16[2432,128]{1,0:T(8,128)(2,1)} %get-tuple-element.203), channel_id=1, source_target_pairs={{0,1},{1,0},{2,3},{3,2},{4,5},{5,4},{6,7},{7,6},{8,9},{9,8},{10,11... | collective-permute-start | bytes 1867784 | tf_op jit(solution)/shard_map/ppermute | solution.py:1439
  156.1 7.9 %collective-permute-done.12.refs_1_ = bf16[768,128]{1,0:T(8,128)(2,1)S(1)} collective-permute-done((bf16[768,128]{1,0:T(8,128)(2,1)S(1)}, bf16[768,128]{1,0:T(8,128)(2,1)S(1)}, u32[]{:S(2)}, u32[]{:S(2)}) %collective-permute-start.12) | collective-permute-done | bytes 196640 | tf_op jit(solution)/shard_map/ppermute | solution.py:1337
  164.0 3.5 %all-to-all-start.3 = ((bf16[4,608,128]{2,1,0:T(8,128)(2,1)}), bf16[4,608,128]{2,1,0:T(8,128)(2,1)S(1)}, u32[]{:S(2)}, u32[]{:S(2)}) async-start(bf16[4,608,128]{2,1,0:T(8,128)(2,1)} %bitcast.10), calls=%async_computation.3 | async-start | bytes 1245184 | tf_op jit(solution)/shard_map/all_to_all | solution.py:1356
  167.9 8.3 %all-to-all-done.3 = bf16[4,608,128]{2,1,0:T(8,128)(2,1)S(1)} async-done(((bf16[4,608,128]{2,1,0:T(8,128)(2,1)}), bf16[4,608,128]{2,1,0:T(8,128)(2,1)S(1)}, u32[]{:S(2)}, u32[]{:S(2)}) %all-to-all-start.3) | async-done | bytes 622624 | tf_op jit(solution)/shard_map/all_to_all | solution.py:1356
  176.3 3.1 %collective-permute-done.13.refs_1_ = bf16[768,128]{1,0:T(8,128)(2,1)S(1)} collective-permute-done((bf16[768,128]{1,0:T(8,128)(2,1)S(1)}, bf16[768,128]{1,0:T(8,128)(2,1)S(1)}, u32[]{:S(2)}, u32[]{:S(2)}) %collective-permute-start.13) | collective-permute-done | bytes 196640 | tf_op jit(solution)/shard_map/ppermute | solution.py:1337
  185.8 2.8 %collective-permute-done.15.refs_3_ = bf16[512,128]{1,0:T(8,128)(2,1)S(1)} collective-permute-done((bf16[512,128]{1,0:T(8,128)(2,1)S(1)}, bf16[512,128]{1,0:T(8,128)(2,1)S(1)}, u32[]{:S(2)}, u32[]{:S(2)}) %collective-permute-start.15) | collective-permute-done | bytes 131104 | tf_op jit(solution)/shard_map/ppermute | solution.py:1337
  194.5 5.9 %collective-permute-done.18 = bf16[608,128]{1,0:T(8,128)(2,1)S(1)} collective-permute-done((bf16[608,128]{1,0:T(8,128)(2,1)S(1)}, bf16[608,128]{1,0:T(8,128)(2,1)S(1)}, u32[]{:S(2)}, u32[]{:S(2)}) %collective-permute-start.18) | collective-permute-done | bytes 155680 | tf_op jit(solution)/shard_map/ppermute | solution.py:1337
  205.8 15.9 %all_to_all.30 = bf16[4,608,128]{2,1,0:T(8,128)(2,1)S(1)} all-to-all(bf16[4,608,128]{2,1,0:T(8,128)(2,1)S(1)} %broadcast_in_dim.37), channel_id=1, replica_groups={{0,2,4,6},{8,10,12,14},{16,18,20,22},{24,26,28,30},{1,3,5,7},{9,11,13,1..., dimensions={0} | all-to-all | bytes 1245184 | tf_op jit(solution)/shard_map/all_to_all | solution.py:1356
  223.4 7.9 %all-to-all-start.5 = ((bf16[32,24,576]{2,1,0:T(8,128)(2,1)}), bf16[32,24,576]{2,1,0:T(8,128)(2,1)S(1)}, u32[]{:S(2)}, u32[]{:S(2)}) async-start(bf16[32,24,576]{2,1,0:T(8,128)(2,1)} %bitcast.18), calls=%async_computation.5 | async-start | bytes 1966080 | tf_op jit(solution)/shard_map/all_to_all | solution.py:1391
  234.8 11.2 %update_first.1 = (f32[1770048]{0:T(1024)}, f32[1770048]{0:T(1024)}, f32[1770048]{0:T(1024)}, f32[1770048]{0:T(1024)}) custom-call(s32[1]{0:T(128)} %bitcast.1.core_ref, s32[3]{0:T(128)} %copy-done.7, bf16[2048,128]{1,0:T(8,128)(2,1)} %copy-done.3, bf16[2048,128]{1,0:T(8,128)(2,1)} %copy-done.9, bf16[2048,128]{1,0:T(8,128)(2,1)} %copy-done.4, ...), custom_call_target="tpu_custom_call" | custom-call | flops 1000000000 | bytes 56641536 | tf_op jit(solution)/shard_map/update_first/pallas_call | solution.py:1289
  247.0 12.8 %update_second.1 = (f32[1770048]{0:T(1024)}, f32[1770048]{0:T(1024)}, f32[1770048]{0:T(1024)}, f32[1770048]{0:T(1024)}) custom-call(s32[1]{0:T(128)} %bitcast.1.core_ref, s32[3]{0:T(128)} %copy-done.7, bf16[2048,128]{1,0:T(8,128)(2,1)} %copy-done.3, ...), custom_call_target="tpu_custom_call", output_to_operand_aliasing={{0}: (15, {}), {1}: (16, {}), {2}: (17, {}), {3}: (18, {})} | custom-call | flops 1000000000 | bytes 56641536 | tf_op jit(solution)/shard_map/update_second/pallas_call | solution.py:1318
  (109 shorter events, 53.2 us)
Async XLA Ops:
  0.6 12.3 %collective-permute-start = (f32[1770048]{0:T(1024)}, f32[1770048]{0:T(1024)}, u32[]{:S(2)}, u32[]{:S(2)}) collective-permute-start(f32[1770048]{0:T(1024)} %rest_10_.1), channel_id=1, source_target_pairs={{0,1},{1,0},{2,3},{3,2},{4,5},{5,4},{6,7},{7,6},{8,9},{9,8},{10,11... | collective-permute-start | bytes 21240584 | tf_op jit(solution)/shard_map/ppermute | solution.py:1396
  3.5 31.0 %all-to-all-start = ((bf16[32,24,576]{2,1,0:T(8,128)(2,1)}), bf16[32,24,576]{2,1,0:T(8,128)(2,1)S(1)}, u32[]{:S(2)}, u32[]{:S(2)}) async-start(bf16[32,24,576]{2,1,0:T(8,128)(2,1)} %gather_fusion), calls=%async_computation | async-start | bytes 1966080 | tf_op jit(solution)/shard_map/all_to_all | solution.py:1391
  34.5 28.5 %all-to-all-start.1 = ((bf16[32,24,576]{2,1,0:T(8,128)(2,1)}), bf16[32,24,576]{2,1,0:T(8,128)(2,1)S(1)}, u32[]{:S(2)}, u32[]{:S(2)}) async-start(bf16[32,24,576]{2,1,0:T(8,128)(2,1)} %param.9), calls=%async_computation.1 | async-start | bytes 1966080 | tf_op jit(solution)/shard_map/all_to_all | solution.py:1391
  92.5 12.6 %collective-permute-start.1 = (bf16[12288,128]{1,0:T(8,128)(2,1)}, bf16[12288,128]{1,0:T(8,128)(2,1)}, u32[]{:S(2)}, u32[]{:S(2)}) collective-permute-start(bf16[12288,128]{1,0:T(8,128)(2,1)} %get-tuple-element.147), channel_id=1, source_target_pairs={{0,1},{1,0},{2,3},{3,2},{4,5},{5,4},{6,7},{7,6},{8,9},{9,8},{10,11... | collective-permute-start | bytes 9437192 | tf_op jit(solution)/shard_map/ppermute | solution.py:1414
  93.9 35.1 %all-to-all-start.2 = ((bf16[32,24,576]{2,1,0:T(8,128)(2,1)}), bf16[32,24,576]{2,1,0:T(8,128)(2,1)S(1)}, u32[]{:S(2)}, u32[]{:S(2)}) async-start(bf16[32,24,576]{2,1,0:T(8,128)(2,1)} %bitcast.21), calls=%async_computation.2 | async-start | bytes 1966080 | tf_op jit(solution)/shard_map/all_to_all | solution.py:1391
  108.0 16.4 %collective-permute-start.2 = (bf16[2048,128]{1,0:T(8,128)(2,1)S(1)}, bf16[2048,128]{1,0:T(8,128)(2,1)S(1)}, u32[]{:S(2)}, u32[]{:S(2)}) collective-permute-start(bf16[2048,128]{1,0:T(8,128)(2,1)S(1)} %get-tuple-element.157), channel_id=1, source_target_pairs={{0,2},{2,0},{4,6},{6,4},{8,10},{10,8},{12,14},{14,12},{16,18},{18,... | collective-permute-start | bytes 1572872 | tf_op jit(solution)/shard_map/ppermute | solution.py:1337
  109.4 16.4 %collective-permute-start.3 = (bf16[2048,128]{1,0:T(8,128)(2,1)S(1)}, bf16[2048,128]{1,0:T(8,128)(2,1)S(1)}, u32[]{:S(2)}, u32[]{:S(2)}) collective-permute-start(bf16[2048,128]{1,0:T(8,128)(2,1)S(1)} %get-tuple-element.158), channel_id=1, source_target_pairs={{0,4},{2,6},{4,0},{6,2},{8,12},{10,14},{12,8},{14,10},{16,20},{18,... | collective-permute-start | bytes 1572872 | tf_op jit(solution)/shard_map/ppermute | solution.py:1337
  110.6 17.3 %collective-permute-start.4 = (bf16[2048,128]{1,0:T(8,128)(2,1)S(1)}, bf16[2048,128]{1,0:T(8,128)(2,1)S(1)}, u32[]{:S(2)}, u32[]{:S(2)}) collective-permute-start(bf16[2048,128]{1,0:T(8,128)(2,1)S(1)} %get-tuple-element.159), channel_id=1, source_target_pairs={{0,8},{2,10},{4,12},{6,14},{8,0},{10,2},{12,4},{14,6},{16,24},{18,... | collective-permute-start | bytes 1572872 | tf_op jit(solution)/shard_map/ppermute | solution.py:1337
  129.1 10.4 %collective-permute-start.5 = (bf16[1024,128]{1,0:T(8,128)(2,1)S(1)}, bf16[1024,128]{1,0:T(8,128)(2,1)S(1)}, u32[]{:S(2)}, u32[]{:S(2)}) collective-permute-start(bf16[1024,128]{1,0:T(8,128)(2,1)S(1)} %get-tuple-element.182), channel_id=1, source_target_pairs={{0,4},{2,6},{4,0},{6,2},{8,12},{10,14},{12,8},{14,10},{16,20},{18,... | collective-permute-start | bytes 786440 | tf_op jit(solution)/shard_map/ppermute | solution.py:1337
  129.9 9.5 %collective-permute-start.6 = (bf16[1024,128]{1,0:T(8,128)(2,1)S(1)}, bf16[1024,128]{1,0:T(8,128)(2,1)S(1)}, u32[]{:S(2)}, u32[]{:S(2)}) collective-permute-start(bf16[1024,128]{1,0:T(8,128)(2,1)S(1)} %get-tuple-element.183), channel_id=1, source_target_pairs={{0,8},{2,10},{4,12},{6,14},{8,0},{10,2},{12,4},{14,6},{16,24},{18,... | collective-permute-start | bytes 786440 | tf_op jit(solution)/shard_map/ppermute | solution.py:1337
  129.9 9.5 %collective-permute-start.7 = (bf16[1024,128]{1,0:T(8,128)(2,1)S(1)}, bf16[1024,128]{1,0:T(8,128)(2,1)S(1)}, u32[]{:S(2)}, u32[]{:S(2)}) collective-permute-start(bf16[1024,128]{1,0:T(8,128)(2,1)S(1)} %get-tuple-element.184), channel_id=1, source_target_pairs={{0,2},{2,0},{4,6},{6,4},{8,10},{10,8},{12,14},{14,12},{16,18},{18,... | collective-permute-start | bytes 786440 | tf_op jit(solution)/shard_map/ppermute | solution.py:1337
  152.1 12.0 %collective-permute-start.12 = (bf16[768,128]{1,0:T(8,128)(2,1)S(1)}, bf16[768,128]{1,0:T(8,128)(2,1)S(1)}, u32[]{:S(2)}, u32[]{:S(2)}) collective-permute-start(bf16[768,128]{1,0:T(8,128)(2,1)S(1)} %get-tuple-element.205), channel_id=1, source_target_pairs={{0,16},{2,18},{4,20},{6,22},{8,24},{10,26},{12,28},{14,30},{16,0},... | collective-permute-start | bytes 589832 | tf_op jit(solution)/shard_map/ppermute | solution.py:1337
  164.0 12.2 %all-to-all-start.3 = ((bf16[4,608,128]{2,1,0:T(8,128)(2,1)}), bf16[4,608,128]{2,1,0:T(8,128)(2,1)S(1)}, u32[]{:S(2)}, u32[]{:S(2)}) async-start(bf16[4,608,128]{2,1,0:T(8,128)(2,1)} %bitcast.10), calls=%async_computation.3 | async-start | bytes 1245184 | tf_op jit(solution)/shard_map/all_to_all | solution.py:1356
  167.8 11.5 %collective-permute-start.13 = (bf16[768,128]{1,0:T(8,128)(2,1)S(1)}, bf16[768,128]{1,0:T(8,128)(2,1)S(1)}, u32[]{:S(2)}, u32[]{:S(2)}) collective-permute-start(bf16[768,128]{1,0:T(8,128)(2,1)S(1)} %gather_sum.11.refs_0_), channel_id=1, source_target_pairs={{0,16},{2,18},{4,20},{6,22},{8,24},{10,26},{12,28},{14,30},{16,0},... | collective-permute-start | bytes 589832 | tf_op jit(solution)/shard_map/ppermute | solution.py:1337
  190.2 10.2 %collective-permute-start.18 = (bf16[608,128]{1,0:T(8,128)(2,1)S(1)}, bf16[608,128]{1,0:T(8,128)(2,1)S(1)}, u32[]{:S(2)}, u32[]{:S(2)}) collective-permute-start(bf16[608,128]{1,0:T(8,128)(2,1)S(1)} %add_convert_fusion.1), channel_id=1, source_target_pairs={{0,16},{2,18},{4,20},{6,22},{8,24},{10,26},{12,28},{14,30},{16,0},... | collective-permute-start | bytes 466952 | tf_op jit(solution)/shard_map/ppermute | solution.py:1337
  190.7 9.7 %collective-permute-start.19 = (bf16[1024,128]{1,0:T(8,128)(2,1)S(1)}, bf16[1024,128]{1,0:T(8,128)(2,1)S(1)}, u32[]{:S(2)}, u32[]{:S(2)}) collective-permute-start(bf16[1024,128]{1,0:T(8,128)(2,1)S(1)} %get-tuple-element.228.refs_0_), channel_id=1, source_target_pairs={{0,4},{2,6},{4,0},{6,2},{8,12},{10,14},{12,8},{14,10},{16,20},{18,... | collective-permute-start | bytes 786440 | tf_op jit(solution)/shard_map/ppermute | solution.py:1337
  192.1 9.6 %collective-permute-start.20 = (bf16[1024,128]{1,0:T(8,128)(2,1)S(1)}, bf16[1024,128]{1,0:T(8,128)(2,1)S(1)}, u32[]{:S(2)}, u32[]{:S(2)}) collective-permute-start(bf16[1024,128]{1,0:T(8,128)(2,1)S(1)} %get-tuple-element.229.refs_1_), channel_id=1, source_target_pairs={{0,8},{2,10},{4,12},{6,14},{8,0},{10,2},{12,4},{14,6},{16,24},{18,... | collective-permute-start | bytes 786440 | tf_op jit(solution)/shard_map/ppermute | solution.py:1337
  202.5 19.2 %collective-permute-start.25 = (bf16[2048,128]{1,0:T(8,128)(2,1)S(1)}, bf16[2048,128]{1,0:T(8,128)(2,1)}, u32[]{:S(2)}, u32[]{:S(2)}) collective-permute-start(bf16[2048,128]{1,0:T(8,128)(2,1)S(1)} %get-tuple-element.239.rest_4_), channel_id=1, source_target_pairs={{0,8},{2,10},{4,12},{6,14},{8,0},{10,2},{12,4},{14,6},{16,24},{18,... | collective-permute-start | bytes 1572872 | tf_op jit(solution)/shard_map/ppermute | solution.py:1337
  202.6 19.1 %collective-permute-start.22 = (bf16[2048,128]{1,0:T(8,128)(2,1)S(1)}, bf16[2048,128]{1,0:T(8,128)(2,1)S(1)}, u32[]{:S(2)}, u32[]{:S(2)}) collective-permute-start(bf16[2048,128]{1,0:T(8,128)(2,1)S(1)} %get-tuple-element.239.rest_4_), channel_id=1, source_target_pairs={{0,1},{2,3},{4,5},{6,7},{8,9},{10,11},{12,13},{14,15},{16,17},{18,... | collective-permute-start | bytes 1572872 | tf_op jit(solution)/shard_map/ppermute | solution.py:1464
  203.9 17.8 %collective-permute-start.23 = (bf16[2048,128]{1,0:T(8,128)(2,1)S(1)}, bf16[2048,128]{1,0:T(8,128)(2,1)S(1)}, u32[]{:S(2)}, u32[]{:S(2)}) collective-permute-start(bf16[2048,128]{1,0:T(8,128)(2,1)S(1)} %get-tuple-element.240.rest_0_), channel_id=1, source_target_pairs={{0,2},{2,0},{4,6},{6,4},{8,10},{10,8},{12,14},{14,12},{16,18},{18,... | collective-permute-start | bytes 1572872 | tf_op jit(solution)/shard_map/ppermute | solution.py:1337
  205.2 16.6 %collective-permute-start.24 = (bf16[2048,128]{1,0:T(8,128)(2,1)S(1)}, bf16[2048,128]{1,0:T(8,128)(2,1)S(1)}, u32[]{:S(2)}, u32[]{:S(2)}) collective-permute-start(bf16[2048,128]{1,0:T(8,128)(2,1)S(1)} %get-tuple-element.241.rest_2_), channel_id=1, source_target_pairs={{0,4},{2,6},{4,0},{6,2},{8,12},{10,14},{12,8},{14,10},{16,20},{18,... | collective-permute-start | bytes 1572872 | tf_op jit(solution)/shard_map/ppermute | solution.py:1337
  223.4 36.5 %all-to-all-start.5 = ((bf16[32,24,576]{2,1,0:T(8,128)(2,1)}), bf16[32,24,576]{2,1,0:T(8,128)(2,1)S(1)}, u32[]{:S(2)}, u32[]{:S(2)}) async-start(bf16[32,24,576]{2,1,0:T(8,128)(2,1)} %bitcast.18), calls=%async_computation.5 | async-start | bytes 1966080 | tf_op jit(solution)/shard_map/all_to_all | solution.py:1391
  231.3 14.7 %collective-permute-start.27 = (bf16[2432,128]{1,0:T(8,128)(2,1)S(1)}, bf16[2432,128]{1,0:T(8,128)(2,1)S(1)}, u32[]{:S(2)}, u32[]{:S(2)}) collective-permute-start(bf16[2432,128]{1,0:T(8,128)(2,1)S(1)} %bitcast.16), channel_id=1, source_target_pairs={{1,0},{3,2},{5,4},{7,6},{9,8},{11,10},{13,12},{15,14},{17,16},{19,... | collective-permute-start | bytes 1867784 | tf_op jit(solution)/shard_map/ppermute | solution.py:1471
  233.5 12.5 %collective-permute-start.26 = (bf16[2048,128]{1,0:T(8,128)(2,1)}, bf16[2048,128]{1,0:T(8,128)(2,1)S(1)}, u32[]{:S(2)}, u32[]{:S(2)}) collective-permute-start(bf16[2048,128]{1,0:T(8,128)(2,1)} %collective-permute-done.25.rest_5_), channel_id=1, source_target_pairs={{0,1},{2,3},{4,5},{6,7},{8,9},{10,11},{12,13},{14,15},{16,17},{18,... | collective-permute-start | bytes 1572872 | tf_op jit(solution)/shard_map/ppermute | solution.py:1472
  (25 other events, 232.6 us)
